TPU v7x, 32 devices: a whole 2x2x4 slice. The times are simulated.
32 devices in a mesh: dp: 4 (over x, core), fsdp: 8 (over z, y).
Axes of the slice: x: 2, y: 2, z: 4, core: 2. Of those that a mesh axis runs over, the one named last changes fastest.
Arguments:
- tokens: bfloat16 [32, 512, 768], P(('dp', 'fsdp')), may hold values from -6 to 6
- out_grad: bfloat16 [32, 512, 768], P(('dp', 'fsdp')), may hold values from -6 to 6
- segment_ids: int32 [32, 512], P(('dp', 'fsdp')), may hold values from 0 to 3, never falling along the last dimension, each value on 1 to 256 neighbouring positions
- labels: int32 [32], P(('dp', 'fsdp')), may hold values from 0 to 2
- query_weight: bfloat16 [768, 768], P('fsdp'), may hold values from -0.3125 to 0.3125
- query_bias: bfloat16 [768], P('fsdp'), may hold values from -3 to 3
- key_weight: bfloat16 [768, 768], P('fsdp'), may hold values from -0.21875 to 0.21875
- value_weight: bfloat16 [768, 768], P('fsdp'), may hold values from -0.21875 to 0.21875
- value_bias: bfloat16 [768], P('fsdp'), may hold values from -3 to 3
- output_weight: bfloat16 [768, 768], P('fsdp'), may hold values from -0.625 to 0.625
- output_bias: bfloat16 [768], P('fsdp'), may hold values from -3 to 3
- first_norm_gain: bfloat16 [768], P('fsdp'), may hold values from 0.5 to 1.5
- first_norm_shift: bfloat16 [768], P('fsdp'), may hold values from -3 to 3
- inner_weight: bfloat16 [768, 3072], P('fsdp'), may hold values from -0.21875 to 0.21875
- inner_bias: bfloat16 [3072], P('fsdp'), may hold values from -3 to 3
- outer_weight: bfloat16 [3072, 768], P('fsdp'), may hold values from -0.109375 to 0.109375
- outer_bias: bfloat16 [768], P('fsdp'), may hold values from -3 to 3
- second_norm_gain: bfloat16 [768], P('fsdp'), may hold values from 0.5 to 1.5
- second_norm_shift: bfloat16 [768], P('fsdp'), may hold values from -3 to 3
- pooler_weight: bfloat16 [768, 768], P('fsdp'), may hold values from -0.21875 to 0.21875
- pooler_bias: bfloat16 [768], P('fsdp'), may hold values from -3 to 3
- class_weight: bfloat16 [768, 3], P('fsdp'), may hold values from -0.625 to 0.625
- class_bias: bfloat16 [3], replicated, may hold values from -1 to 1
Outputs:
- hidden_state: bfloat16 [32, 512, 768], P(('dp', 'fsdp'))
- tokens_grad: float32 [32, 512, 768], P(('dp', 'fsdp'))
- ramp_loss: float32 [32], P(('dp', 'fsdp'))
- query_weight_grad: float32 [768, 768], P('fsdp')
- query_bias_grad: float32 [768], P('fsdp')
- key_weight_grad: float32 [768, 768], P('fsdp')
- value_weight_grad: float32 [768, 768], P('fsdp')
- value_bias_grad: float32 [768], P('fsdp')
- output_weight_grad: float32 [768, 768], P('fsdp')
- output_bias_grad: float32 [768], P('fsdp')
- first_norm_gain_grad: float32 [768], P('fsdp')
- first_norm_shift_grad: float32 [768], P('fsdp')
- inner_weight_grad: float32 [768, 3072], P('fsdp')
- inner_bias_grad: float32 [3072], P('fsdp')
- outer_weight_grad: float32 [3072, 768], P('fsdp')
- outer_bias_grad: float32 [768], P('fsdp')
- second_norm_gain_grad: float32 [768], P('fsdp')
- second_norm_shift_grad: float32 [768], P('fsdp')
- pooler_weight_grad: float32 [768, 768], P('fsdp')
- pooler_bias_grad: float32 [768], P('fsdp')
- class_weight_grad: float32 [768, 3], P('fsdp')
- class_bias_grad: float32 [3], replicated
Inputs may be any that keep to these rules, and one draw needn't show every extreme that they name: `segment_ids`: in each row the ids start at 0 and never fall; each of the 4 ids covers 1 to 256 consecutive positions, and one covers exactly 256.
All inputs are finite; a program needn't handle non-finite values.
Results may differ from a plain program's by a relative error of at most 0.018.
Values may be sent and summed in bfloat16 or wider, within the bound.
No kernel may reach another device: no remote copies, remote signals or barrier semaphores. Data moves between devices by JAX's collectives and lax.ppermute only.
A program may use at most 192 MiB of HBM per device.

v0:
```python
import jax
import jax.numpy as jnp
from jax import lax
from jax.sharding import PartitionSpec as P

HEADS = 12
HEAD_DIM = 64
CLASSES = 3


EPS = 1e-06
NEG = -1000000000.0


def matmul(left_side, right_side):
    return jnp.dot(left_side, right_side, preferred_element_type=jnp.float32)


def inner_rows(left_side, right_side):
    return lax.dot_general(
        left_side, right_side, (((0,), (0,)), ((), ())), preferred_element_type=jnp.float32
    )


def times_transposed(left_side, right_side):
    return lax.dot_general(
        left_side, right_side, (((1,), (1,)), ((), ())), preferred_element_type=jnp.float32
    )


def column_sums(grad_low):
    return jnp.sum(grad_low.astype(jnp.float32), axis=0)


def layer_norm(inputs, gain_row, shift_row):
    row_mean = jnp.mean(inputs, axis=-1, keepdims=True)
    centered = inputs - row_mean
    variance = jnp.mean(centered * centered, axis=-1, keepdims=True)
    return centered * lax.rsqrt(variance + EPS) * gain_row + shift_row


def exact_gelu(inputs):
    return jax.nn.gelu(inputs, approximate=False)


def head_slice(source, head_index):
    return lax.dynamic_slice_in_dim(source, head_index * HEAD_DIM, HEAD_DIM, 2)


def to_tokens(stacked):
    head_count, row_count, seq_len, head_size = stacked.shape
    return jnp.transpose(stacked, (1, 2, 0, 3)).reshape(row_count * seq_len, head_count * head_size)


def attention(queries, key_block, values, same_doc):
    score_scale = HEAD_DIM ** (-0.5)

    def one_head(head_index):
        query_head = head_slice(queries, head_index)
        key_head = head_slice(key_block, head_index)
        value_head = head_slice(values, head_index)
        scores = (
            jnp.einsum("rqd,rkd->rqk", query_head, key_head, preferred_element_type=jnp.float32)
            * score_scale
        )
        scores = jnp.where(same_doc, scores, NEG)
        row_max = jnp.max(scores, axis=-1, keepdims=True)
        exponent = jnp.exp(scores - row_max)
        denominator = jnp.sum(exponent, axis=-1, keepdims=True)
        weights_soft = (exponent / denominator).astype(jnp.bfloat16)
        context = jnp.einsum(
            "rqk,rkd->rqd", weights_soft, value_head, preferred_element_type=jnp.float32
        )
        return (context.astype(jnp.bfloat16), row_max[..., 0] + jnp.log(denominator[..., 0]))

    context, logsum = lax.map(one_head, jnp.arange(HEADS))
    return (to_tokens(context), logsum)


def attention_back(queries, key_block, values, context_grad, logsum, same_doc):
    score_scale = HEAD_DIM ** (-0.5)

    def one_head(head_index):
        query_head = head_slice(queries, head_index)
        key_head = head_slice(key_block, head_index)
        value_head = head_slice(values, head_index)
        grad_head = head_slice(context_grad, head_index)
        scores = (
            jnp.einsum("rqd,rkd->rqk", query_head, key_head, preferred_element_type=jnp.float32)
            * score_scale
        )
        scores = jnp.where(same_doc, scores, NEG)
        weights_soft = jnp.exp(scores - logsum[head_index][..., None])
        value_grad = jnp.einsum(
            "rqk,rqd->rkd",
            weights_soft.astype(jnp.bfloat16),
            grad_head,
            preferred_element_type=jnp.float32,
        )
        soft_grad = jnp.einsum(
            "rqd,rkd->rqk", grad_head, value_head, preferred_element_type=jnp.float32
        )
        row_dot = jnp.sum(soft_grad * weights_soft, axis=-1, keepdims=True)
        score_grad = (weights_soft * (soft_grad - row_dot)).astype(jnp.bfloat16)
        query_grad = (
            jnp.einsum("rqk,rkd->rqd", score_grad, key_head, preferred_element_type=jnp.float32)
            * score_scale
        )
        key_grad = (
            jnp.einsum("rqk,rqd->rkd", score_grad, query_head, preferred_element_type=jnp.float32)
            * score_scale
        )
        return (query_grad, key_grad, value_grad)

    query_stack, key_stack, value_stack = lax.map(one_head, jnp.arange(HEADS))
    return (
        to_tokens(query_stack).astype(jnp.bfloat16),
        to_tokens(key_stack).astype(jnp.bfloat16),
        to_tokens(value_stack).astype(jnp.bfloat16),
    )


def forward_pass(weights, flat_tokens, same_doc, token_shape):
    (
        query_matrix,
        query_offset,
        keys_matrix,
        value_matrix,
        value_offset,
        output_matrix,
        output_offset,
        first_gain,
        first_shift,
        inner_matrix,
        inner_offset,
        outer_matrix,
        outer_offset,
        second_gain,
        second_shift,
        pooler_matrix,
        pooler_offset,
        class_matrix,
    ) = weights
    queries = (
        (matmul(flat_tokens, query_matrix) + query_offset.astype(jnp.float32))
        .astype(jnp.bfloat16)
        .reshape(token_shape)
    )
    key_block = matmul(flat_tokens, keys_matrix).astype(jnp.bfloat16).reshape(token_shape)
    values = (
        (matmul(flat_tokens, value_matrix) + value_offset.astype(jnp.float32))
        .astype(jnp.bfloat16)
        .reshape(token_shape)
    )
    context, logsum = attention(queries, key_block, values, same_doc)
    attended = matmul(context, output_matrix) + output_offset.astype(jnp.float32)
    first_in = flat_tokens.astype(jnp.float32) + attended
    first_out = layer_norm(
        first_in, first_gain.astype(jnp.float32), first_shift.astype(jnp.float32)
    )
    first_low = first_out.astype(jnp.bfloat16)
    inner_pre = matmul(first_low, inner_matrix) + inner_offset.astype(jnp.float32)
    activated = exact_gelu(inner_pre).astype(jnp.bfloat16)
    second_in = first_out + (matmul(activated, outer_matrix) + outer_offset.astype(jnp.float32))
    hidden = layer_norm(
        second_in, second_gain.astype(jnp.float32), second_shift.astype(jnp.float32)
    )
    return (
        queries,
        key_block,
        values,
        context,
        logsum,
        first_in,
        first_low,
        inner_pre,
        activated,
        second_in,
        hidden,
    )


def on_device(
    tokens,
    out_grad,
    segment_ids,
    labels,
    query_weight,
    query_bias,
    key_weight,
    value_weight,
    value_bias,
    output_weight,
    output_bias,
    first_norm_gain,
    first_norm_shift,
    inner_weight,
    inner_bias,
    outer_weight,
    outer_bias,
    second_norm_gain,
    second_norm_shift,
    pooler_weight,
    pooler_bias,
    class_weight,
    class_bias,
):
    row_count, seq_len, width = tokens.shape
    token_count = row_count * seq_len
    token_shape = (row_count, seq_len, width)
    flat_tokens = tokens.reshape(token_count, width)
    same_doc = segment_ids[:, :, None] == segment_ids[:, None, :]
    onehot = (labels[:, None] == jnp.arange(CLASSES)[None, :]).astype(jnp.float32)
    weights = (
        lax.all_gather(query_weight, "fsdp", axis=0, tiled=True),
        lax.all_gather(query_bias, "fsdp", axis=0, tiled=True),
        lax.all_gather(key_weight, "fsdp", axis=0, tiled=True),
        lax.all_gather(value_weight, "fsdp", axis=0, tiled=True),
        lax.all_gather(value_bias, "fsdp", axis=0, tiled=True),
        lax.all_gather(output_weight, "fsdp", axis=0, tiled=True),
        lax.all_gather(output_bias, "fsdp", axis=0, tiled=True),
        lax.all_gather(first_norm_gain, "fsdp", axis=0, tiled=True),
        lax.all_gather(first_norm_shift, "fsdp", axis=0, tiled=True),
        lax.all_gather(inner_weight, "fsdp", axis=0, tiled=True),
        lax.all_gather(inner_bias, "fsdp", axis=0, tiled=True),
        lax.all_gather(outer_weight, "fsdp", axis=0, tiled=True),
        lax.all_gather(outer_bias, "fsdp", axis=0, tiled=True),
        lax.all_gather(second_norm_gain, "fsdp", axis=0, tiled=True),
        lax.all_gather(second_norm_shift, "fsdp", axis=0, tiled=True),
        lax.all_gather(pooler_weight, "fsdp", axis=0, tiled=True),
        lax.all_gather(pooler_bias, "fsdp", axis=0, tiled=True),
        lax.all_gather(class_weight, "fsdp", axis=0, tiled=True),
    )
    state = forward_pass(weights, flat_tokens, same_doc, token_shape)
    hidden = state[10]
    hidden_rows = hidden.reshape(token_shape)
    class_rows = hidden_rows[:, 0, :].astype(jnp.bfloat16)
    pooled_pre = matmul(class_rows, weights[15]) + weights[16].astype(jnp.float32)
    pooled_tanh, tanh_pull = jax.vjp(jnp.tanh, pooled_pre)
    pooled = pooled_tanh.astype(jnp.bfloat16)
    logits = matmul(pooled, weights[17]) + class_bias.astype(jnp.float32)
    row_max = jnp.max(logits, axis=-1, keepdims=True)
    exponent = jnp.exp(logits - row_max)
    class_total = jnp.sum(exponent, axis=-1, keepdims=True)
    ramp_loss = row_max[:, 0] + jnp.log(class_total[:, 0]) - jnp.sum(logits * onehot, axis=-1)
    weights = (
        lax.all_gather(query_weight, "fsdp", axis=0, tiled=True),
        lax.all_gather(query_bias, "fsdp", axis=0, tiled=True),
        lax.all_gather(key_weight, "fsdp", axis=0, tiled=True),
        lax.all_gather(value_weight, "fsdp", axis=0, tiled=True),
        lax.all_gather(value_bias, "fsdp", axis=0, tiled=True),
        lax.all_gather(output_weight, "fsdp", axis=0, tiled=True),
        lax.all_gather(output_bias, "fsdp", axis=0, tiled=True),
        lax.all_gather(first_norm_gain, "fsdp", axis=0, tiled=True),
        lax.all_gather(first_norm_shift, "fsdp", axis=0, tiled=True),
        lax.all_gather(inner_weight, "fsdp", axis=0, tiled=True),
        lax.all_gather(inner_bias, "fsdp", axis=0, tiled=True),
        lax.all_gather(outer_weight, "fsdp", axis=0, tiled=True),
        lax.all_gather(outer_bias, "fsdp", axis=0, tiled=True),
        lax.all_gather(second_norm_gain, "fsdp", axis=0, tiled=True),
        lax.all_gather(second_norm_shift, "fsdp", axis=0, tiled=True),
        lax.all_gather(pooler_weight, "fsdp", axis=0, tiled=True),
        lax.all_gather(pooler_bias, "fsdp", axis=0, tiled=True),
        lax.all_gather(class_weight, "fsdp", axis=0, tiled=True),
    )
    state = forward_pass(weights, flat_tokens, same_doc, token_shape)
    (
        queries,
        key_block,
        values,
        context,
        logsum,
        first_in,
        first_low,
        inner_pre,
        activated,
        second_in,
        hidden,
    ) = state
    query_matrix = weights[0]
    keys_matrix = weights[2]
    value_matrix = weights[3]
    output_matrix = weights[5]
    first_gain = weights[7].astype(jnp.float32)
    first_shift = weights[8].astype(jnp.float32)
    inner_matrix = weights[9]
    outer_matrix = weights[11]
    second_gain = weights[13].astype(jnp.float32)
    second_shift = weights[14].astype(jnp.float32)
    pooler_matrix = weights[15]
    class_matrix = weights[17]
    logit_grad = (exponent / class_total - onehot).astype(jnp.bfloat16)
    class_weight_local = inner_rows(pooled, logit_grad)
    class_bias_local = column_sums(logit_grad)
    pooled_grad = times_transposed(logit_grad, class_matrix)
    pre_grad = tanh_pull(pooled_grad)[0].astype(jnp.bfloat16)
    pooler_weight_local = inner_rows(class_rows, pre_grad)
    pooler_bias_local = column_sums(pre_grad)
    class_row_grad = times_transposed(pre_grad, pooler_matrix)
    final_grad = (
        out_grad.astype(jnp.float32).at[:, 0, :].add(class_row_grad).reshape(token_count, width)
    )
    second_unused, second_pull = jax.vjp(layer_norm, second_in, second_gain, second_shift)
    second_grad, second_gain_local, second_shift_local = second_pull(final_grad)
    branch_grad = second_grad.astype(jnp.bfloat16)
    outer_weight_local = inner_rows(activated, branch_grad)
    outer_bias_local = column_sums(branch_grad)
    activated_grad = times_transposed(branch_grad, outer_matrix)
    gelu_unused, gelu_pull = jax.vjp(exact_gelu, inner_pre)
    inner_grad = gelu_pull(activated_grad)[0].astype(jnp.bfloat16)
    inner_weight_local = inner_rows(first_low, inner_grad)
    inner_bias_local = column_sums(inner_grad)
    first_grad = second_grad + times_transposed(inner_grad, inner_matrix)
    first_unused, first_pull = jax.vjp(layer_norm, first_in, first_gain, first_shift)
    residual_grad, first_gain_local, first_shift_local = first_pull(first_grad)
    attended_grad = residual_grad.astype(jnp.bfloat16)
    output_weight_local = inner_rows(context, attended_grad)
    output_bias_local = column_sums(attended_grad)
    context_grad = (
        times_transposed(attended_grad, output_matrix).astype(jnp.bfloat16).reshape(token_shape)
    )
    query_grad, key_grad, value_grad = attention_back(
        queries, key_block, values, context_grad, logsum, same_doc
    )
    query_weight_local = inner_rows(flat_tokens, query_grad)
    query_bias_local = column_sums(query_grad)
    key_weight_local = inner_rows(flat_tokens, key_grad)
    value_weight_local = inner_rows(flat_tokens, value_grad)
    value_bias_local = column_sums(value_grad)
    tokens_grad = (
        residual_grad
        + times_transposed(query_grad, query_matrix)
        + times_transposed(key_grad, keys_matrix)
        + times_transposed(value_grad, value_matrix)
    )
    every_shard = (
        lax.psum_scatter(query_weight_local, "fsdp", scatter_dimension=0, tiled=True),
        lax.psum_scatter(query_bias_local, "fsdp", scatter_dimension=0, tiled=True),
        lax.psum_scatter(key_weight_local, "fsdp", scatter_dimension=0, tiled=True),
        lax.psum_scatter(value_weight_local, "fsdp", scatter_dimension=0, tiled=True),
        lax.psum_scatter(value_bias_local, "fsdp", scatter_dimension=0, tiled=True),
        lax.psum_scatter(output_weight_local, "fsdp", scatter_dimension=0, tiled=True),
        lax.psum_scatter(output_bias_local, "fsdp", scatter_dimension=0, tiled=True),
        lax.psum_scatter(first_gain_local, "fsdp", scatter_dimension=0, tiled=True),
        lax.psum_scatter(first_shift_local, "fsdp", scatter_dimension=0, tiled=True),
        lax.psum_scatter(inner_weight_local, "fsdp", scatter_dimension=0, tiled=True),
        lax.psum_scatter(inner_bias_local, "fsdp", scatter_dimension=0, tiled=True),
        lax.psum_scatter(outer_weight_local, "fsdp", scatter_dimension=0, tiled=True),
        lax.psum_scatter(outer_bias_local, "fsdp", scatter_dimension=0, tiled=True),
        lax.psum_scatter(second_gain_local, "fsdp", scatter_dimension=0, tiled=True),
        lax.psum_scatter(second_shift_local, "fsdp", scatter_dimension=0, tiled=True),
        lax.psum_scatter(pooler_weight_local, "fsdp", scatter_dimension=0, tiled=True),
        lax.psum_scatter(pooler_bias_local, "fsdp", scatter_dimension=0, tiled=True),
        lax.psum_scatter(class_weight_local, "fsdp", scatter_dimension=0, tiled=True),
    )
    (
        query_weight_grad,
        query_bias_grad,
        key_weight_grad,
        value_weight_grad,
        value_bias_grad,
        output_weight_grad,
        output_bias_grad,
        first_gain_grad,
        first_shift_grad,
        inner_weight_grad,
        inner_bias_grad,
        outer_weight_grad,
        outer_bias_grad,
        second_gain_grad,
        second_shift_grad,
        pooler_weight_grad,
        pooler_bias_grad,
        class_weight_grad,
    ) = (
        lax.psum(every_shard[0].astype(jnp.bfloat16), "dp").astype(jnp.float32),
        lax.psum(every_shard[1].astype(jnp.bfloat16), "dp").astype(jnp.float32),
        lax.psum(every_shard[2].astype(jnp.bfloat16), "dp").astype(jnp.float32),
        lax.psum(every_shard[3].astype(jnp.bfloat16), "dp").astype(jnp.float32),
        lax.psum(every_shard[4].astype(jnp.bfloat16), "dp").astype(jnp.float32),
        lax.psum(every_shard[5].astype(jnp.bfloat16), "dp").astype(jnp.float32),
        lax.psum(every_shard[6].astype(jnp.bfloat16), "dp").astype(jnp.float32),
        lax.psum(every_shard[7].astype(jnp.bfloat16), "dp").astype(jnp.float32),
        lax.psum(every_shard[8].astype(jnp.bfloat16), "dp").astype(jnp.float32),
        lax.psum(every_shard[9].astype(jnp.bfloat16), "dp").astype(jnp.float32),
        lax.psum(every_shard[10].astype(jnp.bfloat16), "dp").astype(jnp.float32),
        lax.psum(every_shard[11].astype(jnp.bfloat16), "dp").astype(jnp.float32),
        lax.psum(every_shard[12].astype(jnp.bfloat16), "dp").astype(jnp.float32),
        lax.psum(every_shard[13].astype(jnp.bfloat16), "dp").astype(jnp.float32),
        lax.psum(every_shard[14].astype(jnp.bfloat16), "dp").astype(jnp.float32),
        lax.psum(every_shard[15].astype(jnp.bfloat16), "dp").astype(jnp.float32),
        lax.psum(every_shard[16].astype(jnp.bfloat16), "dp").astype(jnp.float32),
        lax.psum(every_shard[17].astype(jnp.bfloat16), "dp").astype(jnp.float32),
    )
    class_bias_grad = lax.psum(class_bias_local, ("dp", "fsdp"))
    return (
        hidden.reshape(token_shape).astype(jnp.bfloat16),
        tokens_grad.reshape(token_shape),
        ramp_loss,
        query_weight_grad,
        query_bias_grad,
        key_weight_grad,
        value_weight_grad,
        value_bias_grad,
        output_weight_grad,
        output_bias_grad,
        first_gain_grad,
        first_shift_grad,
        inner_weight_grad,
        inner_bias_grad,
        outer_weight_grad,
        outer_bias_grad,
        second_gain_grad,
        second_shift_grad,
        pooler_weight_grad,
        pooler_bias_grad,
        class_weight_grad,
        class_bias_grad,
    )


def solution(mesh):
    return jax.shard_map(
        on_device,
        mesh=mesh,
        in_specs=(
            P(("dp", "fsdp"), None, None),
            P(("dp", "fsdp"), None, None),
            P(("dp", "fsdp"), None),
            P(("dp", "fsdp")),
            P("fsdp", None),
            P("fsdp"),
            P("fsdp", None),
            P("fsdp", None),
            P("fsdp"),
            P("fsdp", None),
            P("fsdp"),
            P("fsdp"),
            P("fsdp"),
            P("fsdp", None),
            P("fsdp"),
            P("fsdp", None),
            P("fsdp"),
            P("fsdp"),
            P("fsdp"),
            P("fsdp", None),
            P("fsdp"),
            P("fsdp", None),
            P(),
        ),
        out_specs=(
            P(("dp", "fsdp"), None, None),
            P(("dp", "fsdp"), None, None),
            P(("dp", "fsdp")),
            P("fsdp", None),
            P("fsdp"),
            P("fsdp", None),
            P("fsdp", None),
            P("fsdp"),
            P("fsdp", None),
            P("fsdp"),
            P("fsdp"),
            P("fsdp"),
            P("fsdp", None),
            P("fsdp"),
            P("fsdp", None),
            P("fsdp"),
            P("fsdp"),
            P("fsdp"),
            P("fsdp", None),
            P("fsdp"),
            P("fsdp", None),
            P(),
        ),
        check_vma=False,
    )
```

profile of v0, /device:TPU:0, one launch (start us, length us, event | category | flops | bytes accessed | tf_op | source)
XLA Modules:
  0.0 1338.9 jit_solution(8975526153864800655)
XLA Ops:
  22.9 39.1 %all-reduce.20 = (bf16[768]{0:T(1024)(128)(2,1)S(1)}, bf16[768]{0:T(1024)(128)(2,1)S(1)}, bf16[768]{0:T(1024)(128)(2,1)S(1)}, bf16[768]{0:T(1024)(128)(2,1)S(1)}...) all-reduce(bf16[768]{0:T(1024)(128)(2,1)S(1)} %dynamic-update-slice, ...), channel_id=1, replica_groups=mesh['dp'=4,'fsdp'=8] {'fsdp'}, use_global_device_ids=true, to_apply=%add | all-reduce | flops 6912 | bytes 27648
  62.0 16.7 %all-gather.1 = bf16[8,96,3]{1,2,0:T(4,128)(2,1)S(1)} all-gather(bf16[1,96,3]{1,2,0:T(4,128)(2,1)} %bitcast.272), channel_id=1, replica_groups=mesh['dp'=4,'fsdp'=8] {'fsdp'}, dimensions={0}, use_global_device_ids=true | all-gather | bytes 5184 | tf_op jit(solution)/shard_map/all_gather | solution.py:232
  78.8 26.1 %all-gather = bf16[8,1,384]{2,1,0:T(2,128)(2,1)S(1)} all-gather(bf16[1,1,384]{2,1,0:T(2,128)(2,1)S(1)} %reshape.530), channel_id=1, replica_groups=mesh['dp'=4,'fsdp'=8] {'fsdp'}, dimensions={0}, use_global_device_ids=true | all-gather | bytes 6912 | tf_op jit(solution)/shard_map/all_gather | solution.py:257
  112.1 26.4 %all-gather.10.cloned.1.call-done = bf16[768,768]{1,0:T(8,128)(2,1)} async-done(((bf16[96,768]{1,0:T(8,128)(2,1)}), bf16[768,768]{1,0:T(8,128)(2,1)}) %all-gather.10.cloned.1.call-update) | async-done | bytes 1179664 | tf_op jit(solution)/shard_map/all_gather | solution.py:247
  141.5 37.3 %while.41 = (s32[]{:T(128)}, bf16[12,1,512,64]{2,3,1,0:T(8,128)(2,1)S(1)}, s32[12]{0:T(128)S(1)}, bf16[1,512,768]{2,1,0:T(8,128)(2,1)}, bf16[1,512,768]{2,1,0:T(...) while((s32[]{:T(128)}, ...), condition=%wide.region_11.12_spmd.clone, body=%wide.region_8.11_spmd.clone.sunk | while | flops 69499904 | bytes 3620023 | solution.py:76
  179.7 45.2 %while.40 = (s32[]{:T(128)}, bf16[12,1,512,64]{2,3,1,0:T(8,128)(2,1)S(1)}, f32[12,1,512]{2,1,0:T(1,128)}, s32[12]{0:T(128)S(1)}, bf16[1,512,768]{2,1,0:T(8,128)(...) while((s32[]{:T(128)}, ...), condition=%wide.region_3.4_spmd.clone, body=%wide.region_0.3_spmd.clone.sunk | while | flops 69500416 | bytes 3630275 | solution.py:76
  229.4 31.8 %all-gather.18.cloned.1.call-done = bf16[768,3072]{1,0:T(8,128)(2,1)} async-done(((bf16[96,3072]{1,0:T(8,128)(2,1)}), bf16[768,3072]{1,0:T(8,128)(2,1)}) %all-gather.18.cloned.1.call-update) | async-done | bytes 4718608 | tf_op jit(solution)/shard_map/all_gather | solution.py:256
  261.2 80.1 %all-gather.20.cloned.1.call-done = bf16[3072,768]{1,0:T(8,128)(2,1)} async-done(((bf16[384,768]{1,0:T(8,128)(2,1)}), bf16[3072,768]{1,0:T(8,128)(2,1)}) %all-gather.20.cloned.1.call-update) | async-done | bytes 4718608 | tf_op jit(solution)/shard_map/all_gather | solution.py:258
  341.3 21.9 %fusion.158 = (f32[512]{0:T(512)S(1)}, f32[512,768]{1,0:T(8,128)S(1)}) fusion(f32[768]{0:T(1024)S(1)} %convert_element_type.320, bf16[3072,768]{1,0:T(8,128)(2,1)} %all-gather.20.cloned.1.call-done, bf16[768,3072]{1,0:T(8,128)(2,1)} %all-gather.18.cloned.1.call-done, f32[3072]{0:T(1024)S(1)} %bitcast.269, f32[512,768]{1,0:T(8,128)} %copy-done.11, ...), kind=kOutput, calls=%fused_computation.251 | convolution fusion | flops 4940365312 | bytes 12610560 | tf_op jit(solution)/shard_map/dot_general | solution.py:16
  364.8 17.9 %all-gather.22.cloned.1.call-done = bf16[768,768]{1,0:T(8,128)(2,1)} async-done(((bf16[96,768]{1,0:T(8,128)(2,1)}), bf16[768,768]{1,0:T(8,128)(2,1)}) %all-gather.22.cloned.1.call-update) | async-done | bytes 1179664 | tf_op jit(solution)/shard_map/all_gather | solution.py:230
  389.6 19.9 %multiply_convert_fusion.1 = (bf16[512,3072]{1,0:T(8,128)(2,1)S(1)}, f32[512,3072]{1,0:T(8,128)}, f32[512,3072]{1,0:T(8,128)}) fusion(f32[3072]{0:T(1024)S(1)} %bitcast.270, bf16[768,3072]{1,0:T(8,128)(2,1)} %all-gather.18.cloned.1.call-done, f32[512,768]{1,0:T(8,128)S(1)} %get-tuple-element.439, f32[768]{0:T(1024)S(1)} %convert_element_type.316, ...), kind=kOutput, calls=%fused_computation.94 | convolution fusion | flops 2521694208 | bytes 22042624 | tf_op jit(solution)/shard_map/dot_general | solution.py:16
  409.4 6.8 fusion.163
  420.3 9.3 convert_reduce_fusion
  429.7 3.2 multiply_reduce_fusion.2
  435.8 143.0 %while.42 = (s32[]{:T(128)}, bf16[12,1,512,64]{2,3,1,0:T(8,128)(2,1)}, bf16[12,1,512,64]{2,3,1,0:T(8,128)(2,1)}, bf16[12,1,512,64]{2,3,1,0:T(8,128)(2,1)S(1)}, s...) while((s32[]{:T(128)}, ...), condition=%wide.region_24.25_spmd.clone, body=%wide.region_22.24_spmd.clone.sunk | while | flops 170458624 | bytes 9191701 | solution.py:115
  584.2 3.3 convolution_bitcast_fusion.3
  587.5 3.1 copy.56
  590.7 3.3 convolution_bitcast_fusion.2
  594.0 3.1 copy.58
  597.2 3.3 fusion.166
  600.8 8.9 fusion.141
  610.8 8.2 fusion.167
  621.9 39.4 %psum.151 = f32[3]{0:T(128)} all-reduce(bf16[3]{0:T(256)(128)(2,1)S(1)} %get-tuple-element.406), channel_id=1, replica_groups=mesh['dp'=4,'fsdp'=8] {'dp','fsdp'}, use_global_device_ids=true, to_apply=%region_71.72 | all-reduce | flops 3 | bytes 18 | tf_op jit(solution)/shard_map/psum | solution.py:395
  662.8 37.1 %all-reduce.19 = (bf16[768]{0:T(1024)(128)(2,1)S(1)}, bf16[768]{0:T(1024)(128)(2,1)S(1)}, bf16[768]{0:T(1024)(128)(2,1)S(1)}, bf16[768]{0:T(1024)(128)(2,1)S(1)}...) all-reduce(f32[768]{0:T(1024)S(1)} %reduce_sum.262, ...), channel_id=3, replica_groups=mesh['dp'=4,'fsdp'=8] {'fsdp'}, use_global_device_ids=true, to_apply=%region_29.30.clone | all-reduce | flops 9984 | bytes 58368
  704.7 19.8 %reduce-scatter.25.cloned.1.call-done = f32[96,768]{1,0:T(8,128)} async-done(((f32[768,768]{1,0:T(8,128)}), f32[96,768]{1,0:T(8,128)}) %reduce-scatter.25.cloned.1.call-update) | async-done | bytes 294928
  726.3 70.0 %reduce-scatter.27.cloned.1.call-done = f32[96,768]{1,0:T(8,128)} async-done(((f32[768,768]{1,0:T(8,128)}), f32[96,768]{1,0:T(8,128)}) %reduce-scatter.27.cloned.1.call-update) | async-done | bytes 294928
  798.1 69.8 %reduce-scatter.17.cloned.1.call-done = f32[96,768]{1,0:T(8,128)} async-done(((f32[768,768]{1,0:T(8,128)}), f32[96,768]{1,0:T(8,128)}) %reduce-scatter.17.cloned.1.call-update) | async-done | bytes 294928 | tf_op jit(solution)/shard_map/reduce_scatter | solution.py:342
  869.6 164.3 %reduce-scatter.19.cloned.1.call-done = f32[96,3072]{1,0:T(8,128)} async-done(((f32[768,3072]{1,0:T(8,128)}), f32[96,3072]{1,0:T(8,128)}) %reduce-scatter.19.cloned.1.call-update) | async-done | bytes 1179664 | tf_op jit(solution)/shard_map/reduce_scatter | solution.py:346
  1036.1 163.9 %reduce-scatter.21.cloned.1.call-done = f32[384,768]{1,0:T(8,128)} async-done(((f32[3072,768]{1,0:T(8,128)}), f32[384,768]{1,0:T(8,128)}) %reduce-scatter.21.cloned.1.call-update) | async-done | bytes 1179664 | tf_op jit(solution)/shard_map/reduce_scatter | solution.py:348
  1207.7 55.9 %reduce-scatter.31.cloned.1.call-done = f32[96,3]{1,0:T(8,128)} async-done(((f32[768,3]{1,0:T(8,128)}), f32[96,3]{1,0:T(8,128)}) %reduce-scatter.31.cloned.1.call-update) | async-done | bytes 1168
  1264.5 5.8 all-reduce.21
  1276.0 43.1 %all-reduce.25.cloned.1.call-done = (bf16[96,768]{0,1:T(8,128)(2,1)}, bf16[96,768]{0,1:T(8,128)(2,1)}, bf16[96,768]{0,1:T(8,128)(2,1)}, bf16[96,768]{1,0:T(8,128...) async-done(((bf16[96,768]{0,1:T(8,128)(2,1)}, bf16[96,768]{0,1:T(8,128)(2,1)}, bf16[96,768]{0,1:T(8,128)(2,1)}, ...) | async-done | bytes 1916944 | tf_op jit(solution)/shard_map/psum | solution.py:376
  (443 shorter events, 268.8 us)
Async XLA Ops:
  7.2 100.8 %copy-start.2 = (bf16[1,512,768]{2,1,0:T(8,128)(2,1)S(1)}, bf16[1,512,768]{2,1,0:T(8,128)(2,1)}, u32[]{:S(2)}) copy-start(bf16[1,512,768]{2,1,0:T(8,128)(2,1)} %param.31) | copy-start | bytes 2359300
  7.2 100.7 %all-gather.12.cloned.1.call-start = ((), (), s32[]{:S(2)}) async-start(), calls=%async_computation.9 | async-start | bytes 1327104 | tf_op jit(solution)/shard_map/all_gather | solution.py:249
  7.9 102.1 %all-gather.14.cloned.1.call-start = ((), (), s32[]{:S(2)}) async-start(), calls=%async_computation.10 | async-start | bytes 1327104 | tf_op jit(solution)/shard_map/all_gather | solution.py:250
  8.7 129.8 %all-gather.10.cloned.1.call-start = ((), (), s32[]{:S(2)}) async-start(), calls=%async_computation.8 | async-start | bytes 1327104 | tf_op jit(solution)/shard_map/all_gather | solution.py:247
  9.4 215.6 %all-gather.16.cloned.1.call-start = ((), (), s32[]{:S(2)}) async-start(), calls=%async_computation.11 | async-start | bytes 1327104 | tf_op jit(solution)/shard_map/all_gather | solution.py:252
  10.0 251.2 %all-gather.18.cloned.1.call-start = ((), (), s32[]{:S(2)}) async-start(), calls=%async_computation.12 | async-start | bytes 5308416 | tf_op jit(solution)/shard_map/all_gather | solution.py:256
  10.6 330.7 %all-gather.20.cloned.1.call-start = ((), (), s32[]{:S(2)}) async-start(), calls=%async_computation.13 | async-start | bytes 5308416 | tf_op jit(solution)/shard_map/all_gather | solution.py:258
  11.2 371.6 %all-gather.22.cloned.1.call-start = ((), (), s32[]{:S(2)}) async-start(), calls=%async_computation.14 | async-start | bytes 1327104 | tf_op jit(solution)/shard_map/all_gather | solution.py:230
  11.9 689.4 %reduce-scatter.23.cloned.1.call-start = ((), (), s32[]{:S(2)}) async-start(), calls=%async_computation.18 | async-start | bytes 2654208 | tf_op jit(solution)/shard_map/reduce_scatter | solution.py:352
  112.1 29.4 %copy-start.22 = (s32[1,512]{1,0:T(1,128)S(1)}, s32[1,512]{1,0:T(1,128)}, u32[]{:S(2)}) copy-start(s32[1,512]{1,0:T(1,128)} %param.33) | copy-start | bytes 6148
  229.1 160.5 %copy-start.4 = (f32[512,768]{1,0:T(8,128)}, f32[512,768]{1,0:T(8,128)S(1)}, u32[]{:S(2)}) copy-start(f32[512,768]{1,0:T(8,128)S(1)} %get-tuple-element.439) | copy-start | bytes 4718596
  363.2 21.1 %copy-start.25 = (bf16[3]{0:T(256)(128)(2,1)S(1)}, bf16[3]{0:T(256)(128)(2,1)}, u32[]{:S(2)}) copy-start(bf16[3]{0:T(256)(128)(2,1)} %param.53) | copy-start | bytes 22
  389.5 313.4 %reduce-scatter.29.cloned.1.call-start = ((), (), s32[]{:S(2)}) async-start(), calls=%async_computation.21 | async-start | bytes 2654208
  409.4 6.9 copy-start.26
  409.4 7.2 copy-start.6
  409.4 8.3 copy-start
  418.5 11.1 slice-start
  420.3 9.3 copy-start.14
  420.3 9.3 copy-start.5
  420.3 9.3 slice-start.1
  429.6 3.2 copy-start.27
  435.8 143.0 %copy-start.3 = (bf16[1,512,768]{2,1,0:T(8,128)(2,1)S(1)}, bf16[1,512,768]{2,1,0:T(8,128)(2,1)}, u32[]{:S(2)}) copy-start(bf16[1,512,768]{2,1,0:T(8,128)(2,1)} %param.31) | copy-start | bytes 2359300
  584.1 140.4 %reduce-scatter.25.cloned.1.call-start = ((), (), s32[]{:S(2)}) async-start(), calls=%async_computation.19 | async-start | bytes 2654208
  590.6 205.7 %reduce-scatter.27.cloned.1.call-start = ((), (), s32[]{:S(2)}) async-start(), calls=%async_computation.20 | async-start | bytes 2654208
  594.0 3.2 copy-start.9
  597.2 270.8 %reduce-scatter.17.cloned.1.call-start = ((), (), s32[]{:S(2)}) async-start(), calls=%async_computation.15 | async-start | bytes 2654208 | tf_op jit(solution)/shard_map/reduce_scatter | solution.py:342
  600.6 433.4 %reduce-scatter.19.cloned.1.call-start = ((), (), s32[]{:S(2)}) async-start(), calls=%async_computation.16 | async-start | bytes 10616832 | tf_op jit(solution)/shard_map/reduce_scatter | solution.py:346
  609.7 590.2 %reduce-scatter.21.cloned.1.call-start = ((), (), s32[]{:S(2)}) async-start(), calls=%async_computation.17 | async-start | bytes 10616832 | tf_op jit(solution)/shard_map/reduce_scatter | solution.py:348
  619.1 644.5 %reduce-scatter.31.cloned.1.call-start = ((), (), s32[]{:S(2)}) async-start(), calls=%async_computation.22 | async-start | bytes 442368
  621.6 697.5 %all-reduce.25.cloned.1.call-start = ((), (), s32[]{:S(2)}) async-start(), calls=%async_computation.23 | async-start | bytes 4128768 | tf_op jit(solution)/shard_map/psum | solution.py:376
  1202.1 3.3 copy-start.12
  1319.1 10.8 copy-start.16
  (14 other events, 29.5 us)
Sparse Core Ops, SparseCore 0:
  10.2 43.9 all-gather.11
  56.4 40.0 all-gather.13
  98.6 39.8 all-gather.9
  140.5 39.8 all-gather.15
  182.4 78.7 all-gather.17
  263.3 78.0 all-gather.19
  343.5 39.1 all-gather.21
  389.6 67.6 reduce-scatter.22
  584.3 68.1 reduce-scatter.28
  655.8 68.7 reduce-scatter.24
  728.1 68.2 reduce-scatter.26
  799.7 68.2 reduce-scatter.16
  871.5 162.3 reduce-scatter.18
  1037.4 162.5 reduce-scatter.20
  1203.1 60.4 reduce-scatter.30
  1268.0 50.9 all-reduce.24
where the time goes:
time: 1350 us; the launch traced here: 1340 us
  waiting for transfers between devices  748 us (55%)
  matrix products  245 us (18%)
  blocking collectives  164 us (12%)
  local copies, waits for them, and re-layouts  72.1 us (5%)
  loops' own time  47.9 us (4%)
  other arithmetic  40.2 us (3%)
  between operations  20.7 us (2%)
    reduce_scatter x1, waiting for transfers between devices, on_device(): lax.psum_scatter(inner_weight_local, 'fsdp', scatter_dimension=0, tiled=T...  164 us
    reduce_scatter x1, waiting for transfers between devices, on_device(): lax.psum_scatter(outer_weight_local, 'fsdp', scatter_dimension=0, tiled=T...  164 us
    unnamed x20, waiting for transfers between devices  150 us
    all_gather x1, waiting for transfers between devices, on_device(): lax.all_gather(outer_weight, 'fsdp', axis=0, tiled=True)  80.1 us
    unnamed x2, blocking collectives  76.2 us
    reduce_scatter x1, waiting for transfers between devices, on_device(): lax.psum_scatter(output_weight_local, 'fsdp', scatter_dimension=0, tiled=...  69.8 us
    dot_general x10, matrix products, matmul(): return jnp.dot(left_side, right_side, preferred_element_type=jnp.float32)  61.6 us
    dot_general x36, matrix products, one_head(): jnp.einsum('rqd,rkd->rqk', query_head, key_head, preferred_element_type=j...  49.2 us
  transfers between devices with their start and end apart: 16, of which 11 were waited for; matrix products, arithmetic and copies ran while one was open for 25% of the time, Pallas kernels for 0%

commit v1 on v0

v1 whole, which is shorter than its diff:
```python
import functools

import jax
import jax.numpy as jnp
from jax import lax
from jax.experimental import pallas as pl
from jax.experimental.pallas import tpu as pltpu
from jax.sharding import PartitionSpec as P

HEAD_DIM = 64
CLASSES = 3
EPS = 1e-06
NEG = -1000000000.0
SCALE = HEAD_DIM**-0.5
LOW = jnp.bfloat16
F32 = jnp.float32
MESH_AXES = ("dp", "fsdp")
MIB = 1 << 20

QUERY_B, VALUE_B, OUTPUT_B, GAIN1, SHIFT1, OUTER_B, GAIN2, SHIFT2, POOLER_B, INNER_B, CLASS_W = (
    0, 1, 2, 3, 4, 5, 6, 7, 8, 9, 13,
)
TABLE = 16


def dot(a, b, dims=((1,), (0,))):
    return lax.dot_general(a, b, (dims, ((), ())), preferred_element_type=F32)


def dot_nt(a, b):
    return dot(a, b, ((1,), (1,)))


def full(shape):
    zeros = (0,) * len(shape)
    return pl.BlockSpec(shape, lambda *_: zeros)


def call(kernel, outs, in_specs, out_specs, args, *, grid=(1,), scratch=(), prefetch=0, flops=0, moved=0, trans=0, vmem=48):
    return pl.pallas_call(
        kernel,
        out_shape=outs,
        grid_spec=pltpu.PrefetchScalarGridSpec(
            num_scalar_prefetch=prefetch,
            grid=grid,
            in_specs=in_specs,
            out_specs=out_specs,
            scratch_shapes=scratch,
        ),
        compiler_params=pltpu.CompilerParams(
            dimension_semantics=("arbitrary",) * len(grid), vmem_limit_bytes=vmem * MIB
        ),
        cost_estimate=pl.CostEstimate(flops=flops, bytes_accessed=moved, transcendentals=trans),
    )(*args)


def shape(*dims, dtype=LOW):
    return jax.ShapeDtypeStruct(dims, dtype)


def lane_masks(rows):
    lanes = lax.broadcasted_iota(jnp.int32, (rows, 128), 1)
    return lanes < HEAD_DIM


def attention_kernel(tok, wq, wk, wv, table, seg_row, seg_col, q_o, k_o, v_o, ctx_o, lse_o, bias):
    step = pl.program_id(0)
    seq = tok.shape[0]

    @pl.when(step == 0)
    def _():
        bias[...] = jnp.where(seg_col[...] == seg_row[...], 0.0, NEG)

    x = tok[...]
    q = (dot(x, wq[...]) + table[QUERY_B : QUERY_B + 1, :]).astype(LOW)
    k = dot(x, wk[...]).astype(LOW)
    v = (dot(x, wv[...]) + table[VALUE_B : VALUE_B + 1, :]).astype(LOW)
    q_o[...] = q
    k_o[...] = k
    v_o[...] = v
    first = lane_masks(seq)
    zero = jnp.zeros((seq, 128), LOW)
    for pair in range(q.shape[1] // 128):
        cols = slice(pair * 128, pair * 128 + 128)
        q2, k2, v2t = q[:, cols], k[:, cols], v[:, cols].T
        parts = []
        for half in range(2):
            qm = jnp.where(first, q2, zero) if half == 0 else jnp.where(first, zero, q2)
            s = dot_nt(k2, qm) * SCALE + bias[...]
            top = jnp.max(s, axis=0, keepdims=True)
            e = jnp.exp(s - top)
            total = jnp.sum(e, axis=0, keepdims=True)
            out = dot(v2t[half * HEAD_DIM : (half + 1) * HEAD_DIM], e.astype(LOW)) / total
            parts.append(out)
            row = pair * 2 + half
            lse_o[0, row : row + 1, :] = top + jnp.log(total)
        ctx_o[:, cols] = jnp.concatenate(parts, axis=0).astype(LOW).T


def attention(tokens, wq, wk, wv, table, segments):
    seq, width = tokens.shape
    blk = 256
    steps = width // blk
    cols = pl.BlockSpec((seq, blk), lambda i: (0, i))
    wcols = pl.BlockSpec((width, blk), lambda i: (0, i))
    return call(
        attention_kernel,
        (shape(seq, width),) * 4 + (shape(steps, 8, seq, dtype=F32),),
        [full((seq, width)), wcols, wcols, wcols, pl.BlockSpec((TABLE, blk), lambda i: (0, i)), full((1, seq)), full((seq, 1))],
        (cols,) * 4 + (pl.BlockSpec((1, 8, seq), lambda i: (i, 0, 0)),),
        (tokens, wq, wk, wv, table, segments.reshape(1, seq), segments.reshape(seq, 1)),
        grid=(steps,),
        scratch=[pltpu.VMEM((seq, seq), F32)],
        flops=2 * seq * width * (3 * width + 2 * seq),
        moved=8 * seq * width + 6 * width * width,
        trans=seq * seq * width // HEAD_DIM,
    )


def rows_norm(v):
    mean = jnp.mean(v, axis=-1, keepdims=True)
    centered = v - mean
    variance = jnp.mean(centered * centered, axis=-1, keepdims=True)
    scale = lax.rsqrt(variance + EPS)
    return centered * scale, scale


def attended_kernel(ctx, wo, tok, table, n1_o, r1_o, low_o):
    v = dot(ctx[...], wo[...]) + table[OUTPUT_B : OUTPUT_B + 1, :] + tok[...].astype(F32)
    n, r = rows_norm(v)
    n1_o[...] = n
    r1_o[...] = r
    low_o[...] = (n * table[GAIN1 : GAIN1 + 1, :] + table[SHIFT1 : SHIFT1 + 1, :]).astype(LOW)


def attended(ctx, wo, tokens, table):
    seq, width = tokens.shape
    blk = 128
    rows = pl.BlockSpec((blk, width), lambda i: (i, 0))
    return call(
        attended_kernel,
        (shape(seq, width, dtype=F32), shape(seq, 1, dtype=F32), shape(seq, width)),
        [rows, full((width, width)), rows, full((TABLE, width))],
        (rows, pl.BlockSpec((blk, 1), lambda i: (i, 0)), rows),
        (ctx, wo, tokens, table),
        grid=(seq // blk,),
        flops=2 * seq * width * width,
        moved=2 * width * width + 10 * seq * width,
    )


ERFC_POLY = (
    0.2820605933666229,
    0.28293782472610474,
    0.237934872508049,
    0.22901807725429535,
    -0.10879392176866531,
    0.44148358702659607,
    -0.6950507164001465,
    0.44817423820495605,
    -0.13161660730838776,
    0.013852047733962536,
)


def gelu_parts(v):
    u = jnp.abs(v) * (0.5**0.5)
    t = 1.0 / (1.0 + 0.5 * u)
    poly = jnp.full_like(t, ERFC_POLY[-1])
    for coefficient in ERFC_POLY[-2::-1]:
        poly = poly * t + coefficient
    bell = jnp.exp(v * v * -0.5)
    tail = (0.5 * t) * poly * bell
    below = jnp.where(v < 0, tail, 1.0 - tail)
    return v * below, below + v * (bell * 0.3989422804014327)


def inner_kernel(low, wi, bi, act_o, slope_o):
    v = dot(low[...], wi[...]) + bi[...]
    act, slope = gelu_parts(v)
    act_o[...] = act.astype(LOW)
    slope_o[...] = slope.astype(LOW)


def inner(low, wi, bi):
    seq, width = low.shape
    ff = wi.shape[1]
    blk = 512
    cols = pl.BlockSpec((seq, blk), lambda i: (0, i))
    return call(
        inner_kernel,
        (shape(seq, ff), shape(seq, ff)),
        [full((seq, width)), pl.BlockSpec((width, blk), lambda i: (0, i)), pl.BlockSpec((1, blk), lambda i: (0, i))],
        (cols, cols),
        (low, wi, bi),
        grid=(ff // blk,),
        flops=2 * seq * width * ff,
        moved=2 * width * ff + 4 * seq * ff,
        trans=2 * seq * ff,
    )


def outer_kernel(labels, bias3, act, w, n1, table, out_grad, wp, hid_o, sg_o, bg_o, sums_o, head_o, loss_o, acc, n2_s, r2_s):
    step = pl.program_id(0)
    seq, width = n1.shape

    @pl.when(step == 0)
    def _():
        acc[...] = jnp.zeros_like(acc)

    acc[...] += dot(act[...], w[...])

    @pl.when(step == pl.num_programs(0) - 1)
    def _():
        def row(at):
            return table[at : at + 1, :]

        gain2, shift2 = row(GAIN2), row(SHIFT2)
        blk = 64
        for at in range(0, seq, blk):
            rows = slice(at, at + blk)
            v = acc[rows, :] + row(OUTER_B) + (n1[rows, :] * row(GAIN1) + row(SHIFT1))
            n, r = rows_norm(v)
            n2_s[rows, :] = n
            r2_s[rows, :] = r
            hid_o[rows, :] = (n * gain2 + shift2).astype(LOW)
        class_rows = hid_o[0:8, :]
        pooled_pre = dot(class_rows, wp[...])[0:1, :] + row(POOLER_B)
        bent = jnp.tanh(pooled_pre)
        pooled = bent.astype(LOW).astype(F32)
        logits = [
            jnp.sum(pooled * row(CLASS_W + j), axis=-1, keepdims=True) + bias3[j] for j in range(CLASSES)
        ]
        top = functools.reduce(jnp.maximum, logits)
        exps = [jnp.exp(v - top) for v in logits]
        total = functools.reduce(jnp.add, exps)
        label = labels[0]
        hot = [jnp.where(label == j, 1.0, 0.0) for j in range(CLASSES)]
        picked = functools.reduce(jnp.add, [a * b for a, b in zip(logits, hot)])
        loss_o[...] = jnp.broadcast_to(top + jnp.log(total) - picked, loss_o.shape)
        slopes = [(e / total - o).astype(LOW).astype(F32) for e, o in zip(exps, hot)]
        pooled_grad = functools.reduce(
            jnp.add, [g * row(CLASS_W + j) for j, g in enumerate(slopes)]
        )
        pre_grad = (pooled_grad * (1.0 - bent * bent)).astype(LOW)
        row_grad = dot_nt(jnp.broadcast_to(pre_grad, (8, width)), wp[...])[0:1, :]
        head_o[...] = jnp.zeros_like(head_o)
        lanes = lax.broadcasted_iota(jnp.int32, (1, width), 1)
        head_o[0:1, :] = class_rows[0:1, :].astype(F32)
        head_o[1:2, :] = pre_grad.astype(F32)
        head_o[2:3, :] = pooled
        head_o[3:4, :] = functools.reduce(
            jnp.add, [jnp.where(lanes == j, g, 0.0) for j, g in enumerate(slopes)]
        )
        gain_sum = jnp.zeros((1, width), F32)
        shift_sum = jnp.zeros((1, width), F32)
        bias_sum = jnp.zeros((1, width), F32)
        for at in range(0, seq, blk):
            rows = slice(at, at + blk)
            fg = out_grad[rows, :].astype(F32)
            if at == 0:
                lead = lax.broadcasted_iota(jnp.int32, (blk, width), 0) == 0
                fg = fg + jnp.where(lead, jnp.broadcast_to(row_grad, (blk, width)), 0.0)
            n = n2_s[rows, :]
            g = fg * gain2
            gm = jnp.mean(g, axis=-1, keepdims=True)
            gn = jnp.mean(g * n, axis=-1, keepdims=True)
            sg = r2_s[rows, :] * (g - gm - n * gn)
            low = sg.astype(LOW)
            sg_o[rows, :] = sg
            bg_o[rows, :] = low
            gain_sum += jnp.sum(fg * n, axis=0, keepdims=True)
            shift_sum += jnp.sum(fg, axis=0, keepdims=True)
            bias_sum += jnp.sum(low.astype(F32), axis=0, keepdims=True)
        sums_o[...] = jnp.zeros_like(sums_o)
        sums_o[0:1, :] = gain_sum
        sums_o[1:2, :] = shift_sum
        sums_o[2:3, :] = bias_sum


def outer(act, w, n1, table, out_grad, wp, labels, bias3):
    seq, width = n1.shape
    ff = act.shape[1]
    blk = 512
    whole = full((seq, width))
    return call(
        outer_kernel,
        (
            shape(seq, width),
            shape(seq, width, dtype=F32),
            shape(seq, width),
            shape(8, width, dtype=F32),
            shape(8, width, dtype=F32),
            shape(8, 128, dtype=F32),
        ),
        [
            pl.BlockSpec((seq, blk), lambda i, *_: (0, i)),
            pl.BlockSpec((blk, width), lambda i, *_: (i, 0)),
            whole,
            full((TABLE, width)),
            whole,
            full((width, width)),
        ],
        (whole, whole, whole, full((8, width)), full((8, width)), full((8, 128))),
        (labels, bias3, act, w, n1, table, out_grad, wp),
        grid=(ff // blk,),
        scratch=[pltpu.VMEM((seq, width), F32), pltpu.VMEM((seq, width), F32), pltpu.VMEM((seq, 1), F32)],
        prefetch=2,
        flops=2 * seq * width * ff,
        moved=2 * width * ff + 2 * seq * ff + 14 * seq * width,
    )


def inner_back_kernel(bg, w_out, w_in, slope, sg, n1, r1, table, ig_o, ib_o, res_o, ag_o, sums_o, acc):
    step = pl.program_id(0)
    seq, width = n1.shape
    ig = (dot_nt(bg[...], w_out[...]) * slope[...].astype(F32)).astype(LOW)
    ig_o[...] = ig
    ib_o[...] = jnp.sum(ig.astype(F32), axis=0, keepdims=True)

    @pl.when(step == 0)
    def _():
        acc[...] = jnp.zeros_like(acc)

    acc[...] += dot_nt(ig, w_in[...])

    @pl.when(step == pl.num_programs(0) - 1)
    def _():
        gain1 = table[GAIN1 : GAIN1 + 1, :]
        gain_sum = jnp.zeros((1, width), F32)
        shift_sum = jnp.zeros((1, width), F32)
        bias_sum = jnp.zeros((1, width), F32)
        blk = 64
        for at in range(0, seq, blk):
            rows = slice(at, at + blk)
            fg = sg[rows, :] + acc[rows, :]
            n = n1[rows, :]
            g = fg * gain1
            gm = jnp.mean(g, axis=-1, keepdims=True)
            gn = jnp.mean(g * n, axis=-1, keepdims=True)
            res = r1[rows, :] * (g - gm - n * gn)
            low = res.astype(LOW)
            res_o[rows, :] = res
            ag_o[rows, :] = low
            gain_sum += jnp.sum(fg * n, axis=0, keepdims=True)
            shift_sum += jnp.sum(fg, axis=0, keepdims=True)
            bias_sum += jnp.sum(low.astype(F32), axis=0, keepdims=True)
        sums_o[...] = jnp.zeros_like(sums_o)
        sums_o[0:1, :] = gain_sum
        sums_o[1:2, :] = shift_sum
        sums_o[2:3, :] = bias_sum


def inner_back(bg, w_out, w_in, slope, sg, n1, r1, table):
    seq, width = n1.shape
    ff = slope.shape[1]
    blk = 512
    whole = full((seq, width))
    cols = pl.BlockSpec((seq, blk), lambda i: (0, i))
    return call(
        inner_back_kernel,
        (
            shape(seq, ff),
            shape(1, ff, dtype=F32),
            shape(seq, width, dtype=F32),
            shape(seq, width),
            shape(8, width, dtype=F32),
        ),
        [
            whole,
            pl.BlockSpec((blk, width), lambda i: (i, 0)),
            pl.BlockSpec((width, blk), lambda i: (0, i)),
            cols,
            whole,
            whole,
            full((seq, 1)),
            full((TABLE, width)),
        ],
        (cols, pl.BlockSpec((1, blk), lambda i: (0, i)), whole, whole, full((8, width))),
        (bg, w_out, w_in, slope, sg, n1, r1, table),
        grid=(ff // blk,),
        scratch=[pltpu.VMEM((seq, width), F32)],
        flops=4 * seq * width * ff,
        moved=4 * width * ff + 4 * seq * ff + 16 * seq * width,
    )


def attention_back_kernel(q, k, v, lse, ag, wo, seg_row, seg_col, dq_o, dk_o, dv_o, sums_o, bias):
    seq = ag.shape[0]

    @pl.when(pl.program_id(0) == 0)
    def _():
        bias[...] = jnp.where(seg_col[...] == seg_row[...], 0.0, NEG)

    grad = dot_nt(ag[...], wo[...]).astype(LOW)
    first = lane_masks(seq)
    zero = jnp.zeros((seq, 128), LOW)
    sums_o[...] = jnp.zeros_like(sums_o)
    for pair in range(q.shape[1] // 128):
        cols = slice(pair * 128, pair * 128 + 128)
        q2, k2, v2, g2 = q[:, cols], k[:, cols], v[:, cols], grad[:, cols]
        k2t = k2.T
        dqs, dks, dvs = [], [], []
        for half in range(2):
            def own(a):
                return jnp.where(first, a, zero) if half == 0 else jnp.where(first, zero, a)

            row = pair * 2 + half
            s = dot_nt(k2, own(q2)) * SCALE + bias[...]
            p = jnp.exp(s - lse[0, row : row + 1, :])
            dp = dot_nt(v2, own(g2))
            weighted = p * dp
            level = jnp.sum(weighted, axis=0, keepdims=True)
            ds = (weighted - p * level).astype(LOW)
            dvs.append(dot(p.astype(LOW), g2))
            dks.append(dot(ds, q2))
            dqs.append(dot(k2t[half * HEAD_DIM : (half + 1) * HEAD_DIM], ds))
        dq = (jnp.concatenate(dqs, axis=0) * SCALE).astype(LOW).T
        dk = (jnp.where(first, dks[0], dks[1]) * SCALE).astype(LOW)
        dv = jnp.where(first, dvs[0], dvs[1]).astype(LOW)
        dq_o[:, cols] = dq
        dk_o[:, cols] = dk
        dv_o[:, cols] = dv
        sums_o[0:1, cols] = jnp.sum(dq.astype(F32), axis=0, keepdims=True)
        sums_o[1:2, cols] = jnp.sum(dv.astype(F32), axis=0, keepdims=True)


def attention_back(q, k, v, lse, ag, wo, segments):
    seq, width = ag.shape
    blk = 256
    steps = width // blk
    cols = pl.BlockSpec((seq, blk), lambda i: (0, i))
    return call(
        attention_back_kernel,
        (shape(seq, width),) * 3 + (shape(8, width, dtype=F32),),
        [
            cols,
            cols,
            cols,
            pl.BlockSpec((1, 8, seq), lambda i: (i, 0, 0)),
            full((seq, width)),
            pl.BlockSpec((blk, width), lambda i: (i, 0)),
            full((1, seq)),
            full((seq, 1)),
        ],
        (cols,) * 3 + (pl.BlockSpec((8, blk), lambda i: (0, i)),),
        (q, k, v, lse, ag, wo, segments.reshape(1, seq), segments.reshape(seq, 1)),
        grid=(steps,),
        scratch=[pltpu.VMEM((seq, seq), F32)],
        flops=2 * seq * width * (width + 5 * seq),
        moved=16 * seq * width + 2 * width * width,
        trans=seq * seq * width // HEAD_DIM,
    )


def tokens_back_kernel(res, dq, dk, dv, wq, wk, wv, out):
    out[...] = res[...] + dot_nt(dq[...], wq[...]) + dot_nt(dk[...], wk[...]) + dot_nt(dv[...], wv[...])


def tokens_back(res, dq, dk, dv, wq, wk, wv):
    seq, width = res.shape
    blk = 128
    rows = pl.BlockSpec((blk, width), lambda i: (i, 0))
    weight = full((width, width))
    return call(
        tokens_back_kernel,
        shape(seq, width, dtype=F32),
        [rows] * 4 + [weight] * 3,
        rows,
        (res, dq, dk, dv, wq, wk, wv),
        grid=(seq // blk,),
        flops=6 * seq * width * width,
        moved=14 * seq * width + 6 * width * width,
    )


def grads(where, lefts, which, rights, other, add=None):
    seq = lefts[0].shape[0]
    parts = lefts[0].shape[1] // 16
    widths = tuple((w, r.shape[1] // 2) for w, r in zip(which, rights))
    total = sum(w for _, w in widths)
    half = (lambda i, where: (0, 1 - where[3])) if other else (lambda i, where: (0, where[3]))
    right_specs = [pl.BlockSpec((seq, w), half) for _, w in widths]
    piece = (4, parts, total)
    specs = [full(a.shape) for a in lefts] + right_specs
    args = [where, *lefts, *rights]
    if add is not None:
        specs += [full(piece)] * 4
        args += list(add)

    def kernel(where_ref, *refs):
        n, m = len(lefts), len(rights)
        left_refs, right_refs = refs[:n], refs[n : n + m]
        rest = refs[n + m :]
        grad_body(where_ref, left_refs, right_refs, rest, widths, parts, add is not None)

    return call(
        kernel,
        (shape(*piece),) * 4,
        specs,
        (full(piece),) * 4,
        args,
        scratch=[pltpu.VMEM((a.shape[1], seq), LOW) for a in lefts],
        prefetch=1,
        flops=2 * seq * 16 * parts * total,
        moved=2 * 16 * parts * total + 2 * seq * 16 * parts,
    )


def grad_body(where, lefts, rights, rest, widths, parts, with_add):
    adds = rest[:4] if with_add else None
    outs = rest[4:8] if with_add else rest[:4]
    turned = rest[8:] if with_add else rest[4:]
    x, y = where[0], where[1]
    for left, store in zip(lefts, turned):
        for start in range(0, left.shape[1], 256):
            store[start : start + 256, :] = left[:, start : start + 256].T
    for place in range(4):
        hh = jnp.bitwise_xor(x, place // 2)
        yy = jnp.bitwise_xor(y, place % 2)
        column = 0
        for (which, width), right in zip(widths, rights):
            rows = [
                turned[which][pl.ds(pl.multiple_of(((z * 2 + yy) * 2 + hh) * parts, 16), parts), :]
                for z in range(4)
            ]
            got = dot(jnp.concatenate(rows, axis=0), right[...]).reshape(4, parts, width)
            cols = slice(column, column + width)
            if with_add:
                got = got + adds[place][:, :, cols].astype(F32)
            outs[place][:, :, cols] = got.astype(LOW)
            column += width


def weights_kernel(spans, where, *refs):
    pieces, outs, sem = refs[:8], refs[8:-1], refs[-1]
    copies = []
    for place in range(8):
        hh = jnp.bitwise_xor(where[0], place // 4)
        yy = jnp.bitwise_xor(where[1], place // 2 % 2)
        cc = jnp.bitwise_xor(where[3], place % 2)
        for (start, width), out in zip(spans, outs):
            to = out.at[:, yy, hh, :, pl.ds(pl.multiple_of(cc * width, 128), width)]
            copies.append(pltpu.make_async_copy(pieces[place].at[:, :, start : start + width], to, sem.at[len(copies)]))
    for copy in copies:
        copy.start()
    for copy in copies:
        copy.wait()


def place_weights(where, pieces, widths):
    parts = pieces[0].shape[1]
    spans, start = [], 0
    for width in widths:
        spans.append((start, width // 2))
        start += width // 2
    anywhere = pl.BlockSpec(memory_space=pl.ANY)
    outs = call(
        functools.partial(weights_kernel, tuple(spans)),
        tuple(shape(4, 2, 2, parts, w) for w in widths),
        [anywhere] * 8,
        (anywhere,) * len(widths),
        (where, *pieces),
        scratch=[pltpu.SemaphoreType.DMA((8 * len(widths),))],
        prefetch=1,
        moved=4 * 16 * parts * sum(widths),
        vmem=4,
    )
    return [o.reshape(16 * parts, w) for o, w in zip(outs, widths)]


def shards_kernel(spans, where, *refs):
    pieces, outs = refs[:4], refs[4:]
    for place in range(4):
        hh = jnp.bitwise_xor(where[0], place // 2)
        for core in range(2):
            @pl.when(jnp.bitwise_xor(where[3], place % 2) == core)
            def _():
                for (start, width), out in zip(spans, outs):
                    out[hh, :, core * width : (core + 1) * width] = pieces[place][
                        :, start : start + width
                    ].astype(F32)


def place_shards(where, pieces, widths):
    parts = pieces[0].shape[0]
    spans, start = [], 0
    for width in widths:
        spans.append((start, width // 2))
        start += width // 2
    outs = call(
        functools.partial(shards_kernel, tuple(spans)),
        tuple(shape(2, parts, w, dtype=F32) for w in widths),
        [full(pieces[0].shape)] * 4,
        tuple(full((2, parts, w)) for w in widths),
        (where, *pieces),
        prefetch=1,
        moved=12 * parts * sum(widths),
        vmem=16,
    )
    return [o.reshape(2 * parts, w) for o, w in zip(outs, widths)]


def device(x, core, z, y):
    return (x * 2 + core) * 8 + z * 2 + y


ALL = [(x, core, z, y) for x in range(2) for core in range(2) for z in range(4) for y in range(2)]
CORE_SWAP = [(device(*a), device(a[0], 1 - a[1], a[2], a[3])) for a in ALL]
X_SWAP = [(device(*a), device(1 - a[0], a[1], a[2], a[3])) for a in ALL]
Y_SWAP = [(device(*a), device(a[0], a[1], a[2], 1 - a[3])) for a in ALL]
Z_SWAPS = [[(device(*a), device(a[0], a[1], a[2] ^ d, a[3])) for a in ALL] for d in (1, 2)]
Z_GROUPS = [
    [device(x, core, z, y) for z in range(4)] for x in range(2) for core in range(2) for y in range(2)
]


def swap(a, pairs):
    return lax.ppermute(a, MESH_AXES, pairs)


def z_exchange(a):
    four, rows, columns = a.shape
    got = lax.all_to_all(
        a.reshape(four * rows, columns), MESH_AXES, 0, 0, axis_index_groups=Z_GROUPS, tiled=True
    )
    return got.reshape(a.shape)


def gather_weights(place, where, shards, over_y_last):
    x, core = place
    cut = []
    for shard in shards:
        rows, width = shard.shape
        cut.append(lax.dynamic_slice(shard, (x * (rows // 2), core * (width // 2)), (rows // 2, width // 2)))
    own = jnp.concatenate(cut, axis=1) if len(cut) > 1 else cut[0]
    near = z_exchange(jnp.broadcast_to(own[None], (4, *own.shape)))
    by_x = swap(near, X_SWAP)
    by_y = swap(near, Y_SWAP)
    both = swap(by_x, Y_SWAP) if over_y_last else swap(by_y, X_SWAP)
    pieces = []
    for piece in (near, by_y, by_x, both):
        pieces += [piece, swap(piece, CORE_SWAP)]
    return place_weights(where, pieces, [s.shape[1] for s in shards])


def reduce_shards(where, same, by_y, by_x, both, over_y_first, widths):
    if over_y_first:
        got = swap(both, Y_SWAP)
        by_x = (by_x.astype(F32) + got.astype(F32)).astype(LOW)
    else:
        got = swap(both, X_SWAP)
        by_y = (by_y.astype(F32) + got.astype(F32)).astype(LOW)
    from_x, from_y = swap(by_x, X_SWAP), swap(by_y, Y_SWAP)
    total = (same.astype(F32) + from_x.astype(F32) + from_y.astype(F32)).astype(LOW)
    own = jnp.sum(z_exchange(total).astype(F32), axis=0).astype(LOW)
    across = swap(own, X_SWAP)
    pieces = (own, swap(own, CORE_SWAP), across, swap(across, CORE_SWAP))
    return place_shards(where, pieces, widths)


def on_device(
    by_links,
    tokens,
    out_grad,
    segment_ids,
    labels,
    query_weight,
    query_bias,
    key_weight,
    value_weight,
    value_bias,
    output_weight,
    output_bias,
    first_norm_gain,
    first_norm_shift,
    inner_weight,
    inner_bias,
    outer_weight,
    outer_bias,
    second_norm_gain,
    second_norm_shift,
    pooler_weight,
    pooler_bias,
    class_weight,
    class_bias,
):
    _, seq, width = tokens.shape
    tokens = tokens.reshape(seq, width)
    out_grad = out_grad.reshape(seq, width)
    dp, fsdp = lax.axis_index("dp"), lax.axis_index("fsdp")
    where = jnp.stack([dp // 2, fsdp % 2, fsdp // 2, dp % 2]).astype(jnp.int32)
    local = query_bias.shape[0]
    shards = width // local
    ff = inner_weight.shape[1]

    small = jnp.concatenate(
        [
            jnp.stack(
                [
                    query_bias,
                    value_bias,
                    output_bias,
                    first_norm_gain,
                    first_norm_shift,
                    outer_bias,
                    second_norm_gain,
                    second_norm_shift,
                    pooler_bias,
                ]
            ),
            inner_bias.reshape(ff // width, local),
            class_weight.T,
        ]
    )

    def everywhere(a, axis, count):
        if not by_links:
            return lax.all_gather(a, axis)
        rows, columns = a.shape
        got = lax.all_to_all(
            jnp.broadcast_to(a[None], (count, rows, columns)).reshape(count * rows, columns), axis, 0, 0, tiled=True
        )
        return got.reshape(count, rows, columns)

    got = everywhere(small, "fsdp", shards).astype(F32)
    table = jnp.transpose(got, (1, 0, 2)).reshape(TABLE, width)
    inner_row = got[:, INNER_B:CLASS_W, :].reshape(1, ff)

    if by_links:
        place = (where[0], where[3])
        wq, wk, wv = gather_weights(place, where, [query_weight, key_weight, value_weight], False)
        wo, wp = gather_weights(place, where, [output_weight, pooler_weight], False)
        (wi,) = gather_weights(place, where, [inner_weight], True)
        (wf,) = gather_weights(place, where, [outer_weight], False)
    else:
        wq, wk, wv, wo, wp, wi, wf = (
            lax.all_gather(w, "fsdp", axis=0, tiled=True)
            for w in (
                query_weight,
                key_weight,
                value_weight,
                output_weight,
                pooler_weight,
                inner_weight,
                outer_weight,
            )
        )

    q, k, v, context, lse = attention(tokens, wq, wk, wv, table, segment_ids)
    n1, r1, first_low = attended(context, wo, tokens, table)
    activated, slope = inner(first_low, wi, inner_row)
    hidden, second_grad, branch_grad, sums2, head, loss = outer(
        activated, wf, n1, table, out_grad, wp, labels, class_bias.astype(F32)
    )
    if by_links:
        other = grads(where, [activated], [0], [branch_grad], True)
        other = [swap(a, CORE_SWAP) for a in other]
    inner_grad, inner_sums, residual_grad, attended_grad, sums1 = inner_back(
        branch_grad, wf, wi, slope, second_grad, n1, r1, table
    )
    if by_links:
        mine = grads(where, [activated], [0], [branch_grad], False, other)
        (outer_grad,) = reduce_shards(where, *mine, True, [width])
        lefts, rights = [first_low, context], [inner_grad, attended_grad]
        other = grads(where, lefts, [0, 1], rights, True)
        other = [swap(a, CORE_SWAP) for a in other]
    dq, dk, dv, sums0 = attention_back(q, k, v, lse, attended_grad, wo, segment_ids)
    if by_links:
        mine = grads(where, lefts, [0, 1], rights, False, other)
        inner_weight_grad, output_grad = reduce_shards(where, *mine, False, [ff, width])
        rights = [dq, dk, dv]
        other = grads(where, [tokens], [0, 0, 0], rights, True)
        other = [swap(a, CORE_SWAP) for a in other]
        mine = grads(where, [tokens], [0, 0, 0], rights, False, other)
        query_grad, key_grad, value_grad = reduce_shards(where, *mine, True, [width] * 3)
    else:
        def reduced(left, right):
            local_grad = lax.dot_general(left, right, (((0,), (0,)), ((), ())), preferred_element_type=F32)
            shard = lax.psum_scatter(local_grad, "fsdp", scatter_dimension=0, tiled=True)
            return lax.psum(shard.astype(LOW), "dp").astype(F32)

        outer_grad = reduced(activated, branch_grad)
        inner_weight_grad = reduced(first_low, inner_grad)
        output_grad = reduced(context, attended_grad)
        query_grad, key_grad, value_grad = (reduced(tokens, d) for d in (dq, dk, dv))
    tokens_grad = tokens_back(residual_grad, dq, dk, dv, wq, wk, wv)

    sums = jnp.concatenate([sums2[:3], sums1[:3], sums0[:2], inner_sums.reshape(ff // width, width)])
    if by_links:
        for pairs in (CORE_SWAP, X_SWAP, Y_SWAP, *Z_SWAPS):
            sums = sums + swap(sums, pairs)
    else:
        sums = lax.psum(sums, MESH_AXES)
    vectors = lax.dynamic_slice(sums, (0, fsdp * local), (8, local))
    inner_bias_grad = lax.dynamic_slice(sums[8:].reshape(ff), (fsdp * (ff // shards),), (ff // shards,))

    heads = everywhere(head.astype(LOW), "fsdp", shards).reshape(shards * 8, width)
    heads = everywhere(heads, "dp", lax.axis_size("dp")).reshape(-1, 8, width)
    class_rows, pre_grads, pooled = heads[:, 0], heads[:, 1], heads[:, 2]
    logit_grads = heads[:, 3, :CLASSES]

    def own_columns(a):
        return lax.dynamic_slice(a, (0, fsdp * local), (a.shape[0], local))

    def over_rows(a, b):
        return lax.dot_general(a, b, (((0,), (0,)), ((), ())), preferred_element_type=F32)

    pooler_grad = over_rows(own_columns(class_rows), pre_grads)
    pooler_bias_grad = jnp.sum(own_columns(pre_grads).astype(F32), axis=0)
    class_grad = over_rows(own_columns(pooled), logit_grads)
    class_bias_grad = jnp.sum(logit_grads.astype(F32), axis=0)

    return (
        hidden[None],
        tokens_grad[None],
        loss[0, :1],
        query_grad,
        vectors[6],
        key_grad,
        value_grad,
        vectors[7],
        output_grad,
        vectors[5],
        vectors[3],
        vectors[4],
        inner_weight_grad,
        inner_bias_grad,
        outer_grad,
        vectors[2],
        vectors[0],
        vectors[1],
        pooler_grad,
        pooler_bias_grad,
        class_grad,
        class_bias_grad,
    )


def solution(mesh):
    sizes = dict(mesh.shape)
    by_links = sizes == {"dp": 4, "fsdp": 8}
    rows = P(MESH_AXES, None, None)
    ids = P(MESH_AXES, None)
    row = P(MESH_AXES)
    matrix = P("fsdp", None)
    vector = P("fsdp")
    return jax.shard_map(
        functools.partial(on_device, by_links),
        mesh=mesh,
        in_specs=(
            rows, rows, ids, row,
            matrix, vector, matrix, matrix, vector, matrix, vector, vector, vector,
            matrix, vector, matrix, vector, vector, vector, matrix, vector, matrix, P(),
        ),
        out_specs=(
            rows, rows, row,
            matrix, vector, matrix, matrix, vector, matrix, vector, vector, vector,
            matrix, vector, matrix, vector, vector, vector, matrix, vector, matrix, P(),
        ),
        check_vma=False,
    )
```

time: 1350 us -> 409 us (0.30)
  waiting for transfers between devices: 748 us -> 122 us
  matrix products: 245 us -> 1.64 us
  blocking collectives: 164 us -> 0 us
  Pallas kernels: 0 us -> 113 us
  starting transfers between devices: 0.85 us -> 90.4 us
  loops' own time: 47.9 us -> 0 us
  local copies, waits for them, and re-layouts: 72.1 us -> 51.5 us
  between operations: 20.7 us -> 2.59 us
  other arithmetic: 40.2 us -> 22.8 us
    reduce_scatter x4 -> x0, waiting for transfers between devices: 398 us -> none  [the longest x1 164 us: on_device(): lax.psum_scatter(inner_weight_local, 'fsdp', scatter_dimension=0, tiled=T...]
    dot_general x132 -> x2, matrix products: 245 us -> 1.64 us  [over_rows(): lax.dot_general(a, b, (((0,), (0,)), ((), ())), preferred_element_type=F32)]
    all_gather x7 -> x0, waiting for transfers between devices: 156 us -> none  [the longest x1 80.1 us: on_device(): lax.all_gather(outer_weight, 'fsdp', axis=0, tiled=True)]
    unnamed x20 -> x0, waiting for transfers between devices: 150 us -> none
    pallas_call x0 -> x20, Pallas kernels: none -> 113 us  [call(): pl.pallas_call(kernel, out_shape=outs, grid_spec=pltpu.PrefetchScalarGrid...]
    ppermute x0 -> x63, waiting for transfers between devices: none -> 79.5 us  [swap(): return lax.ppermute(a, MESH_AXES, pairs)]
    unnamed x2 -> x0, blocking collectives: 76.2 us -> none
    another operation x3 -> x0, loops' own time: 47.9 us -> none  [the longest x1 31.4 us: attention_back(): query_stack, key_stack, value_stack = lax.map(one_head, jnp.arange(HEADS))]
  transfers between devices with their start and end apart: 16 -> 73, of which waited for: 11 -> 22; matrix products, arithmetic and copies ran while one was open for 25% -> 10% of each run, Pallas kernels for 0% -> 17%
where the time goes in v1:
time: 409 us; the launch traced here: 403 us
  waiting for transfers between devices  122 us (30%)
  Pallas kernels  113 us (28%)
  starting transfers between devices  90.4 us (22%)
  local copies, waits for them, and re-layouts  51.5 us (13%)
  other arithmetic  22.8 us (6%)
    pallas_call x20, Pallas kernels, call(): pl.pallas_call(kernel, out_shape=outs, grid_spec=pltpu.PrefetchScalarGrid...  113 us
    ppermute x63, waiting for transfers between devices, swap(): return lax.ppermute(a, MESH_AXES, pairs)  79.5 us
    ppermute x63, starting transfers between devices, swap(): return lax.ppermute(a, MESH_AXES, pairs)  44.8 us
    all_to_all x7, waiting for transfers between devices, z_exchange(): lax.all_to_all(a.reshape(four * rows, columns), MESH_AXES, 0, 0, axis_ind...  40.8 us
    unnamed x146, local copies, waits for them, and re-layouts  32.9 us
    all_to_all x7, starting transfers between devices, z_exchange(): lax.all_to_all(a.reshape(four * rows, columns), MESH_AXES, 0, 0, axis_ind...  30.7 us
    all_to_all x3, starting transfers between devices, everywhere(): lax.all_to_all(jnp.broadcast_to(a[None], (count, rows, columns)).reshape(...  14.9 us
  transfers between devices with their start and end apart: 73, of which 22 were waited for; matrix products, arithmetic and copies ran while one was open for 10% of the time, Pallas kernels for 17%

profile of v1, /device:TPU:0, one launch (start us, length us, event | category | flops | bytes accessed | tf_op | source)
XLA Modules:
  0.0 403.5 jit_solution(10373085604014028590)
XLA Ops:
  3.0 6.3 %all-to-all-start.2 = ((bf16[4,48,768]{2,1,0:T(8,128)(2,1)}), bf16[4,48,768]{2,1,0:T(8,128)(2,1)S(1)}, u32[]{:S(2)}, u32[]{:S(2)}) async-start(bf16[4,48,768]{2,1,0:T(8,128)(2,1)} %broadcast_in_dim.22), calls=%async_computation.2 | async-start | bytes 589824 | tf_op jit(solution)/shard_map/all_to_all | solution.py:624
  9.4 9.6 %all-to-all-done.2.refs_0_ = bf16[4,48,768]{2,1,0:T(8,128)(2,1)S(1)} async-done(((bf16[4,48,768]{2,1,0:T(8,128)(2,1)}), bf16[4,48,768]{2,1,0:T(8,128)(2,1)S(1)}, u32[]{:S(2)}, u32[]{:S(2)}) %all-to-all-start.2) | async-done | bytes 294944 | tf_op jit(solution)/shard_map/all_to_all | solution.py:624
  24.2 10.2 %all-to-all-done.refs_0_ = bf16[4,48,1152]{2,1,0:T(8,128)(2,1)S(1)} async-done(((bf16[4,48,1152]{2,1,0:T(8,128)(2,1)}), bf16[4,48,1152]{2,1,0:T(8,128)(2,1)S(1)}, u32[]{:S(2)}, u32[]{:S(2)}) %all-to-all-start) | async-done | bytes 442400 | tf_op jit(solution)/shard_map/all_to_all | solution.py:624
  35.2 3.6 all-to-all-start.3
  42.9 9.9 %all-to-all-done.3.refs_0_ = bf16[4,48,1536]{2,1,0:T(8,128)(2,1)S(1)} async-done(((bf16[4,48,1536]{2,1,0:T(8,128)(2,1)}), bf16[4,48,1536]{2,1,0:T(8,128)(2,1)S(1)}, u32[]{:S(2)}, u32[]{:S(2)}) %all-to-all-start.3) | async-done | bytes 589856 | tf_op jit(solution)/shard_map/all_to_all | solution.py:624
  63.4 3.8 collective-permute-done.12.refs_6_
  71.7 4.3 %collective-permute-done.3.refs_4_ = bf16[4,48,1152]{2,1,0:T(8,128)(2,1)} collective-permute-done((bf16[4,48,1152]{2,1,0:T(8,128)(2,1)S(1)}, bf16[4,48,1152]{2,1,0:T(8,128)(2,1)}, u32[]{:S(2)}, u32[]{:S(2)}) %collective-permute-start.3) | collective-permute-done | bytes 442400 | tf_op jit(solution)/shard_map/ppermute | solution.py:619
  79.4 9.1 %collective-permute-done.17.refs_4_ = bf16[4,48,1536]{2,1,0:T(8,128)(2,1)S(1)} collective-permute-done((bf16[4,48,1536]{2,1,0:T(8,128)(2,1)S(1)}, bf16[4,48,1536]{2,1,0:T(8,128)(2,1)S(1)}, u32[]{:S(2)}, u32[]{:S(2)}) %collective-permute-start.17) | collective-permute-done | bytes 589856 | tf_op jit(solution)/shard_map/ppermute | solution.py:619
  90.6 7.8 %collective-permute-done.22.refs_2_ = bf16[4,192,384]{2,1,0:T(8,128)(2,1)} collective-permute-done((bf16[4,192,384]{2,1,0:T(8,128)(2,1)S(1)}, bf16[4,192,384]{2,1,0:T(8,128)(2,1)}, u32[]{:S(2)}, u32[]{:S(2)}) %collective-permute-start.22) | collective-permute-done | bytes 589856 | tf_op jit(solution)/shard_map/ppermute | solution.py:619
  101.3 7.1 %collective-permute-done.5.refs_6_ = bf16[4,48,1152]{2,1,0:T(8,128)(2,1)} collective-permute-done((bf16[4,48,1152]{2,1,0:T(8,128)(2,1)S(1)}, bf16[4,48,1152]{2,1,0:T(8,128)(2,1)}, u32[]{:S(2)}, u32[]{:S(2)}) %collective-permute-start.5) | collective-permute-done | bytes 442400 | tf_op jit(solution)/shard_map/ppermute | solution.py:619
  113.8 5.9 %all-to-all-start.1 = ((bf16[8,16,96]{2,1,0:T(8,128)(2,1)}), bf16[8,16,96]{2,1,0:T(8,128)(2,1)}, u32[]{:S(2)}, u32[]{:S(2)}) async-start(bf16[8,16,96]{2,1,0:T(8,128)(2,1)} %broadcast_in_dim.21), calls=%async_computation.1 | async-start | bytes 65536 | tf_op jit(solution)/shard_map/all_to_all | solution.py:721
  141.1 10.2 %shard_map.391 = (bf16[512,768]{1,0:T(8,128)(2,1)S(1)}, bf16[512,768]{1,0:T(8,128)(2,1)S(1)}, bf16[512,768]{1,0:T(8,128)(2,1)S(1)}, bf16[512,768]{1,0:T(8,128)(2,1)S(1)}, f32[3,8,512]{2,1,0:T(8,128)S(1)}) custom-call(bf16[512,768]{1,0:T(8,128)(2,1)S(1)} %bitcast.70, bf16[768,768]{1,0:T(8,128)(2,1)S(1)} %bitcast.74, bf16[768,768]{1,0:T(8,128)(2,1)} %bitcast.76, ...), custom_call_target="tpu_custom_call" | custom-call | flops 2617245696 | bytes 6684672 | tf_op jit(solution)/shard_map/pallas_call | solution.py:40
  161.1 12.8 %shard_map.395 = (bf16[512,3072]{1,0:T(8,128)(2,1)S(1)}, bf16[512,3072]{1,0:T(8,128)(2,1)}) custom-call(bf16[512,768]{1,0:T(8,128)(2,1)S(1)} %get-tuple-element.86.low.refs_0_, bf16[768,3072]{1,0:T(8,128)(2,1)} %bitcast.68, f32[1,3072]{1,0:T(1,128)S(1)} %reshape.186.bi), custom_call_target="tpu_custom_call" | custom-call | flops 2415919104 | bytes 11010048 | tf_op jit(solution)/shard_map/pallas_call | solution.py:40
  173.9 3.5 shard_map.396
  179.7 10.3 %shard_map.397 = (bf16[512,768]{1,0:T(8,128)(2,1)}, f32[512,768]{1,0:T(8,128)S(1)}, bf16[512,768]{1,0:T(8,128)(2,1)S(1)}, f32[8,768]{1,0:T(8,128)S(1)}, f32[8,768]{1,0:T(8,128)S(1)}, /*index=5*/f32[8,128]{1,0:T(8,128)S(1)}) custom-call(s32[1]{0:T(128)S(6)} %copy.73.labels, f32[3]{0:T(128)S(1)} %convert_element_type.85.bias3, bf16[512,3072]{1,0:T(8,128)(2,1)} %copy-done.1, ...), custom_call_target="tpu_custom_call" | custom-call | flops 2415919104 | bytes 13369344 | tf_op jit(solution)/shard_map/pallas_call | solution.py:40
  190.0 14.2 %shard_map.398 = (bf16[512,3072]{1,0:T(8,128)(2,1)}, f32[1,3072]{1,0:T(1,128)S(1)}, f32[512,768]{1,0:T(8,128)S(1)}, bf16[512,768]{1,0:T(8,128)(2,1)S(1)}, f32[8,768]{1,0:T(8,128)S(1)}) custom-call(bf16[512,768]{1,0:T(8,128)(2,1)S(1)} %get-tuple-element.91.bg.refs_1_, bf16[3072,768]{1,0:T(8,128)(2,1)} %bitcast.67, bf16[768,3072]{1,0:T(8,128)(2,1)} %bitcast.69, ...), custom_call_target="tpu_custom_call" | custom-call | flops 4831838208 | bytes 22020096 | tf_op jit(solution)/shard_map/pallas_call | solution.py:40
  205.4 12.3 %shard_map.399 = (bf16[512,768]{1,0:T(8,128)(2,1)S(1)}, bf16[512,768]{1,0:T(8,128)(2,1)S(1)}, bf16[512,768]{1,0:T(8,128)(2,1)S(1)}, f32[8,768]{1,0:T(8,128)S(1)}) custom-call(bf16[512,768]{1,0:T(8,128)(2,1)S(1)} %copy-done.63, bf16[512,768]{1,0:T(8,128)(2,1)S(1)} %copy-done.65, bf16[512,768]{1,0:T(8,128)(2,1)S(1)} %copy-done.67, ...), custom_call_target="tpu_custom_call" | custom-call | flops 2617245696 | bytes 7471104 | tf_op jit(solution)/shard_map/pallas_call | solution.py:40
  221.0 5.1 %shard_map.407 = (bf16[4,192,384]{2,1,0:T(8,128)(2,1)S(1)}, bf16[4,192,384]{2,1,0:T(8,128)(2,1)S(1)}, bf16[4,192,384]{2,1,0:T(8,128)(2,1)S(1)}, bf16[4,192,384]{2,1,0:T(8,128)(2,1)S(1)}) custom-call(s32[4]{0:T(128)S(1)} %pad_add_fusion.where.where_ref, bf16[512,3072]{1,0:T(8,128)(2,1)} %copy-done.1, bf16[512,768]{1,0:T(8,128)(2,1)S(1)} %get-tuple-element.91.bg.refs_1_), custom_call_target="tpu_custom_call" | custom-call | flops 1207959552 | bytes 5505024 | tf_op jit(solution)/shard_map/pallas_call | solution.py:40
  227.2 4.0 %shard_map.402 = (bf16[4,48,1152]{2,1,0:T(8,128)(2,1)S(1)}, bf16[4,48,1152]{2,1,0:T(8,128)(2,1)}, bf16[4,48,1152]{2,1,0:T(8,128)(2,1)S(1)}, bf16[4,48,1152]{2,1,0:T(8,128)(2,1)}) custom-call(s32[4]{0:T(128)S(1)} %pad_add_fusion.where.where_ref, bf16[512,768]{1,0:T(8,128)(2,1)S(1)} %bitcast.73, bf16[512,768]{1,0:T(8,128)(2,1)S(1)} %get-tuple-element.101.dq.refs_1_, ...), custom_call_target="tpu_custom_call" | custom-call | flops 905969664 | bytes 2555904 | tf_op jit(solution)/shard_map/pallas_call | solution.py:40
  233.3 5.0 %shard_map.404 = (bf16[4,48,1920]{2,1,0:T(8,128)(2,1)}, bf16[4,48,1920]{2,1,0:T(8,128)(2,1)}, bf16[4,48,1920]{2,1,0:T(8,128)(2,1)}, bf16[4,48,1920]{2,1,0:T(8,128)(2,1)}) custom-call(s32[4]{0:T(128)S(1)} %pad_add_fusion.where.where_ref, bf16[512,768]{1,0:T(8,128)(2,1)S(1)} %get-tuple-element.86.low.refs_0_, ...), custom_call_target="tpu_custom_call" | custom-call | flops 1509949440 | bytes 3735552 | tf_op jit(solution)/shard_map/pallas_call | solution.py:40
  243.4 4.9 %all-to-all-start.8 = ((bf16[8,8,768]{2,1,0:T(8,128)(2,1)}), bf16[8,8,768]{2,1,0:T(8,128)(2,1)S(1)}, u32[]{:S(2)}, u32[]{:S(2)}) async-start(bf16[8,8,768]{2,1,0:T(8,128)(2,1)} %broadcast_in_dim.27), calls=%async_computation.8 | async-start | bytes 196608 | tf_op jit(solution)/shard_map/all_to_all | solution.py:721
  252.5 5.9 %shard_map.408 = (bf16[4,192,384]{2,1,0:T(8,128)(2,1)S(1)}, bf16[4,192,384]{2,1,0:T(8,128)(2,1)S(1)}, bf16[4,192,384]{2,1,0:T(8,128)(2,1)S(1)}, bf16[4,192,384]{2,1,0:T(8,128)(2,1)}) custom-call(s32[4]{0:T(128)S(1)} %pad_add_fusion.where.where_ref, bf16[512,3072]{1,0:T(8,128)(2,1)} %copy-done.1, bf16[512,768]{1,0:T(8,128)(2,1)S(1)} %copy-done.20, ...), custom_call_target="tpu_custom_call" | custom-call | flops 1207959552 | bytes 5505024 | tf_op jit(solution)/shard_map/pallas_call | solution.py:40
  265.2 4.1 %all-to-all-start.9 = ((bf16[4,64,768]{2,1,0:T(8,128)(2,1)}), bf16[4,64,768]{2,1,0:T(8,128)(2,1)}, u32[]{:S(2)}, u32[]{:S(2)}) async-start(bf16[4,64,768]{2,1,0:T(8,128)(2,1)} %broadcast_in_dim.58), calls=%async_computation.9 | async-start | bytes 786432 | tf_op jit(solution)/shard_map/all_to_all | solution.py:721
  271.1 6.2 %shard_map.405 = (bf16[4,48,1920]{2,1,0:T(8,128)(2,1)S(1)}, bf16[4,48,1920]{2,1,0:T(8,128)(2,1)S(1)}, bf16[4,48,1920]{2,1,0:T(8,128)(2,1)}, bf16[4,48,1920]{2,1,0:T(8,128)(2,1)}) custom-call(s32[4]{0:T(128)S(1)} %pad_add_fusion.where.where_ref, bf16[512,768]{1,0:T(8,128)(2,1)} %copy-done.17, bf16[512,768]{1,0:T(8,128)(2,1)} %copy-done.6, ...), custom_call_target="tpu_custom_call" | custom-call | flops 1509949440 | bytes 3735552 | tf_op jit(solution)/shard_map/pallas_call | solution.py:40
  288.2 5.1 %all-to-all-start.5 = ((bf16[4,48,1152]{2,1,0:T(8,128)(2,1)}), bf16[4,48,1152]{2,1,0:T(8,128)(2,1)}, u32[]{:S(2)}, u32[]{:S(2)}) async-start(bf16[4,48,1152]{2,1,0:T(8,128)(2,1)} %add_convert_fusion.4), calls=%async_computation.5 | async-start | bytes 884736 | tf_op jit(solution)/shard_map/all_to_all | solution.py:624
  293.3 4.5 %collective-permute-done.48 = bf16[4,48,1920]{2,1,0:T(8,128)(2,1)} collective-permute-done((bf16[4,48,1920]{2,1,0:T(8,128)(2,1)}, bf16[4,48,1920]{2,1,0:T(8,128)(2,1)}, u32[]{:S(2)}, u32[]{:S(2)}) %collective-permute-start.48) | collective-permute-done | bytes 737312 | tf_op jit(solution)/shard_map/ppermute | solution.py:619
  300.3 25.1 %collective-permute-done.58 = bf16[4,192,384]{2,1,0:T(8,128)(2,1)} collective-permute-done((bf16[4,192,384]{2,1,0:T(8,128)(2,1)}, bf16[4,192,384]{2,1,0:T(8,128)(2,1)}, u32[]{:S(2)}, u32[]{:S(2)}) %collective-permute-start.58) | collective-permute-done | bytes 589856 | tf_op jit(solution)/shard_map/ppermute | solution.py:619
  327.7 4.5 %all-to-all-start.7 = ((bf16[4,192,384]{2,1,0:T(8,128)(2,1)}), bf16[4,192,384]{2,1,0:T(8,128)(2,1)}, u32[]{:S(2)}, u32[]{:S(2)}) async-start(bf16[4,192,384]{2,1,0:T(8,128)(2,1)} %add_convert_fusion.2), calls=%async_computation.7 | async-start | bytes 1179648 | tf_op jit(solution)/shard_map/all_to_all | solution.py:624
  336.4 11.2 %all-to-all-done.7 = bf16[4,192,384]{2,1,0:T(8,128)(2,1)} async-done(((bf16[4,192,384]{2,1,0:T(8,128)(2,1)}), bf16[4,192,384]{2,1,0:T(8,128)(2,1)}, u32[]{:S(2)}, u32[]{:S(2)}) %all-to-all-start.7) | async-done | bytes 589856 | tf_op jit(solution)/shard_map/all_to_all | solution.py:624
  347.6 4.2 %all-to-all-start.6 = ((bf16[4,48,1920]{2,1,0:T(8,128)(2,1)}), bf16[4,48,1920]{2,1,0:T(8,128)(2,1)}, u32[]{:S(2)}, u32[]{:S(2)}) async-start(bf16[4,48,1920]{2,1,0:T(8,128)(2,1)} %add_convert_fusion), calls=%async_computation.6 | async-start | bytes 1474560 | tf_op jit(solution)/shard_map/all_to_all | solution.py:624
  357.4 3.5 collective-permute-done.40
  372.4 6.9 %shard_map.400 = f32[512,768]{1,0:T(8,128)} custom-call(f32[512,768]{1,0:T(8,128)} %copy-done.7, bf16[512,768]{1,0:T(8,128)(2,1)S(1)} %get-tuple-element.101.dq.refs_1_, bf16[512,768]{1,0:T(8,128)(2,1)S(1)} %get-tuple-element.102.dk.refs_2_, bf16[512,768]{1,0:T(8,128)(2,1)S(1)} %copy-done.4, bf16[768,768]{1,0:T(8,128)(2,1)S(1)} %bitcast.75, ...), custom_call_target="tpu_custom_call" | custom-call | flops 1811939328 | bytes 9043968 | tf_op jit(solution)/shard_map/pallas_call | solution.py:40
  (345 shorter events, 159.8 us)
Async XLA Ops:
  40.5 20.3 %collective-permute-start.10 = (bf16[4,48,768]{2,1,0:T(8,128)(2,1)S(1)}, bf16[4,48,768]{2,1,0:T(8,128)(2,1)S(1)}, u32[]{:S(2)}, u32[]{:S(2)}) collective-permute-start(bf16[4,48,768]{2,1,0:T(8,128)(2,1)S(1)} %all-to-all-done.2.refs_0_), channel_id=1, source_target_pairs={{0,16},{1,17},{2,18},{3,19},{4,20},{5,21},{6,22},{7,23},{8,24},{9,... | collective-permute-start | bytes 884744 | tf_op jit(solution)/shard_map/ppermute | solution.py:619
  53.6 22.4 %all-to-all-start.4 = ((bf16[4,192,384]{2,1,0:T(8,128)(2,1)}), bf16[4,192,384]{2,1,0:T(8,128)(2,1)S(1)}, u32[]{:S(2)}, u32[]{:S(2)}) async-start(bf16[4,192,384]{2,1,0:T(8,128)(2,1)} %broadcast_in_dim.24), calls=%async_computation.4 | async-start | bytes 1179648 | tf_op jit(solution)/shard_map/all_to_all | solution.py:624
  67.9 20.6 %collective-permute-start.17 = (bf16[4,48,1536]{2,1,0:T(8,128)(2,1)S(1)}, bf16[4,48,1536]{2,1,0:T(8,128)(2,1)S(1)}, u32[]{:S(2)}, u32[]{:S(2)}) collective-permute-start(bf16[4,48,1536]{2,1,0:T(8,128)(2,1)S(1)} %all-to-all-done.3.refs_0_), channel_id=1, source_target_pairs={{0,16},{1,17},{2,18},{3,19},{4,20},{5,21},{6,22},{7,23},{8,24},{9,... | collective-permute-start | bytes 1769480 | tf_op jit(solution)/shard_map/ppermute | solution.py:619
  70.2 19.9 %collective-permute-start.15 = (bf16[4,48,1536]{2,1,0:T(8,128)(2,1)S(1)}, bf16[4,48,1536]{2,1,0:T(8,128)(2,1)S(1)}, u32[]{:S(2)}, u32[]{:S(2)}) collective-permute-start(bf16[4,48,1536]{2,1,0:T(8,128)(2,1)S(1)} %all-to-all-done.3.refs_0_), channel_id=1, source_target_pairs={{0,1},{1,0},{2,3},{3,2},{4,5},{5,4},{6,7},{7,6},{8,9},{9,8},{10,11... | collective-permute-start | bytes 1769480 | tf_op jit(solution)/shard_map/ppermute | solution.py:619
  76.0 22.3 %collective-permute-start.22 = (bf16[4,192,384]{2,1,0:T(8,128)(2,1)S(1)}, bf16[4,192,384]{2,1,0:T(8,128)(2,1)}, u32[]{:S(2)}, u32[]{:S(2)}) collective-permute-start(bf16[4,192,384]{2,1,0:T(8,128)(2,1)S(1)} %all-to-all-done.4.refs_0_), channel_id=1, source_target_pairs={{0,1},{1,0},{2,3},{3,2},{4,5},{5,4},{6,7},{7,6},{8,9},{9,8},{10,11... | collective-permute-start | bytes 1769480 | tf_op jit(solution)/shard_map/ppermute | solution.py:619
  77.9 23.4 %collective-permute-start.24 = (bf16[4,192,384]{2,1,0:T(8,128)(2,1)S(1)}, bf16[4,192,384]{2,1,0:T(8,128)(2,1)}, u32[]{:S(2)}, u32[]{:S(2)}) collective-permute-start(bf16[4,192,384]{2,1,0:T(8,128)(2,1)S(1)} %all-to-all-done.4.refs_0_), channel_id=1, source_target_pairs={{0,16},{1,17},{2,18},{3,19},{4,20},{5,21},{6,22},{7,23},{8,24},{9,... | collective-permute-start | bytes 1769480 | tf_op jit(solution)/shard_map/ppermute | solution.py:619
  88.5 19.8 %collective-permute-start.5 = (bf16[4,48,1152]{2,1,0:T(8,128)(2,1)S(1)}, bf16[4,48,1152]{2,1,0:T(8,128)(2,1)}, u32[]{:S(2)}, u32[]{:S(2)}) collective-permute-start(bf16[4,48,1152]{2,1,0:T(8,128)(2,1)S(1)} %collective-permute-done.1.refs_2_), channel_id=1, source_target_pairs={{0,16},{1,17},{2,18},{3,19},{4,20},{5,21},{6,22},{7,23},{8,24},{9,... | collective-permute-start | bytes 1327112 | tf_op jit(solution)/shard_map/ppermute | solution.py:619
  90.1 20.6 %collective-permute-start.4 = (bf16[4,48,1152]{2,1,0:T(8,128)(2,1)}, bf16[4,48,1152]{2,1,0:T(8,128)(2,1)S(1)}, u32[]{:S(2)}, u32[]{:S(2)}) collective-permute-start(bf16[4,48,1152]{2,1,0:T(8,128)(2,1)} %collective-permute-done.3.refs_4_), channel_id=1, source_target_pairs={{0,8},{1,9},{2,10},{3,11},{4,12},{5,13},{6,14},{7,15},{8,0},{9,1},... | collective-permute-start | bytes 1327112 | tf_op jit(solution)/shard_map/ppermute | solution.py:619
  98.4 21.4 %collective-permute-start.19 = (bf16[4,48,1536]{2,1,0:T(8,128)(2,1)S(1)}, bf16[4,48,1536]{2,1,0:T(8,128)(2,1)}, u32[]{:S(2)}, u32[]{:S(2)}) collective-permute-start(bf16[4,48,1536]{2,1,0:T(8,128)(2,1)S(1)} %collective-permute-done.17.refs_4_), channel_id=1, source_target_pairs={{0,1},{1,0},{2,3},{3,2},{4,5},{5,4},{6,7},{7,6},{8,9},{9,8},{10,11... | collective-permute-start | bytes 1769480 | tf_op jit(solution)/shard_map/ppermute | solution.py:619
  101.3 21.4 %collective-permute-start.16 = (bf16[4,48,1536]{2,1,0:T(8,128)(2,1)S(1)}, bf16[4,48,1536]{2,1,0:T(8,128)(2,1)}, u32[]{:S(2)}, u32[]{:S(2)}) collective-permute-start(bf16[4,48,1536]{2,1,0:T(8,128)(2,1)S(1)} %collective-permute-done.15.refs_2_), channel_id=1, source_target_pairs={{0,8},{1,9},{2,10},{3,11},{4,12},{5,13},{6,14},{7,15},{8,0},{9,1},... | collective-permute-start | bytes 1769480 | tf_op jit(solution)/shard_map/ppermute | solution.py:619
  119.7 36.5 %collective-permute-start.20 = (bf16[4,48,1536]{2,1,0:T(8,128)(2,1)}, bf16[4,48,1536]{2,1,0:T(8,128)(2,1)}, u32[]{:S(2)}, u32[]{:S(2)}) collective-permute-start(bf16[4,48,1536]{2,1,0:T(8,128)(2,1)} %collective-permute-done.19.refs_6_), channel_id=1, source_target_pairs={{0,8},{1,9},{2,10},{3,11},{4,12},{5,13},{6,14},{7,15},{8,0},{9,1},... | collective-permute-start | bytes 1769480 | tf_op jit(solution)/shard_map/ppermute | solution.py:619
  122.1 51.8 %collective-permute-start.21 = (bf16[4,192,384]{2,1,0:T(8,128)(2,1)S(1)}, bf16[4,192,384]{2,1,0:T(8,128)(2,1)}, u32[]{:S(2)}, u32[]{:S(2)}) collective-permute-start(bf16[4,192,384]{2,1,0:T(8,128)(2,1)S(1)} %all-to-all-done.4.refs_0_), channel_id=1, source_target_pairs={{0,8},{1,9},{2,10},{3,11},{4,12},{5,13},{6,14},{7,15},{8,0},{9,1},... | collective-permute-start | bytes 1769480 | tf_op jit(solution)/shard_map/ppermute | solution.py:619
  122.6 51.3 %collective-permute-start.23 = (bf16[4,192,384]{2,1,0:T(8,128)(2,1)}, bf16[4,192,384]{2,1,0:T(8,128)(2,1)}, u32[]{:S(2)}, u32[]{:S(2)}) collective-permute-start(bf16[4,192,384]{2,1,0:T(8,128)(2,1)} %collective-permute-done.22.refs_2_), channel_id=1, source_target_pairs={{0,8},{1,9},{2,10},{3,11},{4,12},{5,13},{6,14},{7,15},{8,0},{9,1},... | collective-permute-start | bytes 1769480 | tf_op jit(solution)/shard_map/ppermute | solution.py:619
  122.7 51.2 %collective-permute-start.25 = (bf16[4,192,384]{2,1,0:T(8,128)(2,1)}, bf16[4,192,384]{2,1,0:T(8,128)(2,1)}, u32[]{:S(2)}, u32[]{:S(2)}) collective-permute-start(bf16[4,192,384]{2,1,0:T(8,128)(2,1)} %collective-permute-done.24.refs_4_), channel_id=1, source_target_pairs={{0,8},{1,9},{2,10},{3,11},{4,12},{5,13},{6,14},{7,15},{8,0},{9,1},... | collective-permute-start | bytes 1769480 | tf_op jit(solution)/shard_map/ppermute | solution.py:619
  125.2 48.7 %collective-permute-start.27 = (bf16[4,192,384]{2,1,0:T(8,128)(2,1)}, bf16[4,192,384]{2,1,0:T(8,128)(2,1)}, u32[]{:S(2)}, u32[]{:S(2)}) collective-permute-start(bf16[4,192,384]{2,1,0:T(8,128)(2,1)} %collective-permute-done.26.refs_6_), channel_id=1, source_target_pairs={{0,8},{1,9},{2,10},{3,11},{4,12},{5,13},{6,14},{7,15},{8,0},{9,1},... | collective-permute-start | bytes 1769480 | tf_op jit(solution)/shard_map/ppermute | solution.py:619
  232.8 25.6 %collective-permute-start.32 = (bf16[4,48,1152]{2,1,0:T(8,128)(2,1)}, bf16[4,48,1152]{2,1,0:T(8,128)(2,1)}, u32[]{:S(2)}, u32[]{:S(2)}) collective-permute-start(bf16[4,48,1152]{2,1,0:T(8,128)(2,1)} %get-tuple-element.111), channel_id=1, source_target_pairs={{0,1},{1,0},{2,3},{3,2},{4,5},{5,4},{6,7},{7,6},{8,9},{9,8},{10,11... | collective-permute-start | bytes 1327112 | tf_op jit(solution)/shard_map/ppermute | solution.py:619
  239.2 23.3 %collective-permute-start.43 = (bf16[4,48,1920]{2,1,0:T(8,128)(2,1)}, bf16[4,48,1920]{2,1,0:T(8,128)(2,1)S(1)}, u32[]{:S(2)}, u32[]{:S(2)}) collective-permute-start(bf16[4,48,1920]{2,1,0:T(8,128)(2,1)} %get-tuple-element.121), channel_id=1, source_target_pairs={{0,8},{1,9},{2,10},{3,11},{4,12},{5,13},{6,14},{7,15},{8,0},{9,1},... | collective-permute-start | bytes 2211848 | tf_op jit(solution)/shard_map/ppermute | solution.py:619
  240.0 22.9 %collective-permute-start.44 = (bf16[4,48,1920]{2,1,0:T(8,128)(2,1)}, bf16[4,48,1920]{2,1,0:T(8,128)(2,1)}, u32[]{:S(2)}, u32[]{:S(2)}) collective-permute-start(bf16[4,48,1920]{2,1,0:T(8,128)(2,1)} %get-tuple-element.122), channel_id=1, source_target_pairs={{0,8},{1,9},{2,10},{3,11},{4,12},{5,13},{6,14},{7,15},{8,0},{9,1},... | collective-permute-start | bytes 2211848 | tf_op jit(solution)/shard_map/ppermute | solution.py:619
  241.4 27.9 %collective-permute-start.45 = (bf16[4,48,1920]{2,1,0:T(8,128)(2,1)}, bf16[4,48,1920]{2,1,0:T(8,128)(2,1)}, u32[]{:S(2)}, u32[]{:S(2)}) collective-permute-start(bf16[4,48,1920]{2,1,0:T(8,128)(2,1)} %get-tuple-element.123), channel_id=1, source_target_pairs={{0,8},{1,9},{2,10},{3,11},{4,12},{5,13},{6,14},{7,15},{8,0},{9,1},... | collective-permute-start | bytes 2211848 | tf_op jit(solution)/shard_map/ppermute | solution.py:619
  242.2 28.9 %collective-permute-start.46 = (bf16[4,48,1920]{2,1,0:T(8,128)(2,1)}, bf16[4,48,1920]{2,1,0:T(8,128)(2,1)}, u32[]{:S(2)}, u32[]{:S(2)}) collective-permute-start(bf16[4,48,1920]{2,1,0:T(8,128)(2,1)} %get-tuple-element.124), channel_id=1, source_target_pairs={{0,8},{1,9},{2,10},{3,11},{4,12},{5,13},{6,14},{7,15},{8,0},{9,1},... | collective-permute-start | bytes 2211848 | tf_op jit(solution)/shard_map/ppermute | solution.py:619
  243.4 21.0 %all-to-all-start.8 = ((bf16[8,8,768]{2,1,0:T(8,128)(2,1)}), bf16[8,8,768]{2,1,0:T(8,128)(2,1)S(1)}, u32[]{:S(2)}, u32[]{:S(2)}) async-start(bf16[8,8,768]{2,1,0:T(8,128)(2,1)} %broadcast_in_dim.27), calls=%async_computation.8 | async-start | bytes 196608 | tf_op jit(solution)/shard_map/all_to_all | solution.py:721
  258.5 21.6 %collective-permute-start.57 = (bf16[4,192,384]{2,1,0:T(8,128)(2,1)}, bf16[4,192,384]{2,1,0:T(8,128)(2,1)}, u32[]{:S(2)}, u32[]{:S(2)}) collective-permute-start(bf16[4,192,384]{2,1,0:T(8,128)(2,1)} %get-tuple-element.137), channel_id=1, source_target_pairs={{0,1},{1,0},{2,3},{3,2},{4,5},{5,4},{6,7},{7,6},{8,9},{9,8},{10,11... | collective-permute-start | bytes 1769480 | tf_op jit(solution)/shard_map/ppermute | solution.py:619
  262.5 22.0 %collective-permute-start.34 = (bf16[4,48,1152]{2,1,0:T(8,128)(2,1)}, bf16[4,48,1152]{2,1,0:T(8,128)(2,1)}, u32[]{:S(2)}, u32[]{:S(2)}) collective-permute-start(bf16[4,48,1152]{2,1,0:T(8,128)(2,1)} %get-tuple-element.112), channel_id=1, source_target_pairs={{0,1},{1,0},{2,3},{3,2},{4,5},{5,4},{6,7},{7,6},{8,9},{9,8},{10,11... | collective-permute-start | bytes 1327112 | tf_op jit(solution)/shard_map/ppermute | solution.py:619
  262.9 23.1 %collective-permute-start.33 = (bf16[4,48,1152]{2,1,0:T(8,128)(2,1)}, bf16[4,48,1152]{2,1,0:T(8,128)(2,1)}, u32[]{:S(2)}, u32[]{:S(2)}) collective-permute-start(bf16[4,48,1152]{2,1,0:T(8,128)(2,1)} %add_convert_fusion.5), channel_id=1, source_target_pairs={{0,16},{1,17},{2,18},{3,19},{4,20},{5,21},{6,22},{7,23},{8,24},{9,... | collective-permute-start | bytes 1327112 | tf_op jit(solution)/shard_map/ppermute | solution.py:619
  265.2 23.0 %all-to-all-start.9 = ((bf16[4,64,768]{2,1,0:T(8,128)(2,1)}), bf16[4,64,768]{2,1,0:T(8,128)(2,1)}, u32[]{:S(2)}, u32[]{:S(2)}) async-start(bf16[4,64,768]{2,1,0:T(8,128)(2,1)} %broadcast_in_dim.58), calls=%async_computation.9 | async-start | bytes 786432 | tf_op jit(solution)/shard_map/all_to_all | solution.py:721
  269.3 31.0 %collective-permute-start.59 = (bf16[4,192,384]{2,1,0:T(8,128)(2,1)}, bf16[4,192,384]{2,1,0:T(8,128)(2,1)}, u32[]{:S(2)}, u32[]{:S(2)}) collective-permute-start(bf16[4,192,384]{2,1,0:T(8,128)(2,1)} %copy-done.61), channel_id=1, source_target_pairs={{0,1},{1,0},{2,3},{3,2},{4,5},{5,4},{6,7},{7,6},{8,9},{9,8},{10,11... | collective-permute-start | bytes 1769480 | tf_op jit(solution)/shard_map/ppermute | solution.py:619
  280.0 54.1 %collective-permute-start.47 = (bf16[4,48,1920]{2,1,0:T(8,128)(2,1)}, bf16[4,48,1920]{2,1,0:T(8,128)(2,1)}, u32[]{:S(2)}, u32[]{:S(2)}) collective-permute-start(bf16[4,48,1920]{2,1,0:T(8,128)(2,1)} %get-tuple-element.126), channel_id=1, source_target_pairs={{0,16},{1,17},{2,18},{3,19},{4,20},{5,21},{6,22},{7,23},{8,24},{9,... | collective-permute-start | bytes 2211848 | tf_op jit(solution)/shard_map/ppermute | solution.py:619
  284.5 40.8 %collective-permute-start.58 = (bf16[4,192,384]{2,1,0:T(8,128)(2,1)}, bf16[4,192,384]{2,1,0:T(8,128)(2,1)}, u32[]{:S(2)}, u32[]{:S(2)}) collective-permute-start(bf16[4,192,384]{2,1,0:T(8,128)(2,1)} %add_convert_fusion.3), channel_id=1, source_target_pairs={{0,16},{1,17},{2,18},{3,19},{4,20},{5,21},{6,22},{7,23},{8,24},{9,... | collective-permute-start | bytes 1769480 | tf_op jit(solution)/shard_map/ppermute | solution.py:619
  288.2 39.5 %all-to-all-start.5 = ((bf16[4,48,1152]{2,1,0:T(8,128)(2,1)}), bf16[4,48,1152]{2,1,0:T(8,128)(2,1)}, u32[]{:S(2)}, u32[]{:S(2)}) async-start(bf16[4,48,1152]{2,1,0:T(8,128)(2,1)} %add_convert_fusion.4), calls=%async_computation.5 | async-start | bytes 884736 | tf_op jit(solution)/shard_map/all_to_all | solution.py:624
  300.0 34.1 %collective-permute-start.49 = (bf16[4,48,1920]{2,1,0:T(8,128)(2,1)}, bf16[4,48,1920]{2,1,0:T(8,128)(2,1)S(1)}, u32[]{:S(2)}, u32[]{:S(2)}) collective-permute-start(bf16[4,48,1920]{2,1,0:T(8,128)(2,1)} %add_convert_fusion.1), channel_id=1, source_target_pairs={{0,1},{1,0},{2,3},{3,2},{4,5},{5,4},{6,7},{7,6},{8,9},{9,8},{10,11... | collective-permute-start | bytes 2211848 | tf_op jit(solution)/shard_map/ppermute | solution.py:619
  327.7 19.9 %all-to-all-start.7 = ((bf16[4,192,384]{2,1,0:T(8,128)(2,1)}), bf16[4,192,384]{2,1,0:T(8,128)(2,1)}, u32[]{:S(2)}, u32[]{:S(2)}) async-start(bf16[4,192,384]{2,1,0:T(8,128)(2,1)} %add_convert_fusion.2), calls=%async_computation.7 | async-start | bytes 1179648 | tf_op jit(solution)/shard_map/all_to_all | solution.py:624
  347.6 39.7 %all-to-all-start.6 = ((bf16[4,48,1920]{2,1,0:T(8,128)(2,1)}), bf16[4,48,1920]{2,1,0:T(8,128)(2,1)}, u32[]{:S(2)}, u32[]{:S(2)}) async-start(bf16[4,48,1920]{2,1,0:T(8,128)(2,1)} %add_convert_fusion), calls=%async_computation.6 | async-start | bytes 1474560 | tf_op jit(solution)/shard_map/all_to_all | solution.py:624
  (117 other events, 1396.5 us)

commit v2 on v1

--- a/solution.py
+++ b/solution.py
@@ -1,4 +1,5 @@
 import functools
+import math
 
 import jax
 import jax.numpy as jnp
@@ -33,12 +34,17 @@
 
 def full(shape):
     zeros = (0,) * len(shape)
-    return pl.BlockSpec(shape, lambda *_: zeros)
-
-
-def call(kernel, outs, in_specs, out_specs, args, *, grid=(1,), scratch=(), prefetch=0, flops=0, moved=0, trans=0, vmem=48):
+    return pl.BlockSpec(shape, lambda *_: zeros, pipeline_mode=pl.Buffered(1))
+
+
+def after(a, *others):
+    return lax.optimization_barrier((a, *others))[0]
+
+
+def call(kernel, outs, in_specs, out_specs, args, *, grid=(1,), scratch=(), prefetch=0, flops=0, moved=0, trans=0, vmem=20, name=None):
     return pl.pallas_call(
         kernel,
+        name=name,
         out_shape=outs,
         grid_spec=pltpu.PrefetchScalarGridSpec(
             num_scalar_prefetch=prefetch,
@@ -50,7 +56,7 @@
         compiler_params=pltpu.CompilerParams(
             dimension_semantics=("arbitrary",) * len(grid), vmem_limit_bytes=vmem * MIB
         ),
-        cost_estimate=pl.CostEstimate(flops=flops, bytes_accessed=moved, transcendentals=trans),
+        cost_estimate=pl.CostEstimate(flops=flops // 16, bytes_accessed=moved // 16, transcendentals=trans // 16),
     )(*args)
 
 
@@ -114,6 +120,7 @@
         flops=2 * seq * width * (3 * width + 2 * seq),
         moved=8 * seq * width + 6 * width * width,
         trans=seq * seq * width // HEAD_DIM,
+        name="attention",
     )
 
 
@@ -146,6 +153,7 @@
         grid=(seq // blk,),
         flops=2 * seq * width * width,
         moved=2 * width * width + 10 * seq * width,
+        name="attended",
     )
 
 
@@ -197,6 +205,7 @@
         flops=2 * seq * width * ff,
         moved=2 * width * ff + 4 * seq * ff,
         trans=2 * seq * ff,
+        name="inner",
     )
 
 
@@ -308,21 +317,43 @@
         prefetch=2,
         flops=2 * seq * width * ff,
         moved=2 * width * ff + 2 * seq * ff + 14 * seq * width,
-    )
-
-
-def inner_back_kernel(bg, w_out, w_in, slope, sg, n1, r1, table, ig_o, ib_o, res_o, ag_o, sums_o, acc):
+        name="outer",
+    )
+
+
+def inner_grad_kernel(bg, w_out, slope, ig_o):
+    ig_o[...] = (dot_nt(bg[...], w_out[...]) * slope[...].astype(F32)).astype(LOW)
+
+
+def inner_grads(bg, w_out, slope):
+    seq, width = bg.shape
+    ff = slope.shape[1]
+    blk = 512
+    cols = pl.BlockSpec((seq, blk), lambda i: (0, i))
+    return call(
+        inner_grad_kernel,
+        shape(seq, ff),
+        [full((seq, width)), pl.BlockSpec((blk, width), lambda i: (i, 0)), cols],
+        cols,
+        (bg, w_out, slope),
+        grid=(ff // blk,),
+        flops=2 * seq * width * ff,
+        moved=2 * width * ff + 4 * seq * ff,
+        name="inner_grads",
+    )
+
+
+def inner_back_kernel(ig, w_in, sg, n1, r1, table, res_o, ag_o, sums_o, acc, ib):
     step = pl.program_id(0)
     seq, width = n1.shape
-    ig = (dot_nt(bg[...], w_out[...]) * slope[...].astype(F32)).astype(LOW)
-    ig_o[...] = ig
-    ib_o[...] = jnp.sum(ig.astype(F32), axis=0, keepdims=True)
+    blk = ig.shape[1]
+    ib[:, pl.ds(pl.multiple_of(step * blk, blk), blk)] = jnp.sum(ig[...].astype(F32), axis=0, keepdims=True)
 
     @pl.when(step == 0)
     def _():
         acc[...] = jnp.zeros_like(acc)
 
-    acc[...] += dot_nt(ig, w_in[...])
+    acc[...] += dot_nt(ig[...], w_in[...])
 
     @pl.when(step == pl.num_programs(0) - 1)
     def _():
@@ -349,39 +380,33 @@
         sums_o[0:1, :] = gain_sum
         sums_o[1:2, :] = shift_sum
         sums_o[2:3, :] = bias_sum
-
-
-def inner_back(bg, w_out, w_in, slope, sg, n1, r1, table):
+        for at in range(ib.shape[1] // width):
+            sums_o[3 + at : 4 + at, :] = ib[:, at * width : (at + 1) * width]
+
+
+def inner_back(ig, w_in, sg, n1, r1, table):
     seq, width = n1.shape
-    ff = slope.shape[1]
+    ff = ig.shape[1]
     blk = 512
     whole = full((seq, width))
-    cols = pl.BlockSpec((seq, blk), lambda i: (0, i))
     return call(
         inner_back_kernel,
-        (
-            shape(seq, ff),
-            shape(1, ff, dtype=F32),
-            shape(seq, width, dtype=F32),
-            shape(seq, width),
-            shape(8, width, dtype=F32),
-        ),
+        (shape(seq, width, dtype=F32), shape(seq, width), shape(8, width, dtype=F32)),
         [
-            whole,
-            pl.BlockSpec((blk, width), lambda i: (i, 0)),
+            pl.BlockSpec((seq, blk), lambda i: (0, i)),
             pl.BlockSpec((width, blk), lambda i: (0, i)),
-            cols,
             whole,
             whole,
             full((seq, 1)),
             full((TABLE, width)),
         ],
-        (cols, pl.BlockSpec((1, blk), lambda i: (0, i)), whole, whole, full((8, width))),
-        (bg, w_out, w_in, slope, sg, n1, r1, table),
+        (whole, whole, full((8, width))),
+        (ig, w_in, sg, n1, r1, table),
         grid=(ff // blk,),
-        scratch=[pltpu.VMEM((seq, width), F32)],
-        flops=4 * seq * width * ff,
-        moved=4 * width * ff + 4 * seq * ff + 16 * seq * width,
+        scratch=[pltpu.VMEM((seq, width), F32), pltpu.VMEM((1, ff), F32)],
+        flops=2 * seq * width * ff,
+        moved=2 * width * ff + 2 * seq * ff + 16 * seq * width,
+        name="inner_back",
     )
 
 
@@ -425,31 +450,33 @@
         sums_o[1:2, cols] = jnp.sum(dv.astype(F32), axis=0, keepdims=True)
 
 
-def attention_back(q, k, v, lse, ag, wo, segments):
+def attention_back(q, k, v, lse, ag, wo, segments, begin, count):
     seq, width = ag.shape
     blk = 256
-    steps = width // blk
-    cols = pl.BlockSpec((seq, blk), lambda i: (0, i))
+    begin, steps = begin // blk, count // blk
+    cols = pl.BlockSpec((seq, blk), lambda i: (0, i + begin))
+    out = pl.BlockSpec((seq, blk), lambda i: (0, i))
     return call(
         attention_back_kernel,
-        (shape(seq, width),) * 3 + (shape(8, width, dtype=F32),),
+        (shape(seq, count),) * 3 + (shape(8, count, dtype=F32),),
         [
             cols,
             cols,
             cols,
-            pl.BlockSpec((1, 8, seq), lambda i: (i, 0, 0)),
+            pl.BlockSpec((1, 8, seq), lambda i: (i + begin, 0, 0)),
             full((seq, width)),
-            pl.BlockSpec((blk, width), lambda i: (i, 0)),
+            pl.BlockSpec((blk, width), lambda i: (i + begin, 0)),
             full((1, seq)),
             full((seq, 1)),
         ],
-        (cols,) * 3 + (pl.BlockSpec((8, blk), lambda i: (0, i)),),
+        (out,) * 3 + (pl.BlockSpec((8, blk), lambda i: (0, i)),),
         (q, k, v, lse, ag, wo, segments.reshape(1, seq), segments.reshape(seq, 1)),
         grid=(steps,),
         scratch=[pltpu.VMEM((seq, seq), F32)],
-        flops=2 * seq * width * (width + 5 * seq),
-        moved=16 * seq * width + 2 * width * width,
-        trans=seq * seq * width // HEAD_DIM,
+        flops=2 * seq * count * (width + 5 * seq),
+        moved=16 * seq * count + 2 * width * count,
+        trans=seq * seq * count // HEAD_DIM,
+        name="attention_back",
     )
 
 
@@ -471,65 +498,111 @@
         grid=(seq // blk,),
         flops=6 * seq * width * width,
         moved=14 * seq * width + 6 * width * width,
-    )
-
-
-def grads(where, lefts, which, rights, other, add=None):
+        name="tokens_back",
+    )
+
+
+def grads(name, where, lefts, which, rights, add=None, form=None):
     seq = lefts[0].shape[0]
     parts = lefts[0].shape[1] // 16
     widths = tuple((w, r.shape[1] // 2) for w, r in zip(which, rights))
     total = sum(w for _, w in widths)
-    half = (lambda i, where: (0, 1 - where[3])) if other else (lambda i, where: (0, where[3]))
-    right_specs = [pl.BlockSpec((seq, w), half) for _, w in widths]
-    piece = (4, parts, total)
-    specs = [full(a.shape) for a in lefts] + right_specs
+    half = (lambda i, where: (0, 1 - where[3])) if add is None else (lambda i, where: (0, where[3]))
+    specs = [full(a.shape) for a in lefts]
+    specs += [pl.BlockSpec((seq, w), half, pipeline_mode=pl.Buffered(1)) for _, w in widths]
     args = [where, *lefts, *rights]
+    if add is None:
+        outs = ((4, 4, parts, total),)
+    elif form == "z":
+        outs = ((2, 4, parts, total),) * 2
+    else:
+        outs = ((4, parts, total),) * 4
     if add is not None:
-        specs += [full(piece)] * 4
-        args += list(add)
-
-    def kernel(where_ref, *refs):
-        n, m = len(lefts), len(rights)
-        left_refs, right_refs = refs[:n], refs[n : n + m]
-        rest = refs[n + m :]
-        grad_body(where_ref, left_refs, right_refs, rest, widths, parts, add is not None)
-
-    return call(
+        specs.append(full(add.shape))
+        args.append(add)
+
+    def kernel(where, *refs):
+        left_refs, refs = refs[: len(lefts)], refs[len(lefts) :]
+        right_refs, refs = refs[: len(rights)], refs[len(rights) :]
+        add_ref = None if add is None else refs[0]
+        out_refs, turned = refs[: len(outs)] if add is None else refs[1 : 1 + len(outs)], refs[-len(lefts) :]
+        x, y, z0 = where[0], where[1], where[2]
+        for left, store in zip(left_refs, turned):
+            for start in range(0, left.shape[1], 256):
+                store[start : start + 256, :] = left[:, start : start + 256].T
+        for place in range(4):
+            hh = jnp.bitwise_xor(x, place // 2)
+            yy = jnp.bitwise_xor(y, place % 2)
+            column = 0
+            for (at, width), right in zip(widths, right_refs):
+                rows = []
+                for dz in range(4):
+                    shard = jnp.bitwise_xor(z0, dz) * 2 + yy
+                    rows.append(turned[at][pl.ds(pl.multiple_of((shard * 2 + hh) * parts, 16), parts), :])
+                got = dot(jnp.concatenate(rows, axis=0), right[...]).reshape(4, parts, width)
+                cols = slice(column, column + width)
+                if add is not None:
+                    got = got + add_ref[place, :, :, cols].astype(F32)
+                got = got.astype(LOW)
+                if add is None:
+                    out_refs[0][place, :, :, cols] = got
+                elif form == "z":
+                    for dz in range(4):
+                        out_refs[dz % 2][dz // 2, place, :, cols] = got[dz]
+                else:
+                    out_refs[place][:, :, cols] = got
+                column += width
+
+    got = call(
         kernel,
-        (shape(*piece),) * 4,
+        tuple(shape(*o) for o in outs),
         specs,
-        (full(piece),) * 4,
+        tuple(full(o) for o in outs),
         args,
         scratch=[pltpu.VMEM((a.shape[1], seq), LOW) for a in lefts],
         prefetch=1,
         flops=2 * seq * 16 * parts * total,
         moved=2 * 16 * parts * total + 2 * seq * 16 * parts,
-    )
-
-
-def grad_body(where, lefts, rights, rest, widths, parts, with_add):
-    adds = rest[:4] if with_add else None
-    outs = rest[4:8] if with_add else rest[:4]
-    turned = rest[8:] if with_add else rest[4:]
-    x, y = where[0], where[1]
-    for left, store in zip(lefts, turned):
-        for start in range(0, left.shape[1], 256):
-            store[start : start + 256, :] = left[:, start : start + 256].T
-    for place in range(4):
-        hh = jnp.bitwise_xor(x, place // 2)
-        yy = jnp.bitwise_xor(y, place % 2)
-        column = 0
-        for (which, width), right in zip(widths, rights):
-            rows = [
-                turned[which][pl.ds(pl.multiple_of(((z * 2 + yy) * 2 + hh) * parts, 16), parts), :]
-                for z in range(4)
-            ]
-            got = dot(jnp.concatenate(rows, axis=0), right[...]).reshape(4, parts, width)
-            cols = slice(column, column + width)
-            if with_add:
-                got = got + adds[place][:, :, cols].astype(F32)
-            outs[place][:, :, cols] = got.astype(LOW)
-            column += width
+        name=name,
+    )
+    return got[0] if add is None else got
+
+
+def pack_kernel(where, wq, wk, wv, wo, wi, wf, wp, small, own_a, own_b, own_c):
+    for out, weights in ((own_a, (wq, wk, wv)), (own_b, (wo, wi))):
+        left = 0
+        for ref in weights:
+            out[: ref.shape[0], left : left + ref.shape[1]] = ref[...]
+            left += ref.shape[1]
+    at = wq.shape[0]
+    own_a[at:, :] = jnp.zeros((8, own_a.shape[1]), LOW)
+    for top in range(0, small.shape[0], 8):
+        own_a[at:, top * 16 : top * 16 + small.shape[1]] = small[top : top + 8, :]
+    rows = wf.shape[0]
+    own_c[:rows, :] = wf[...]
+    own_c[rows:, :] = wp[...]
+
+
+def pack(where, wq, wk, wv, wo, wi, wf, wp, small):
+    rows, width = wq.shape
+    deep = wf.shape[0] // 2
+    ff = wi.shape[1]
+    outs = (shape(rows // 2 + 8, 3 * width // 2), shape(rows // 2, (width + ff) // 2), shape(deep + rows // 2, width // 2))
+    weights = (wq, wk, wv, wo, wi, wf, wp)
+    quarters = [
+        pl.BlockSpec((w.shape[0] // 2, w.shape[1] // 2), lambda i, where: (where[0], where[3])) for w in weights
+    ]
+    return call(
+        pack_kernel,
+        outs,
+        quarters + [full(small.shape)],
+        tuple(full(o.shape) for o in outs),
+        (where, *(pltpu.with_memory_space_constraint(w, pltpu.HBM) for w in weights), small),
+        prefetch=1,
+        moved=4 * sum(math.prod(o.shape) for o in outs),
+        vmem=8,
+        name="pack",
+    )
 
 
 def weights_kernel(spans, where, *refs):
@@ -539,34 +612,33 @@
         hh = jnp.bitwise_xor(where[0], place // 4)
         yy = jnp.bitwise_xor(where[1], place // 2 % 2)
         cc = jnp.bitwise_xor(where[3], place % 2)
-        for (start, width), out in zip(spans, outs):
-            to = out.at[:, yy, hh, :, pl.ds(pl.multiple_of(cc * width, 128), width)]
-            copies.append(pltpu.make_async_copy(pieces[place].at[:, :, start : start + width], to, sem.at[len(copies)]))
-    for copy in copies:
-        copy.start()
-    for copy in copies:
-        copy.wait()
-
-
-def place_weights(where, pieces, widths):
-    parts = pieces[0].shape[1]
-    spans, start = [], 0
-    for width in widths:
-        spans.append((start, width // 2))
-        start += width // 2
+        for dz in range(4):
+            zz = jnp.bitwise_xor(where[2], dz)
+            for (top, rows, left, width), out in zip(spans, outs):
+                to = out.at[zz, yy, hh, :, pl.ds(pl.multiple_of(cc * width, 128), width)]
+                come = pieces[place].at[dz, top : top + rows, left : left + width]
+                copies.append(pltpu.make_async_copy(come, to, sem.at[len(copies)]))
+    for one in copies:
+        one.start()
+    for one in copies:
+        one.wait()
+
+
+def place_weights(where, pieces, spans):
     anywhere = pl.BlockSpec(memory_space=pl.ANY)
     outs = call(
         functools.partial(weights_kernel, tuple(spans)),
-        tuple(shape(4, 2, 2, parts, w) for w in widths),
+        tuple(shape(4, 2, 2, rows, 2 * width) for _, rows, _, width in spans),
         [anywhere] * 8,
-        (anywhere,) * len(widths),
-        (where, *pieces),
-        scratch=[pltpu.SemaphoreType.DMA((8 * len(widths),))],
+        (anywhere,) * len(spans),
+        (where, *(pltpu.with_memory_space_constraint(p, pltpu.VMEM) for p in pieces)),
+        scratch=[pltpu.SemaphoreType.DMA((32 * len(spans),))],
         prefetch=1,
-        moved=4 * 16 * parts * sum(widths),
+        moved=4 * 8 * pieces[0].size,
         vmem=4,
-    )
-    return [o.reshape(16 * parts, w) for o, w in zip(outs, widths)]
+        name="place_weights",
+    )
+    return [o.reshape(16 * rows, 2 * width) for o, (_, rows, _, width) in zip(outs, spans)]
 
 
 def shards_kernel(spans, where, *refs):
@@ -596,7 +668,8 @@
         (where, *pieces),
         prefetch=1,
         moved=12 * parts * sum(widths),
-        vmem=16,
+        vmem=12,
+        name="place_shards",
     )
     return [o.reshape(2 * parts, w) for o, w in zip(outs, widths)]
 
@@ -609,54 +682,38 @@
 CORE_SWAP = [(device(*a), device(a[0], 1 - a[1], a[2], a[3])) for a in ALL]
 X_SWAP = [(device(*a), device(1 - a[0], a[1], a[2], a[3])) for a in ALL]
 Y_SWAP = [(device(*a), device(a[0], a[1], a[2], 1 - a[3])) for a in ALL]
-Z_SWAPS = [[(device(*a), device(a[0], a[1], a[2] ^ d, a[3])) for a in ALL] for d in (1, 2)]
-Z_GROUPS = [
-    [device(x, core, z, y) for z in range(4)] for x in range(2) for core in range(2) for y in range(2)
-]
+Z_SWAPS = [[(device(*a), device(a[0], a[1], a[2] ^ d, a[3])) for a in ALL] for d in range(4)]
+X_CORE_SWAP = [(device(*a), device(1 - a[0], 1 - a[1], a[2], a[3])) for a in ALL]
+XY_SWAP = [(device(*a), device(1 - a[0], a[1], a[2], 1 - a[3])) for a in ALL]
 
 
 def swap(a, pairs):
     return lax.ppermute(a, MESH_AXES, pairs)
 
 
-def z_exchange(a):
-    four, rows, columns = a.shape
-    got = lax.all_to_all(
-        a.reshape(four * rows, columns), MESH_AXES, 0, 0, axis_index_groups=Z_GROUPS, tiled=True
-    )
-    return got.reshape(a.shape)
-
-
-def gather_weights(place, where, shards, over_y_last):
-    x, core = place
-    cut = []
-    for shard in shards:
-        rows, width = shard.shape
-        cut.append(lax.dynamic_slice(shard, (x * (rows // 2), core * (width // 2)), (rows // 2, width // 2)))
-    own = jnp.concatenate(cut, axis=1) if len(cut) > 1 else cut[0]
-    near = z_exchange(jnp.broadcast_to(own[None], (4, *own.shape)))
-    by_x = swap(near, X_SWAP)
-    by_y = swap(near, Y_SWAP)
-    both = swap(by_x, Y_SWAP) if over_y_last else swap(by_y, X_SWAP)
-    pieces = []
-    for piece in (near, by_y, by_x, both):
-        pieces += [piece, swap(piece, CORE_SWAP)]
-    return place_weights(where, pieces, [s.shape[1] for s in shards])
-
-
-def reduce_shards(where, same, by_y, by_x, both, over_y_first, widths):
-    if over_y_first:
-        got = swap(both, Y_SWAP)
-        by_x = (by_x.astype(F32) + got.astype(F32)).astype(LOW)
-    else:
-        got = swap(both, X_SWAP)
-        by_y = (by_y.astype(F32) + got.astype(F32)).astype(LOW)
-    from_x, from_y = swap(by_x, X_SWAP), swap(by_y, Y_SWAP)
-    total = (same.astype(F32) + from_x.astype(F32) + from_y.astype(F32)).astype(LOW)
-    own = jnp.sum(z_exchange(total).astype(F32), axis=0).astype(LOW)
-    across = swap(own, X_SWAP)
-    pieces = (own, swap(own, CORE_SWAP), across, swap(across, CORE_SWAP))
-    return place_shards(where, pieces, widths)
+def wide(*arrays):
+    return functools.reduce(jnp.add, [a.astype(F32) for a in arrays])
+
+
+def along_z(own):
+    return [swap(own, Z_SWAPS[d]) for d in (1, 2, 3)]
+
+
+def to_core(arrays):
+    return [swap(a, CORE_SWAP) for a in arrays]
+
+
+def together(*groups):
+    leaves, tree = jax.tree.flatten(groups)
+    return jax.tree.unflatten(tree, lax.optimization_barrier(tuple(leaves)))
+
+
+def low(a):
+    return a.astype(LOW)
+
+
+def sums_by_z(parts):
+    return [wide(*(p[d] for p in parts)) for d in range(4)]
 
 
 def on_device(
@@ -714,25 +771,76 @@
         ]
     )
 
-    def everywhere(a, axis, count):
-        if not by_links:
-            return lax.all_gather(a, axis)
-        rows, columns = a.shape
-        got = lax.all_to_all(
-            jnp.broadcast_to(a[None], (count, rows, columns)).reshape(count * rows, columns), axis, 0, 0, tiled=True
+    def tables(got):
+        table = jnp.transpose(got, (1, 0, 2)).reshape(TABLE, width)
+        return table, got[:, INNER_B:CLASS_W, :].reshape(1, ff)
+
+    bias3 = class_bias.astype(F32)
+    if by_links:
+        own_a, own_b, own_c = pack(
+            where,
+            query_weight,
+            key_weight,
+            value_weight,
+            output_weight,
+            inner_weight,
+            outer_weight,
+            pooler_weight,
+            small,
         )
-        return got.reshape(count, rows, columns)
-
-    got = everywhere(small, "fsdp", shards).astype(F32)
-    table = jnp.transpose(got, (1, 0, 2)).reshape(TABLE, width)
-    inner_row = got[:, INNER_B:CLASS_W, :].reshape(1, ff)
-
-    if by_links:
-        place = (where[0], where[3])
-        wq, wk, wv = gather_weights(place, where, [query_weight, key_weight, value_weight], False)
-        wo, wp = gather_weights(place, where, [output_weight, pooler_weight], False)
-        (wi,) = gather_weights(place, where, [inner_weight], True)
-        (wf,) = gather_weights(place, where, [outer_weight], False)
+        parts, deep = local // 2, outer_weight.shape[0] // 2
+        spans_a = [(0, parts, at * (width // 2), width // 2) for at in range(3)]
+        spans_b = [(0, parts, 0, width // 2), (0, parts, width // 2, ff // 2)]
+        spans_c = [(0, deep, 0, width // 2), (deep, parts, 0, width // 2)]
+
+        def mixed(near, other):
+            return [a for pair in zip(near, other) for a in pair]
+
+        z_a = along_z(own_a)
+        (z_a, own_a, own_b, own_c) = together(z_a, own_a, own_b, own_c)
+        z_b = along_z(own_b)
+        far_a = jnp.stack([own_a, *z_a])
+        x_a, y_a = swap(far_a, X_SWAP), swap(far_a, Y_SWAP)
+        (far_a, x_a, y_a, z_b, own_b, own_c) = together(far_a, x_a, y_a, z_b, own_b, own_c)
+        z_c = along_z(own_c)
+        far_b = jnp.stack([own_b, *z_b])
+        xy_a = swap(x_a, Y_SWAP)
+        x_b = swap(far_b, X_SWAP)
+        (core_a,) = to_core([jnp.concatenate([far_a, y_a, x_a])])
+        order = [((where[2] ^ d) * 2 + (where[1] ^ e)) for e in range(2) for d in range(4)]
+        spread = (jnp.stack(order)[None, :] == jnp.arange(shards)[:, None]).astype(LOW)
+        small = jnp.concatenate([far_a[:, parts:, :256], y_a[:, parts:, :256]])
+        small = jnp.concatenate([small[:, :, :local], small[:, :, 128 : 128 + local]], axis=1)
+        table, inner_row = tables(jnp.einsum("sp,pji->sji", spread, small, preferred_element_type=F32))
+        (far_a, y_a, x_a, xy_a, far_b, x_b, z_c, core_a, own_c, table, inner_row) = together(
+            far_a, y_a, x_a, xy_a, far_b, x_b, z_c, core_a, own_c, table, inner_row
+        )
+        y_b = swap(far_b, Y_SWAP)
+        far_c = jnp.stack([own_c, *z_c])
+        x_c = swap(far_c, X_SWAP)
+        core_a = [core_a[:4], core_a[4:8], core_a[8:]] + to_core([xy_a])
+        wq, wk, wv = place_weights(where, mixed((far_a, y_a, x_a, xy_a), core_a), spans_a)
+        q, k, v, context, lse = attention(tokens, wq, wk, wv, table, segment_ids)
+        (q, k, v, context, lse, far_b, x_b, y_b, far_c, x_c) = together(
+            q, k, v, context, lse, far_b, x_b, y_b, far_c, x_c
+        )
+        xy_b = swap(y_b, X_SWAP)
+        y_c = swap(far_c, Y_SWAP)
+        core_b = to_core([far_b, y_b, x_b])
+        (far_b, y_b, x_b, xy_b, core_b, far_c, x_c, y_c) = together(
+            far_b, y_b, x_b, xy_b, core_b, far_c, x_c, y_c
+        )
+        xy_c = swap(x_c, Y_SWAP)
+        core_b += to_core([xy_b])
+        core_c = to_core([far_c, y_c, x_c])
+        wo, wi = place_weights(where, mixed((far_b, y_b, x_b, xy_b), core_b), spans_b)
+        n1, r1, first_low = attended(context, wo, tokens, table)
+        activated, slope = inner(first_low, wi, inner_row)
+        (far_c, y_c, x_c, xy_c, core_c, activated, slope) = together(
+            far_c, y_c, x_c, xy_c, core_c, activated, slope
+        )
+        core_c += to_core([xy_c])
+        wf, wp = place_weights(where, mixed((far_c, y_c, x_c, xy_c), core_c), spans_c)
     else:
         wq, wk, wv, wo, wp, wi, wf = (
             lax.all_gather(w, "fsdp", axis=0, tiled=True)
@@ -746,57 +854,119 @@
                 outer_weight,
             )
         )
-
-    q, k, v, context, lse = attention(tokens, wq, wk, wv, table, segment_ids)
-    n1, r1, first_low = attended(context, wo, tokens, table)
-    activated, slope = inner(first_low, wi, inner_row)
+        table, inner_row = tables(lax.all_gather(small, "fsdp").astype(F32))
+        q, k, v, context, lse = attention(tokens, wq, wk, wv, table, segment_ids)
+        n1, r1, first_low = attended(context, wo, tokens, table)
+        activated, slope = inner(first_low, wi, inner_row)
+
     hidden, second_grad, branch_grad, sums2, head, loss = outer(
-        activated, wf, n1, table, out_grad, wp, labels, class_bias.astype(F32)
-    )
+        activated, wf, n1, table, out_grad, wp, labels, bias3
+    )
+    def attention_step(attended_grad, begin, count):
+        return attention_back(q, k, v, lse, attended_grad, wo, segment_ids, begin, count)
+
+    cut = 512
     if by_links:
-        other = grads(where, [activated], [0], [branch_grad], True)
-        other = [swap(a, CORE_SWAP) for a in other]
-    inner_grad, inner_sums, residual_grad, attended_grad, sums1 = inner_back(
-        branch_grad, wf, wi, slope, second_grad, n1, r1, table
-    )
-    if by_links:
-        mine = grads(where, [activated], [0], [branch_grad], False, other)
-        (outer_grad,) = reduce_shards(where, *mine, True, [width])
+
+        def doubled(both, pairs):
+            come = swap(both, pairs)
+            return jnp.concatenate([both[:3] + come[:3], both[3:], come[3:]])
+
+        def plane(parts):
+            same, y, x, xy = parts
+            return [same, swap(x, X_SWAP), swap(y, Y_SWAP), swap(xy, XY_SWAP)]
+
+        other = grads("outer_grad_a", where, [activated], [0], [branch_grad])
+        (other, branch_grad) = together(other, branch_grad)
+        other = swap(other, CORE_SWAP)
+        inner_grad = inner_grads(branch_grad, wf, slope)
+        (other, inner_grad) = together(other, inner_grad)
+        mine = grads("outer_grad_b", where, [activated], [0], [branch_grad], other, "place")
+        (mine, inner_grad) = together(mine, inner_grad)
+        same_f, y_f, x_f, xy_f = mine
+        from_x, from_y = swap(x_f[:2], X_SWAP), swap(y_f[:2], Y_SWAP)
+        residual_grad, attended_grad, sums1 = inner_back(inner_grad, wi, second_grad, n1, r1, table)
+        (attended_grad, inner_grad) = together(attended_grad, inner_grad)
         lefts, rights = [first_low, context], [inner_grad, attended_grad]
-        other = grads(where, lefts, [0, 1], rights, True)
-        other = [swap(a, CORE_SWAP) for a in other]
-    dq, dk, dv, sums0 = attention_back(q, k, v, lse, attended_grad, wo, segment_ids)
-    if by_links:
-        mine = grads(where, lefts, [0, 1], rights, False, other)
-        inner_weight_grad, output_grad = reduce_shards(where, *mine, False, [ff, width])
+        other = grads("inner_grad_a", where, lefts, [0, 1], rights)
+        (other, attended_grad, from_x, from_y, x_f, y_f, xy_f) = together(
+            other, attended_grad, from_x, from_y, x_f[2:], y_f[2:], xy_f
+        )
+        other = swap(other, CORE_SWAP)
+        x_f, y_f, xy_f = swap(x_f, X_SWAP), swap(y_f, Y_SWAP), swap(xy_f, XY_SWAP)
+        back_a = attention_step(attended_grad, 0, cut)
+        (other, back_a, attended_grad) = together(other, back_a, attended_grad)
+        mine = grads("inner_grad_b", where, lefts, [0, 1], rights, other, "place")
+        (mine, attended_grad) = together(mine, attended_grad)
+        back_b = attention_step(attended_grad, cut, width - cut)
+        dq, dk, dv, sums0 = (jnp.concatenate([a, b], axis=1) for a, b in zip(back_a, back_b))
         rights = [dq, dk, dv]
-        other = grads(where, [tokens], [0, 0, 0], rights, True)
-        other = [swap(a, CORE_SWAP) for a in other]
-        mine = grads(where, [tokens], [0, 0, 0], rights, False, other)
-        query_grad, key_grad, value_grad = reduce_shards(where, *mine, True, [width] * 3)
+        other = grads("query_grad_a", where, [tokens], [0, 0, 0], rights)
+        (other, dq, dk, dv, sums0, x_f, y_f, xy_f, mine) = together(other, dq, dk, dv, sums0, x_f, y_f, xy_f, mine)
+        rights = [dq, dk, dv]
+        parts_i = plane(mine)
+        other = swap(other, CORE_SWAP)
+        totals_f = [wide(same_f[d], xy_f[d], from_x[d], from_y[d]) for d in range(2)]
+        totals_f += [wide(same_f[2 + d], xy_f[2 + d], x_f[d], y_f[d]) for d in range(2)]
+        mine = grads("query_grad_b", where, [tokens], [0, 0, 0], rights, other, "place")
+        odd_f = swap(low(jnp.stack([totals_f[1], totals_f[3]])), Z_SWAPS[1])
+        both = jnp.concatenate([jnp.stack([sums2, sums1, sums0]), head[None]])
+        (mine, odd_f, even_f, dq, dk, dv, both) = together(mine, odd_f, [totals_f[0], totals_f[2]], dq, dk, dv, both)
+        go_f = swap(low(wide(even_f[1], odd_f[1])), Z_SWAPS[2])
+        both = doubled(both, Z_SWAPS[1])
+        tokens_grad = tokens_back(residual_grad, dq, dk, dv, wq, wk, wv)
+        (parts_i, mine, go_f, stay_f, tokens_grad, both) = together(
+            parts_i, mine, go_f, wide(even_f[0], odd_f[0]), tokens_grad, both
+        )
+        parts_q = plane(mine)
+        own_f = low(wide(stay_f, go_f))
+        totals_i = sums_by_z(parts_i)
+        odd_i = swap(low(jnp.stack([totals_i[1], totals_i[3]])), Z_SWAPS[1])
+        both = doubled(both, Z_SWAPS[2])
+        (odd_i, own_f, even_i, both) = together(odd_i, own_f, [totals_i[0], totals_i[2]], both)
+        go_i = swap(low(wide(even_i[1], odd_i[1])), Z_SWAPS[2])
+        stay_i = wide(even_i[0], odd_i[0])
+        (parts_q, go_i, stay_i, own_f, both) = together(parts_q, go_i, stay_i, own_f, both)
+        totals_q = sums_by_z(parts_q)
+        z_q = [swap(low(totals_q[d]), Z_SWAPS[d]) for d in (1, 2, 3)]
+        own_i = low(wide(stay_i, go_i))
+        both = doubled(both, X_SWAP)
+        (z_q, own_q, own_i, both, own_f) = together(z_q, totals_q[0], own_i, both, own_f)
+        def shared(own):
+            return [own, swap(own, CORE_SWAP), swap(own, X_SWAP), swap(own, X_CORE_SWAP)]
+
+        all_f = shared(own_f)
+        own_q = low(wide(own_q, *z_q))
+        both = doubled(both, Y_SWAP)
+        (all_f, own_q, both, own_i) = together(all_f, own_q, both, own_i)
+        all_q, all_i = shared(own_q), shared(own_i)
+        both = doubled(both, CORE_SWAP)
+        (outer_grad,) = place_shards(where, all_f, [width])
+        inner_weight_grad, output_grad = place_shards(where, all_i, [ff, width])
+        query_grad, key_grad, value_grad = place_shards(where, all_q, [width] * 3)
+        sums, heads = both[:3], both[3:]
     else:
+
         def reduced(left, right):
             local_grad = lax.dot_general(left, right, (((0,), (0,)), ((), ())), preferred_element_type=F32)
             shard = lax.psum_scatter(local_grad, "fsdp", scatter_dimension=0, tiled=True)
-            return lax.psum(shard.astype(LOW), "dp").astype(F32)
-
+            return lax.psum(low(shard), "dp").astype(F32)
+
+        inner_grad = inner_grads(branch_grad, wf, slope)
+        residual_grad, attended_grad, sums1 = inner_back(inner_grad, wi, second_grad, n1, r1, table)
+        dq, dk, dv, sums0 = attention_step(attended_grad, 0, width)
         outer_grad = reduced(activated, branch_grad)
         inner_weight_grad = reduced(first_low, inner_grad)
         output_grad = reduced(context, attended_grad)
         query_grad, key_grad, value_grad = (reduced(tokens, d) for d in (dq, dk, dv))
-    tokens_grad = tokens_back(residual_grad, dq, dk, dv, wq, wk, wv)
-
-    sums = jnp.concatenate([sums2[:3], sums1[:3], sums0[:2], inner_sums.reshape(ff // width, width)])
-    if by_links:
-        for pairs in (CORE_SWAP, X_SWAP, Y_SWAP, *Z_SWAPS):
-            sums = sums + swap(sums, pairs)
-    else:
-        sums = lax.psum(sums, MESH_AXES)
-    vectors = lax.dynamic_slice(sums, (0, fsdp * local), (8, local))
-    inner_bias_grad = lax.dynamic_slice(sums[8:].reshape(ff), (fsdp * (ff // shards),), (ff // shards,))
-
-    heads = everywhere(head.astype(LOW), "fsdp", shards).reshape(shards * 8, width)
-    heads = everywhere(heads, "dp", lax.axis_size("dp")).reshape(-1, 8, width)
+        tokens_grad = tokens_back(residual_grad, dq, dk, dv, wq, wk, wv)
+        sums = lax.psum(jnp.stack([sums2, sums1, sums0]), MESH_AXES)
+        heads = lax.all_gather(head, MESH_AXES)
+
+    vectors = lax.dynamic_slice(sums, (0, 0, fsdp * local), (3, 8, local))
+    inner_bias_grad = lax.dynamic_slice(
+        sums[1, 3 : 3 + ff // width].reshape(ff), (fsdp * (ff // shards),), (ff // shards,)
+    )
     class_rows, pre_grads, pooled = heads[:, 0], heads[:, 1], heads[:, 2]
     logit_grads = heads[:, 3, :CLASSES]
 
@@ -816,20 +986,20 @@
         tokens_grad[None],
         loss[0, :1],
         query_grad,
-        vectors[6],
+        vectors[2, 0],
         key_grad,
         value_grad,
-        vectors[7],
+        vectors[2, 1],
         output_grad,
-        vectors[5],
-        vectors[3],
-        vectors[4],
+        vectors[1, 2],
+        vectors[1, 0],
+        vectors[1, 1],
         inner_weight_grad,
         inner_bias_grad,
         outer_grad,
-        vectors[2],
-        vectors[0],
-        vectors[1],
+        vectors[0, 2],
+        vectors[0, 0],
+        vectors[0, 1],
         pooler_grad,
         pooler_bias_grad,
         class_grad,

time: 409 us -> 289 us (0.71)
  local copies, waits for them, and re-layouts: 51.5 us -> 7.26 us
  starting transfers between devices: 90.4 us -> 59.2 us
  Pallas kernels: 113 us -> 89.5 us
  other arithmetic: 22.8 us -> 5.72 us
    all_to_all x10 -> x0, starting transfers between devices: 45.6 us -> none  [the longest x7 30.7 us: z_exchange(): lax.all_to_all(a.reshape(four * rows, columns), MESH_AXES, 0, 0, axis_ind...]
    all_to_all x10 -> x0, waiting for transfers between devices: 42.1 us -> none  [the longest x7 40.8 us: z_exchange(): lax.all_to_all(a.reshape(four * rows, columns), MESH_AXES, 0, 0, axis_ind...]
    ppermute x63, waiting for transfers between devices: 79.5 us -> 120 us  [swap(): return lax.ppermute(a, MESH_AXES, pairs)]
    unnamed x146 -> x14, local copies, waits for them, and re-layouts: 32.9 us -> 0.98 us
    pallas_call x20 -> x22, Pallas kernels: 113 us -> 89.5 us  [call(): pl.pallas_call(kernel, name=name, out_shape=outs, grid_spec=pltpu.Prefetc...]
    ppermute x63, starting transfers between devices: 44.8 us -> 59.2 us  [swap(): return lax.ppermute(a, MESH_AXES, pairs)]
    convert_element_type x8 -> x4, other arithmetic: 13.5 us -> 0.13 us  [the longest x3 0.13 us: low(): return a.astype(LOW)]
    broadcast_in_dim x7 -> x0, local copies, waits for them, and re-layouts: 5.29 us -> none  [the longest x4 3.25 us: gather_weights(): near = z_exchange(jnp.broadcast_to(own[None], (4, *own.shape)))]
  transfers between devices with their start and end apart: 73 -> 63, of which waited for: 22 -> 31; matrix products, arithmetic and copies ran while one was open for 10% -> 1% of each run, Pallas kernels for 17% -> 25%
where the time goes in v2:
time: 289 us; the launch traced here: 286 us
  waiting for transfers between devices  120 us (42%)
  Pallas kernels  89.5 us (31%)
  starting transfers between devices  59.2 us (20%)
  local copies, waits for them, and re-layouts  7.26 us (3%)
  other arithmetic  5.72 us (2%)
    ppermute x63, waiting for transfers between devices, swap(): return lax.ppermute(a, MESH_AXES, pairs)  120 us
    pallas_call x22, Pallas kernels, call(): pl.pallas_call(kernel, name=name, out_shape=outs, grid_spec=pltpu.Prefetc...  89.5 us
    ppermute x63, starting transfers between devices, swap(): return lax.ppermute(a, MESH_AXES, pairs)  59.2 us
  transfers between devices with their start and end apart: 63, of which 31 were waited for; matrix products, arithmetic and copies ran while one was open for 1% of the time, Pallas kernels for 25%

profile of v2, /device:TPU:0, one launch (start us, length us, event | category | flops | bytes accessed | tf_op | source)
XLA Modules:
  0.0 285.9 jit_solution(2018677153113230467)
XLA Ops:
  4.7 5.1 %collective-permute-start.2 = (bf16[56,1152]{1,0:T(8,128)(2,1)S(1)}, bf16[56,1152]{1,0:T(8,128)(2,1)S(1)}, u32[]{:S(2)}, u32[]{:S(2)}) collective-permute-start(bf16[56,1152]{1,0:T(8,128)(2,1)S(1)} %get-tuple-element.226), channel_id=1, source_target_pairs={{0,6},{1,7},{2,4},{3,5},{4,2},{5,3},{6,0},{7,1},{8,14},{9,15},{10,... | collective-permute-start | bytes 387080 | tf_op jit(solution)/shard_map/ppermute | solution.py:691
  10.5 3.7 %collective-permute-done.2 = bf16[56,1152]{1,0:T(8,128)(2,1)S(1)} collective-permute-done((bf16[56,1152]{1,0:T(8,128)(2,1)S(1)}, bf16[56,1152]{1,0:T(8,128)(2,1)S(1)}, u32[]{:S(2)}, u32[]{:S(2)}) %collective-permute-start.2) | collective-permute-done | bytes 129056 | tf_op jit(solution)/shard_map/ppermute | solution.py:691
  14.2 6.5 %collective-permute-done.1 = bf16[56,1152]{1,0:T(8,128)(2,1)S(1)} collective-permute-done((bf16[56,1152]{1,0:T(8,128)(2,1)S(1)}, bf16[56,1152]{1,0:T(8,128)(2,1)S(1)}, u32[]{:S(2)}, u32[]{:S(2)}) %collective-permute-start.1) | collective-permute-done | bytes 129056 | tf_op jit(solution)/shard_map/ppermute | solution.py:691
  28.3 5.0 %collective-permute-done.7 = bf16[48,1920]{1,0:T(8,128)(2,1)S(1)} collective-permute-done((bf16[48,1920]{1,0:T(8,128)(2,1)S(1)}, bf16[48,1920]{1,0:T(8,128)(2,1)S(1)}, u32[]{:S(2)}, u32[]{:S(2)}) %collective-permute-start.7) | collective-permute-done | bytes 184352 | tf_op jit(solution)/shard_map/ppermute | solution.py:691
  33.3 7.3 %collective-permute-done.6 = bf16[48,1920]{1,0:T(8,128)(2,1)S(1)} collective-permute-done((bf16[48,1920]{1,0:T(8,128)(2,1)S(1)}, bf16[48,1920]{1,0:T(8,128)(2,1)S(1)}, u32[]{:S(2)}, u32[]{:S(2)}) %collective-permute-start.6) | collective-permute-done | bytes 184352 | tf_op jit(solution)/shard_map/ppermute | solution.py:691
  44.9 7.8 %collective-permute-done.12 = bf16[240,384]{1,0:T(8,128)(2,1)S(1)} collective-permute-done((bf16[240,384]{1,0:T(8,128)(2,1)S(1)}, bf16[240,384]{1,0:T(8,128)(2,1)S(1)}, u32[]{:S(2)}, u32[]{:S(2)}) %collective-permute-start.12) | collective-permute-done | bytes 184352 | tf_op jit(solution)/shard_map/ppermute | solution.py:691
  52.7 3.5 %collective-permute-start.10 = (bf16[240,384]{1,0:T(8,128)(2,1)S(1)}, bf16[240,384]{1,0:T(8,128)(2,1)}, u32[]{:S(2)}, u32[]{:S(2)}) collective-permute-start(bf16[240,384]{1,0:T(8,128)(2,1)S(1)} %get-tuple-element.256), channel_id=1, source_target_pairs={{0,2},{1,3},{2,0},{3,1},{4,6},{5,7},{6,4},{7,5},{8,10},{9,11},{10,... | collective-permute-start | bytes 552968 | tf_op jit(solution)/shard_map/ppermute | solution.py:691
  56.6 3.5 %collective-permute-done.11 = bf16[240,384]{1,0:T(8,128)(2,1)} collective-permute-done((bf16[240,384]{1,0:T(8,128)(2,1)S(1)}, bf16[240,384]{1,0:T(8,128)(2,1)}, u32[]{:S(2)}, u32[]{:S(2)}) %collective-permute-start.11) | collective-permute-done | bytes 184352 | tf_op jit(solution)/shard_map/ppermute | solution.py:691
  69.3 3.1 %place_weights.3 = (bf16[4,2,2,48,768]{4,3,2,1,0:T(8,128)(2,1)S(1)}, bf16[4,2,2,48,768]{4,3,2,1,0:T(8,128)(2,1)S(1)}, bf16[4,2,2,48,768]{4,3,2,1,0:T(8,128)(2,1)S(1)}) custom-call(s32[4]{0:T(128)S(1)} %pad_add_fusion.where, bf16[4,56,1152]{2,1,0:T(8,128)(2,1)S(1)} %pad_maximum_fusion.3.refs_0_, bf16[4,56,1152]{2,1,0:T(8,128)(2,1)S(1)} %get-tuple-element.443.refs_1_, ...), custom_call_target="tpu_custom_call" | custom-call | bytes 516096 | tf_op jit(solution)/shard_map/place_weights/pallas_call | solution.py:45
  72.5 8.9 %attention.1 = (bf16[512,768]{1,0:T(8,128)(2,1)S(1)}, bf16[512,768]{1,0:T(8,128)(2,1)S(1)}, bf16[512,768]{1,0:T(8,128)(2,1)S(1)}, bf16[512,768]{1,0:T(8,128)(2,1)S(1)}, f32[3,8,512]{2,1,0:T(8,128)S(1)}) custom-call(bf16[512,768]{1,0:T(8,128)(2,1)S(1)} %bitcast.119, bf16[768,768]{1,0:T(8,128)(2,1)S(1)} %bitcast.126, bf16[768,768]{1,0:T(8,128)(2,1)S(1)} %bitcast.128, ...), custom_call_target="tpu_custom_call" | custom-call | flops 163577856 | bytes 417792 | tf_op jit(solution)/shard_map/attention/pallas_call | solution.py:45
  85.0 15.6 %collective-permute-done.21.refs_2_ = bf16[4,240,384]{2,1,0:T(8,128)(2,1)S(1)} collective-permute-done((bf16[4,240,384]{2,1,0:T(8,128)(2,1)S(1)}, bf16[4,240,384]{2,1,0:T(8,128)(2,1)S(1)}, u32[]{:S(2)}, u32[]{:S(2)}) %collective-permute-start.21) | collective-permute-done | bytes 737312 | tf_op jit(solution)/shard_map/ppermute | solution.py:691
  105.1 2.7 place_weights.4
  110.1 11.4 %inner.1 = (bf16[512,3072]{1,0:T(8,128)(2,1)S(1)}, bf16[512,3072]{1,0:T(8,128)(2,1)S(1)}) custom-call(bf16[512,768]{1,0:T(8,128)(2,1)S(1)} %get-tuple-element.277.low.refs_0_, bf16[768,3072]{1,0:T(8,128)(2,1)S(1)} %bitcast.115, f32[1,3072]{1,0:T(1,128)S(1)} %reshape.177.bi), custom_call_target="tpu_custom_call" | custom-call | flops 150994944 | bytes 688128 | tf_op jit(solution)/shard_map/inner/pallas_call | solution.py:45
  124.7 2.8 place_weights.5
  127.6 7.8 %outer.1 = (bf16[512,768]{1,0:T(8,128)(2,1)}, f32[512,768]{1,0:T(8,128)S(1)}, bf16[512,768]{1,0:T(8,128)(2,1)S(1)}, f32[8,768]{1,0:T(8,128)S(1)}, f32[8,768]{1,0:T(8,128)S(1)}, /*index=5*/f32[8,128]{1,0:T(8,128)S(1)}) custom-call(s32[1]{0:T(128)S(6)} %copy.64.labels, f32[3]{0:T(128)S(1)} %convert_element_type.255.bias3, ...), custom_call_target="tpu_custom_call" | custom-call | flops 150994944 | bytes 835584 | tf_op jit(solution)/shard_map/outer/pallas_call | solution.py:45
  135.4 3.2 %outer_grad_a.1 = bf16[4,4,192,384]{3,2,1,0:T(8,128)(2,1)S(1)} custom-call(s32[4]{0:T(128)S(1)} %pad_add_fusion.where, bf16[512,3072]{1,0:T(8,128)(2,1)S(1)} %get-tuple-element.282.act.refs_0_, bf16[512,768]{1,0:T(8,128)(2,1)S(1)} %get-tuple-element.295.refs_1_.bg), custom_call_target="tpu_custom_call" | custom-call | flops 75497472 | bytes 344064 | tf_op jit(solution)/shard_map/outer_grad_a/pallas_call | solution.py:45
  138.8 4.1 %inner_grads.1.ig.refs_2_ = bf16[512,3072]{1,0:T(8,128)(2,1)S(1)} custom-call(bf16[512,768]{1,0:T(8,128)(2,1)S(1)} %get-tuple-element.295.refs_1_.bg, bf16[3072,768]{1,0:T(8,128)(2,1)S(1)} %bitcast.118, bf16[512,3072]{1,0:T(8,128)(2,1)S(1)} %get-tuple-element.297.slope), custom_call_target="tpu_custom_call" | custom-call | flops 150994944 | bytes 688128 | tf_op jit(solution)/shard_map/inner_grads/pallas_call | solution.py:45
  143.2 3.2 %outer_grad_b.1 = (bf16[4,192,384]{2,1,0:T(8,128)(2,1)S(1)}, bf16[4,192,384]{2,1,0:T(8,128)(2,1)S(1)}, bf16[4,192,384]{2,1,0:T(8,128)(2,1)S(1)}, bf16[4,192,384]{2,1,0:T(8,128)(2,1)S(1)}) custom-call(s32[4]{0:T(128)S(1)} %pad_add_fusion.where, bf16[512,3072]{1,0:T(8,128)(2,1)S(1)} %get-tuple-element.282.act.refs_0_, ...), custom_call_target="tpu_custom_call" | custom-call | flops 75497472 | bytes 344064 | tf_op jit(solution)/shard_map/outer_grad_b/pallas_call | solution.py:45
  148.6 6.0 %inner_back.1 = (f32[512,768]{1,0:T(8,128)S(1)}, bf16[512,768]{1,0:T(8,128)(2,1)S(1)}, f32[8,768]{1,0:T(8,128)S(1)}) custom-call(bf16[512,3072]{1,0:T(8,128)(2,1)S(1)} %inner_grads.1.ig.refs_2_, bf16[768,3072]{1,0:T(8,128)(2,1)S(1)} %bitcast.116, f32[512,768]{1,0:T(8,128)S(1)} %get-tuple-element.305.sg, f32[512,768]{1,0:T(8,128)S(1)} %get-tuple-element.291.n1, ...), custom_call_target="tpu_custom_call" | custom-call | flops 150994944 | bytes 884736 | tf_op jit(solution)/shard_map/inner_back/pallas_call | solution.py:45
  154.7 2.6 inner_grad_a.1
  161.0 7.9 %attention_back.2 = (bf16[512,512]{1,0:T(8,128)(2,1)S(1)}, bf16[512,512]{1,0:T(8,128)(2,1)S(1)}, bf16[512,512]{1,0:T(8,128)(2,1)S(1)}, f32[8,512]{1,0:T(8,128)S(1)}) custom-call(bf16[512,768]{1,0:T(8,128)(2,1)S(1)} %get-tuple-element.314.q, bf16[512,768]{1,0:T(8,128)(2,1)S(1)} %get-tuple-element.315.k, bf16[512,768]{1,0:T(8,128)(2,1)S(1)} %get-tuple-element.316.v, ...), custom_call_target="tpu_custom_call" | custom-call | flops 109051904 | bytes 311296 | tf_op jit(solution)/shard_map/attention_back/pallas_call | solution.py:45
  168.9 2.6 inner_grad_b.1
  171.6 3.6 %attention_back.3 = (bf16[512,256]{1,0:T(8,128)(2,1)S(1)}, bf16[512,256]{1,0:T(8,128)(2,1)S(1)}, bf16[512,256]{1,0:T(8,128)(2,1)S(1)}, f32[8,256]{1,0:T(8,128)S(1)}) custom-call(bf16[512,768]{1,0:T(8,128)(2,1)S(1)} %get-tuple-element.314.q, bf16[512,768]{1,0:T(8,128)(2,1)S(1)} %get-tuple-element.315.k, bf16[512,768]{1,0:T(8,128)(2,1)S(1)} %get-tuple-element.316.v, ...), custom_call_target="tpu_custom_call" | custom-call | flops 54525952 | bytes 155648 | tf_op jit(solution)/shard_map/attention_back/pallas_call | solution.py:45
  186.0 3.6 %collective-permute-done.39 = bf16[2,192,384]{2,1,0:T(8,128)(2,1)S(1)} collective-permute-done((bf16[2,192,384]{2,1,0:T(8,128)(2,1)S(1)}, bf16[2,192,384]{2,1,0:T(8,128)(2,1)S(1)}, u32[]{:S(2)}, u32[]{:S(2)}) %collective-permute-start.39) | collective-permute-done | bytes 294944 | tf_op jit(solution)/shard_map/ppermute | solution.py:691
  192.3 6.1 %tokens_back.1 = f32[512,768]{1,0:T(8,128)} custom-call(f32[512,768]{1,0:T(8,128)S(1)} %get-tuple-element.374.res, bf16[512,768]{1,0:T(8,128)(2,1)S(1)} %constant_dynamic-update-slice_fusion.refs_1_.dq, bf16[512,768]{1,0:T(8,128)(2,1)S(1)} %constant_dynamic-update-slice_fusion.2.refs_2_.dk, ...), custom_call_target="tpu_custom_call" | custom-call | flops 113246208 | bytes 565248 | tf_op jit(solution)/shard_map/tokens_back/pallas_call | solution.py:45
  199.6 16.6 %collective-permute-done.36 = bf16[4,48,1920]{2,1,0:T(8,128)(2,1)S(1)} collective-permute-done((bf16[4,48,1920]{2,1,0:T(8,128)(2,1)S(1)}, bf16[4,48,1920]{2,1,0:T(8,128)(2,1)S(1)}, u32[]{:S(2)}, u32[]{:S(2)}) %collective-permute-start.36) | collective-permute-done | bytes 737312 | tf_op jit(solution)/shard_map/ppermute | solution.py:691
  224.6 7.2 %collective-permute-done.45 = bf16[2,48,1920]{2,1,0:T(8,128)(2,1)S(1)} collective-permute-done((bf16[2,48,1920]{2,1,0:T(8,128)(2,1)S(1)}, bf16[2,48,1920]{2,1,0:T(8,128)(2,1)S(1)}, u32[]{:S(2)}, u32[]{:S(2)}) %collective-permute-start.45) | collective-permute-done | bytes 368672 | tf_op jit(solution)/shard_map/ppermute | solution.py:691
  232.1 6.7 %collective-permute-done.44 = bf16[4,48,1152]{2,1,0:T(8,128)(2,1)S(1)} collective-permute-done((bf16[4,48,1152]{2,1,0:T(8,128)(2,1)S(1)}, bf16[4,48,1152]{2,1,0:T(8,128)(2,1)S(1)}, u32[]{:S(2)}, u32[]{:S(2)}) %collective-permute-start.44) | collective-permute-done | bytes 442400 | tf_op jit(solution)/shard_map/ppermute | solution.py:691
  246.8 4.3 %collective-permute-done.51 = f32[7,8,768]{2,1,0:T(8,128)S(1)} collective-permute-done((f32[7,8,768]{2,1,0:T(8,128)S(1)}, f32[7,8,768]{2,1,0:T(8,128)S(1)}, u32[]{:S(2)}, u32[]{:S(2)}) %collective-permute-start.51) | collective-permute-done | bytes 172064 | tf_op jit(solution)/shard_map/ppermute | solution.py:691
  256.6 6.9 %collective-permute-done.55 = f32[11,8,768]{2,1,0:T(8,128)S(1)} collective-permute-done((f32[11,8,768]{2,1,0:T(8,128)S(1)}, f32[11,8,768]{2,1,0:T(8,128)S(1)}, u32[]{:S(2)}, u32[]{:S(2)}) %collective-permute-start.55) | collective-permute-done | bytes 270368 | tf_op jit(solution)/shard_map/ppermute | solution.py:691
  269.4 2.5 collective-permute-done.57.refs_2_
  275.8 3.5 %collective-permute-done.61.refs_2_ = bf16[48,1920]{1,0:T(8,128)(2,1)S(1)} collective-permute-done((bf16[48,1920]{1,0:T(8,128)(2,1)S(1)}, bf16[48,1920]{1,0:T(8,128)(2,1)S(1)}, u32[]{:S(2)}, u32[]{:S(2)}) %collective-permute-start.61) | collective-permute-done | bytes 184352 | tf_op jit(solution)/shard_map/ppermute | solution.py:691
  (197 shorter events, 98.1 us)
Async XLA Ops:
  9.8 10.9 %collective-permute-start.1 = (bf16[56,1152]{1,0:T(8,128)(2,1)S(1)}, bf16[56,1152]{1,0:T(8,128)(2,1)S(1)}, u32[]{:S(2)}, u32[]{:S(2)}) collective-permute-start(bf16[56,1152]{1,0:T(8,128)(2,1)S(1)} %get-tuple-element.226), channel_id=1, source_target_pairs={{0,4},{1,5},{2,6},{3,7},{4,0},{5,1},{6,2},{7,3},{8,12},{9,13},{10,... | collective-permute-start | bytes 387080 | tf_op jit(solution)/shard_map/ppermute | solution.py:691
  20.8 19.8 %collective-permute-start.4 = (bf16[4,56,1152]{2,1,0:T(8,128)(2,1)S(1)}, bf16[4,56,1152]{2,1,0:T(8,128)(2,1)S(1)}, u32[]{:S(2)}, u32[]{:S(2)}) collective-permute-start(bf16[4,56,1152]{2,1,0:T(8,128)(2,1)S(1)} %pad_maximum_fusion.3.refs_0_), channel_id=1, source_target_pairs={{0,1},{1,0},{2,3},{3,2},{4,5},{5,4},{6,7},{7,6},{8,9},{9,8},{10,11... | collective-permute-start | bytes 1548296 | tf_op jit(solution)/shard_map/ppermute | solution.py:691
  22.4 18.2 %collective-permute-start.3 = (bf16[4,56,1152]{2,1,0:T(8,128)(2,1)S(1)}, bf16[4,56,1152]{2,1,0:T(8,128)(2,1)S(1)}, u32[]{:S(2)}, u32[]{:S(2)}) collective-permute-start(bf16[4,56,1152]{2,1,0:T(8,128)(2,1)S(1)} %pad_maximum_fusion.3.refs_0_), channel_id=1, source_target_pairs={{0,16},{1,17},{2,18},{3,19},{4,20},{5,21},{6,22},{7,23},{8,24},{9,... | collective-permute-start | bytes 1548296 | tf_op jit(solution)/shard_map/ppermute | solution.py:691
  26.4 14.2 %collective-permute-start.6 = (bf16[48,1920]{1,0:T(8,128)(2,1)S(1)}, bf16[48,1920]{1,0:T(8,128)(2,1)S(1)}, u32[]{:S(2)}, u32[]{:S(2)}) collective-permute-start(bf16[48,1920]{1,0:T(8,128)(2,1)S(1)} %get-tuple-element.235), channel_id=1, source_target_pairs={{0,4},{1,5},{2,6},{3,7},{4,0},{5,1},{6,2},{7,3},{8,12},{9,13},{10,... | collective-permute-start | bytes 552968 | tf_op jit(solution)/shard_map/ppermute | solution.py:691
  26.4 14.2 %collective-permute-start.5 = (bf16[48,1920]{1,0:T(8,128)(2,1)S(1)}, bf16[48,1920]{1,0:T(8,128)(2,1)S(1)}, u32[]{:S(2)}, u32[]{:S(2)}) collective-permute-start(bf16[48,1920]{1,0:T(8,128)(2,1)S(1)} %get-tuple-element.235), channel_id=1, source_target_pairs={{0,2},{1,3},{2,0},{3,1},{4,6},{5,7},{6,4},{7,5},{8,10},{9,11},{10,... | collective-permute-start | bytes 552968 | tf_op jit(solution)/shard_map/ppermute | solution.py:691
  42.0 20.0 %collective-permute-start.13 = (bf16[12,56,1152]{2,1,0:T(8,128)(2,1)}, bf16[12,56,1152]{2,1,0:T(8,128)(2,1)}, u32[]{:S(2)}, u32[]{:S(2)}) collective-permute-start(bf16[12,56,1152]{2,1,0:T(8,128)(2,1)} %pad_maximum_fusion), channel_id=1, source_target_pairs={{0,8},{1,9},{2,10},{3,11},{4,12},{5,13},{6,14},{7,15},{8,0},{9,1},... | collective-permute-start | bytes 4644872 | tf_op jit(solution)/shard_map/ppermute | solution.py:691
  42.1 19.8 %collective-permute-start.9 = (bf16[4,48,1920]{2,1,0:T(8,128)(2,1)S(1)}, bf16[4,48,1920]{2,1,0:T(8,128)(2,1)S(1)}, u32[]{:S(2)}, u32[]{:S(2)}) collective-permute-start(bf16[4,48,1920]{2,1,0:T(8,128)(2,1)S(1)} %pad_maximum_fusion.1.refs_0_), channel_id=1, source_target_pairs={{0,16},{1,17},{2,18},{3,19},{4,20},{5,21},{6,22},{7,23},{8,24},{9,... | collective-permute-start | bytes 2211848 | tf_op jit(solution)/shard_map/ppermute | solution.py:691
  42.7 19.2 %collective-permute-start.8 = (bf16[4,56,1152]{2,1,0:T(8,128)(2,1)S(1)}, bf16[4,56,1152]{2,1,0:T(8,128)(2,1)}, u32[]{:S(2)}, u32[]{:S(2)}) collective-permute-start(bf16[4,56,1152]{2,1,0:T(8,128)(2,1)S(1)} %collective-permute-done.3.refs_4_), channel_id=1, source_target_pairs={{0,1},{1,0},{2,3},{3,2},{4,5},{5,4},{6,7},{7,6},{8,9},{9,8},{10,11... | collective-permute-start | bytes 1548296 | tf_op jit(solution)/shard_map/ppermute | solution.py:691
  44.9 15.2 %collective-permute-start.11 = (bf16[240,384]{1,0:T(8,128)(2,1)S(1)}, bf16[240,384]{1,0:T(8,128)(2,1)}, u32[]{:S(2)}, u32[]{:S(2)}) collective-permute-start(bf16[240,384]{1,0:T(8,128)(2,1)S(1)} %get-tuple-element.256), channel_id=1, source_target_pairs={{0,4},{1,5},{2,6},{3,7},{4,0},{5,1},{6,2},{7,3},{8,12},{9,13},{10,... | collective-permute-start | bytes 552968 | tf_op jit(solution)/shard_map/ppermute | solution.py:691
  63.9 17.5 %collective-permute-start.16 = (bf16[4,240,384]{2,1,0:T(8,128)(2,1)S(1)}, bf16[4,240,384]{2,1,0:T(8,128)(2,1)}, u32[]{:S(2)}, u32[]{:S(2)}) collective-permute-start(bf16[4,240,384]{2,1,0:T(8,128)(2,1)S(1)} %pad_maximum_fusion.2.refs_0_), channel_id=1, source_target_pairs={{0,16},{1,17},{2,18},{3,19},{4,20},{5,21},{6,22},{7,23},{8,24},{9,... | collective-permute-start | bytes 2211848 | tf_op jit(solution)/shard_map/ppermute | solution.py:691
  65.5 16.3 %collective-permute-start.15 = (bf16[4,48,1920]{2,1,0:T(8,128)(2,1)S(1)}, bf16[4,48,1920]{2,1,0:T(8,128)(2,1)}, u32[]{:S(2)}, u32[]{:S(2)}) collective-permute-start(bf16[4,48,1920]{2,1,0:T(8,128)(2,1)S(1)} %pad_maximum_fusion.1.refs_0_), channel_id=1, source_target_pairs={{0,1},{1,0},{2,3},{3,2},{4,5},{5,4},{6,7},{7,6},{8,9},{9,8},{10,11... | collective-permute-start | bytes 2211848 | tf_op jit(solution)/shard_map/ppermute | solution.py:691
  82.3 18.4 %collective-permute-start.21 = (bf16[4,240,384]{2,1,0:T(8,128)(2,1)S(1)}, bf16[4,240,384]{2,1,0:T(8,128)(2,1)S(1)}, u32[]{:S(2)}, u32[]{:S(2)}) collective-permute-start(bf16[4,240,384]{2,1,0:T(8,128)(2,1)S(1)} %pad_maximum_fusion.2.refs_0_), channel_id=1, source_target_pairs={{0,1},{1,0},{2,3},{3,2},{4,5},{5,4},{6,7},{7,6},{8,9},{9,8},{10,11... | collective-permute-start | bytes 2211848 | tf_op jit(solution)/shard_map/ppermute | solution.py:691
  83.8 16.9 %collective-permute-start.19 = (bf16[4,48,1920]{2,1,0:T(8,128)(2,1)}, bf16[4,48,1920]{2,1,0:T(8,128)(2,1)S(1)}, u32[]{:S(2)}, u32[]{:S(2)}) collective-permute-start(bf16[4,48,1920]{2,1,0:T(8,128)(2,1)} %collective-permute-done.15.refs_2_), channel_id=1, source_target_pairs={{0,8},{1,9},{2,10},{3,11},{4,12},{5,13},{6,14},{7,15},{8,0},{9,1},... | collective-permute-start | bytes 2211848 | tf_op jit(solution)/shard_map/ppermute | solution.py:691
  83.8 19.1 %collective-permute-start.17 = (bf16[4,48,1920]{2,1,0:T(8,128)(2,1)}, bf16[4,48,1920]{2,1,0:T(8,128)(2,1)S(1)}, u32[]{:S(2)}, u32[]{:S(2)}) collective-permute-start(bf16[4,48,1920]{2,1,0:T(8,128)(2,1)} %collective-permute-done.15.refs_2_), channel_id=1, source_target_pairs={{0,16},{1,17},{2,18},{3,19},{4,20},{5,21},{6,22},{7,23},{8,24},{9,... | collective-permute-start | bytes 2211848 | tf_op jit(solution)/shard_map/ppermute | solution.py:691
  102.9 18.6 %collective-permute-start.23 = (bf16[4,240,384]{2,1,0:T(8,128)(2,1)S(1)}, bf16[4,240,384]{2,1,0:T(8,128)(2,1)S(1)}, u32[]{:S(2)}, u32[]{:S(2)}) collective-permute-start(bf16[4,240,384]{2,1,0:T(8,128)(2,1)S(1)} %pad_maximum_fusion.2.refs_0_), channel_id=1, source_target_pairs={{0,8},{1,9},{2,10},{3,11},{4,12},{5,13},{6,14},{7,15},{8,0},{9,1},... | collective-permute-start | bytes 2211848 | tf_op jit(solution)/shard_map/ppermute | solution.py:691
  103.4 18.1 %collective-permute-start.24 = (bf16[4,240,384]{2,1,0:T(8,128)(2,1)S(1)}, bf16[4,240,384]{2,1,0:T(8,128)(2,1)S(1)}, u32[]{:S(2)}, u32[]{:S(2)}) collective-permute-start(bf16[4,240,384]{2,1,0:T(8,128)(2,1)S(1)} %collective-permute-done.21.refs_2_), channel_id=1, source_target_pairs={{0,8},{1,9},{2,10},{3,11},{4,12},{5,13},{6,14},{7,15},{8,0},{9,1},... | collective-permute-start | bytes 2211848 | tf_op jit(solution)/shard_map/ppermute | solution.py:691
  103.4 18.1 %collective-permute-start.25 = (bf16[4,240,384]{2,1,0:T(8,128)(2,1)}, bf16[4,240,384]{2,1,0:T(8,128)(2,1)S(1)}, u32[]{:S(2)}, u32[]{:S(2)}) collective-permute-start(bf16[4,240,384]{2,1,0:T(8,128)(2,1)} %collective-permute-done.16.refs_4_), channel_id=1, source_target_pairs={{0,8},{1,9},{2,10},{3,11},{4,12},{5,13},{6,14},{7,15},{8,0},{9,1},... | collective-permute-start | bytes 2211848 | tf_op jit(solution)/shard_map/ppermute | solution.py:691
  103.9 18.6 %collective-permute-start.22 = (bf16[4,240,384]{2,1,0:T(8,128)(2,1)}, bf16[4,240,384]{2,1,0:T(8,128)(2,1)S(1)}, u32[]{:S(2)}, u32[]{:S(2)}) collective-permute-start(bf16[4,240,384]{2,1,0:T(8,128)(2,1)} %collective-permute-done.16.refs_4_), channel_id=1, source_target_pairs={{0,1},{1,0},{2,3},{3,2},{4,5},{5,4},{6,7},{7,6},{8,9},{9,8},{10,11... | collective-permute-start | bytes 2211848 | tf_op jit(solution)/shard_map/ppermute | solution.py:691
  157.3 11.6 %collective-permute-start.31 = (bf16[4,4,48,1920]{3,2,1,0:T(8,128)(2,1)S(1)}, bf16[4,4,48,1920]{3,2,1,0:T(8,128)(2,1)S(1)}, u32[]{:S(2)}, u32[]{:S(2)}) collective-permute-start(bf16[4,4,48,1920]{3,2,1,0:T(8,128)(2,1)S(1)} %inner_grad_a.1), channel_id=1, source_target_pairs={{0,8},{1,9},{2,10},{3,11},{4,12},{5,13},{6,14},{7,15},{8,0},{9,1},... | collective-permute-start | bytes 8847368 | tf_op jit(solution)/shard_map/ppermute | solution.py:691
  157.4 20.2 %collective-permute-start.32 = (bf16[2,192,384]{2,1,0:T(8,128)(2,1)S(1)}, bf16[2,192,384]{2,1,0:T(8,128)(2,1)S(1)}, u32[]{:S(2)}, u32[]{:S(2)}) collective-permute-start(bf16[2,192,384]{2,1,0:T(8,128)(2,1)S(1)} %get-tuple-element.338), channel_id=1, source_target_pairs={{0,16},{1,17},{2,18},{3,19},{4,20},{5,21},{6,22},{7,23},{8,24},{9,... | collective-permute-start | bytes 884744 | tf_op jit(solution)/shard_map/ppermute | solution.py:691
  158.1 21.7 %collective-permute-start.33 = (bf16[2,192,384]{2,1,0:T(8,128)(2,1)S(1)}, bf16[2,192,384]{2,1,0:T(8,128)(2,1)S(1)}, u32[]{:S(2)}, u32[]{:S(2)}) collective-permute-start(bf16[2,192,384]{2,1,0:T(8,128)(2,1)S(1)} %get-tuple-element.339), channel_id=1, source_target_pairs={{0,1},{1,0},{2,3},{3,2},{4,5},{5,4},{6,7},{7,6},{8,9},{9,8},{10,11... | collective-permute-start | bytes 884744 | tf_op jit(solution)/shard_map/ppermute | solution.py:691
  159.6 20.2 %collective-permute-start.34 = (bf16[4,192,384]{2,1,0:T(8,128)(2,1)S(1)}, bf16[4,192,384]{2,1,0:T(8,128)(2,1)S(1)}, u32[]{:S(2)}, u32[]{:S(2)}) collective-permute-start(bf16[4,192,384]{2,1,0:T(8,128)(2,1)S(1)} %get-tuple-element.340), channel_id=1, source_target_pairs={{0,17},{1,16},{2,19},{3,18},{4,21},{5,20},{6,23},{7,22},{8,25},{9,... | collective-permute-start | bytes 1769480 | tf_op jit(solution)/shard_map/ppermute | solution.py:691
  180.2 19.3 %collective-permute-start.35 = (bf16[4,48,1920]{2,1,0:T(8,128)(2,1)S(1)}, bf16[4,48,1920]{2,1,0:T(8,128)(2,1)S(1)}, u32[]{:S(2)}, u32[]{:S(2)}) collective-permute-start(bf16[4,48,1920]{2,1,0:T(8,128)(2,1)S(1)} %get-tuple-element.346), channel_id=1, source_target_pairs={{0,16},{1,17},{2,18},{3,19},{4,20},{5,21},{6,22},{7,23},{8,24},{9,... | collective-permute-start | bytes 2211848 | tf_op jit(solution)/shard_map/ppermute | solution.py:691
  181.7 34.4 %collective-permute-start.36 = (bf16[4,48,1920]{2,1,0:T(8,128)(2,1)S(1)}, bf16[4,48,1920]{2,1,0:T(8,128)(2,1)S(1)}, u32[]{:S(2)}, u32[]{:S(2)}) collective-permute-start(bf16[4,48,1920]{2,1,0:T(8,128)(2,1)S(1)} %get-tuple-element.347), channel_id=1, source_target_pairs={{0,1},{1,0},{2,3},{3,2},{4,5},{5,4},{6,7},{7,6},{8,9},{9,8},{10,11... | collective-permute-start | bytes 2211848 | tf_op jit(solution)/shard_map/ppermute | solution.py:691
  182.3 33.8 %collective-permute-start.37 = (bf16[4,48,1920]{2,1,0:T(8,128)(2,1)S(1)}, bf16[4,48,1920]{2,1,0:T(8,128)(2,1)S(1)}, u32[]{:S(2)}, u32[]{:S(2)}) collective-permute-start(bf16[4,48,1920]{2,1,0:T(8,128)(2,1)S(1)} %get-tuple-element.348), channel_id=1, source_target_pairs={{0,17},{1,16},{2,19},{3,18},{4,21},{5,20},{6,23},{7,22},{8,25},{9,... | collective-permute-start | bytes 2211848 | tf_op jit(solution)/shard_map/ppermute | solution.py:691
  190.0 26.2 %collective-permute-start.40 = (bf16[192,384]{1,0:T(8,128)(2,1)S(1)}, bf16[192,384]{1,0:T(8,128)(2,1)S(1)}, u32[]{:S(2)}, u32[]{:S(2)}) collective-permute-start(bf16[192,384]{1,0:T(8,128)(2,1)S(1)} %get-tuple-element.455), channel_id=1, source_target_pairs={{0,4},{1,5},{2,6},{3,7},{4,0},{5,1},{6,2},{7,3},{8,12},{9,13},{10,... | collective-permute-start | bytes 442376 | tf_op jit(solution)/shard_map/ppermute | solution.py:691
  217.9 14.2 %collective-permute-start.42 = (bf16[4,48,1152]{2,1,0:T(8,128)(2,1)S(1)}, bf16[4,48,1152]{2,1,0:T(8,128)(2,1)S(1)}, u32[]{:S(2)}, u32[]{:S(2)}) collective-permute-start(bf16[4,48,1152]{2,1,0:T(8,128)(2,1)S(1)} %get-tuple-element.382), channel_id=1, source_target_pairs={{0,16},{1,17},{2,18},{3,19},{4,20},{5,21},{6,22},{7,23},{8,24},{9,... | collective-permute-start | bytes 1327112 | tf_op jit(solution)/shard_map/ppermute | solution.py:691
  219.0 13.2 %collective-permute-start.43 = (bf16[4,48,1152]{2,1,0:T(8,128)(2,1)S(1)}, bf16[4,48,1152]{2,1,0:T(8,128)(2,1)S(1)}, u32[]{:S(2)}, u32[]{:S(2)}) collective-permute-start(bf16[4,48,1152]{2,1,0:T(8,128)(2,1)S(1)} %get-tuple-element.383), channel_id=1, source_target_pairs={{0,1},{1,0},{2,3},{3,2},{4,5},{5,4},{6,7},{7,6},{8,9},{9,8},{10,11... | collective-permute-start | bytes 1327112 | tf_op jit(solution)/shard_map/ppermute | solution.py:691
  219.9 18.9 %collective-permute-start.44 = (bf16[4,48,1152]{2,1,0:T(8,128)(2,1)S(1)}, bf16[4,48,1152]{2,1,0:T(8,128)(2,1)S(1)}, u32[]{:S(2)}, u32[]{:S(2)}) collective-permute-start(bf16[4,48,1152]{2,1,0:T(8,128)(2,1)S(1)} %get-tuple-element.384), channel_id=1, source_target_pairs={{0,17},{1,16},{2,19},{3,18},{4,21},{5,20},{6,23},{7,22},{8,25},{9,... | collective-permute-start | bytes 1327112 | tf_op jit(solution)/shard_map/ppermute | solution.py:691
  252.4 11.1 %collective-permute-start.54 = (bf16[192,384]{1,0:T(8,128)(2,1)S(1)}, bf16[192,384]{1,0:T(8,128)(2,1)S(1)}, u32[]{:S(2)}, u32[]{:S(2)}) collective-permute-start(bf16[192,384]{1,0:T(8,128)(2,1)S(1)} %add_convert_fusion.3.refs_0_), channel_id=1, source_target_pairs={{0,24},{1,25},{2,26},{3,27},{4,28},{5,29},{6,30},{7,31},{8,16},{9,... | collective-permute-start | bytes 442376 | tf_op jit(solution)/shard_map/ppermute | solution.py:691
  263.6 17.6 %collective-permute-start.59 = (f32[19,8,768]{2,1,0:T(8,128)S(1)}, f32[19,8,768]{2,1,0:T(8,128)S(1)}, u32[]{:S(2)}, u32[]{:S(2)}) collective-permute-start(f32[19,8,768]{2,1,0:T(8,128)S(1)} %pad_maximum_fusion.4), channel_id=1, source_target_pairs={{0,8},{1,9},{2,10},{3,11},{4,12},{5,13},{6,14},{7,15},{8,0},{9,1},... | collective-permute-start | bytes 1400840 | tf_op jit(solution)/shard_map/ppermute | solution.py:691
  266.1 13.2 %collective-permute-start.61 = (bf16[48,1920]{1,0:T(8,128)(2,1)S(1)}, bf16[48,1920]{1,0:T(8,128)(2,1)S(1)}, u32[]{:S(2)}, u32[]{:S(2)}) collective-permute-start(bf16[48,1920]{1,0:T(8,128)(2,1)S(1)} %add_convert_fusion.refs_0_), channel_id=1, source_target_pairs={{0,16},{1,17},{2,18},{3,19},{4,20},{5,21},{6,22},{7,23},{8,24},{9,... | collective-permute-start | bytes 552968 | tf_op jit(solution)/shard_map/ppermute | solution.py:691
  (37 other events, 289.3 us)

commit v3 on v2

--- a/solution.py
+++ b/solution.py
@@ -22,6 +22,7 @@
     0, 1, 2, 3, 4, 5, 6, 7, 8, 9, 13,
 )
 TABLE = 16
+COLUMNS = 384
 
 
 def dot(a, b, dims=((1,), (0,))):
@@ -502,7 +503,7 @@
     )
 
 
-def grads(name, where, lefts, which, rights, add=None, form=None):
+def grads(name, where, lefts, which, rights, add=None):
     seq = lefts[0].shape[0]
     parts = lefts[0].shape[1] // 16
     widths = tuple((w, r.shape[1] // 2) for w, r in zip(which, rights))
@@ -511,12 +512,8 @@
     specs = [full(a.shape) for a in lefts]
     specs += [pl.BlockSpec((seq, w), half, pipeline_mode=pl.Buffered(1)) for _, w in widths]
     args = [where, *lefts, *rights]
-    if add is None:
-        outs = ((4, 4, parts, total),)
-    elif form == "z":
-        outs = ((2, 4, parts, total),) * 2
-    else:
-        outs = ((4, parts, total),) * 4
+    piece = (4, parts * total // COLUMNS, COLUMNS)
+    outs = ((4, *piece),) if add is None else (piece,) * 4
     if add is not None:
         specs.append(full(add.shape))
         args.append(add)
@@ -533,25 +530,21 @@
         for place in range(4):
             hh = jnp.bitwise_xor(x, place // 2)
             yy = jnp.bitwise_xor(y, place % 2)
-            column = 0
+            top = 0
             for (at, width), right in zip(widths, right_refs):
                 rows = []
                 for dz in range(4):
                     shard = jnp.bitwise_xor(z0, dz) * 2 + yy
                     rows.append(turned[at][pl.ds(pl.multiple_of((shard * 2 + hh) * parts, 16), parts), :])
                 got = dot(jnp.concatenate(rows, axis=0), right[...]).reshape(4, parts, width)
-                cols = slice(column, column + width)
-                if add is not None:
-                    got = got + add_ref[place, :, :, cols].astype(F32)
-                got = got.astype(LOW)
-                if add is None:
-                    out_refs[0][place, :, :, cols] = got
-                elif form == "z":
-                    for dz in range(4):
-                        out_refs[dz % 2][dz // 2, place, :, cols] = got[dz]
-                else:
-                    out_refs[place][:, :, cols] = got
-                column += width
+                for column in range(0, width, COLUMNS):
+                    one = got[:, :, column : column + COLUMNS]
+                    if add is None:
+                        out_refs[0][place, :, top : top + parts, :] = one.astype(LOW)
+                    else:
+                        one = one + add_ref[place, :, top : top + parts, :].astype(F32)
+                        out_refs[place][:, top : top + parts, :] = one.astype(LOW)
+                    top += parts
 
     got = call(
         kernel,
@@ -646,32 +639,31 @@
     for place in range(4):
         hh = jnp.bitwise_xor(where[0], place // 2)
         for core in range(2):
+
             @pl.when(jnp.bitwise_xor(where[3], place % 2) == core)
             def _():
-                for (start, width), out in zip(spans, outs):
-                    out[hh, :, core * width : (core + 1) * width] = pieces[place][
-                        :, start : start + width
-                    ].astype(F32)
-
-
-def place_shards(where, pieces, widths):
-    parts = pieces[0].shape[0]
-    spans, start = [], 0
-    for width in widths:
-        spans.append((start, width // 2))
-        start += width // 2
+                for (top, rows, blocks), out in zip(spans, outs):
+                    for block in range(blocks):
+                        left = (core * blocks + block) * COLUMNS
+                        out[hh, :, left : left + COLUMNS] = pieces[place][
+                            top + block * rows : top + (block + 1) * rows, :
+                        ].astype(F32)
+
+
+def place_shards(where, pieces, spans):
+    sizes = [(2, rows, 2 * blocks * COLUMNS) for _, rows, blocks in spans]
     outs = call(
         functools.partial(shards_kernel, tuple(spans)),
-        tuple(shape(2, parts, w, dtype=F32) for w in widths),
+        tuple(shape(*size, dtype=F32) for size in sizes),
         [full(pieces[0].shape)] * 4,
-        tuple(full((2, parts, w)) for w in widths),
+        tuple(full(size) for size in sizes),
         (where, *pieces),
         prefetch=1,
-        moved=12 * parts * sum(widths),
+        moved=24 * pieces[0].size,
         vmem=12,
         name="place_shards",
     )
-    return [o.reshape(2 * parts, w) for o, w in zip(outs, widths)]
+    return [o.reshape(2 * size[1], size[2]) for o, size in zip(outs, sizes)]
 
 
 def device(x, core, z, y):
@@ -868,9 +860,10 @@
     cut = 512
     if by_links:
 
-        def doubled(both, pairs):
-            come = swap(both, pairs)
-            return jnp.concatenate([both[:3] + come[:3], both[3:], come[3:]])
+        def gathered(heads, pairs):
+            return jnp.concatenate([heads, swap(heads, pairs)])
+
+        heads = low(head)[None]
 
         def plane(parts):
             same, y, x, xy = parts
@@ -878,73 +871,80 @@
 
         other = grads("outer_grad_a", where, [activated], [0], [branch_grad])
         (other, branch_grad) = together(other, branch_grad)
-        other = swap(other, CORE_SWAP)
+        other, heads = swap(other, CORE_SWAP), gathered(heads, Z_SWAPS[1])
         inner_grad = inner_grads(branch_grad, wf, slope)
-        (other, inner_grad) = together(other, inner_grad)
-        mine = grads("outer_grad_b", where, [activated], [0], [branch_grad], other, "place")
-        (mine, inner_grad) = together(mine, inner_grad)
+        (other, inner_grad, heads) = together(other, inner_grad, heads)
+        mine = grads("outer_grad_b", where, [activated], [0], [branch_grad], other)
+        (mine, inner_grad, heads) = together(mine, inner_grad, heads)
         same_f, y_f, x_f, xy_f = mine
         from_x, from_y = swap(x_f[:2], X_SWAP), swap(y_f[:2], Y_SWAP)
+        heads = gathered(gathered(heads, Z_SWAPS[2]), Y_SWAP)
         residual_grad, attended_grad, sums1 = inner_back(inner_grad, wi, second_grad, n1, r1, table)
         (attended_grad, inner_grad) = together(attended_grad, inner_grad)
-        lefts, rights = [first_low, context], [inner_grad, attended_grad]
+        lefts, rights = [context, first_low], [attended_grad, inner_grad]
         other = grads("inner_grad_a", where, lefts, [0, 1], rights)
-        (other, attended_grad, from_x, from_y, x_f, y_f, xy_f) = together(
-            other, attended_grad, from_x, from_y, x_f[2:], y_f[2:], xy_f
+        (other, attended_grad, from_x, from_y, x_f, y_f, xy_f, heads) = together(
+            other, attended_grad, from_x, from_y, x_f[2:], y_f[2:], xy_f, heads
         )
         other = swap(other, CORE_SWAP)
         x_f, y_f, xy_f = swap(x_f, X_SWAP), swap(y_f, Y_SWAP), swap(xy_f, XY_SWAP)
+        heads = gathered(heads, X_SWAP)
         back_a = attention_step(attended_grad, 0, cut)
-        (other, back_a, attended_grad) = together(other, back_a, attended_grad)
-        mine = grads("inner_grad_b", where, lefts, [0, 1], rights, other, "place")
-        (mine, attended_grad) = together(mine, attended_grad)
+        (other, back_a, attended_grad, heads) = together(other, back_a, attended_grad, heads)
+        mine = grads("inner_grad_b", where, lefts, [0, 1], rights, other)
+        (mine, attended_grad, heads) = together(mine, attended_grad, heads)
+        heads = gathered(heads, CORE_SWAP)
         back_b = attention_step(attended_grad, cut, width - cut)
         dq, dk, dv, sums0 = (jnp.concatenate([a, b], axis=1) for a, b in zip(back_a, back_b))
         rights = [dq, dk, dv]
         other = grads("query_grad_a", where, [tokens], [0, 0, 0], rights)
-        (other, dq, dk, dv, sums0, x_f, y_f, xy_f, mine) = together(other, dq, dk, dv, sums0, x_f, y_f, xy_f, mine)
+        sums = jnp.stack([sums2, sums1, sums0])
+        (other, dq, dk, dv, sums, x_f, y_f, xy_f, mine, heads) = together(
+            other, dq, dk, dv, sums, x_f, y_f, xy_f, mine, heads
+        )
         rights = [dq, dk, dv]
         parts_i = plane(mine)
         other = swap(other, CORE_SWAP)
         totals_f = [wide(same_f[d], xy_f[d], from_x[d], from_y[d]) for d in range(2)]
         totals_f += [wide(same_f[2 + d], xy_f[2 + d], x_f[d], y_f[d]) for d in range(2)]
-        mine = grads("query_grad_b", where, [tokens], [0, 0, 0], rights, other, "place")
         odd_f = swap(low(jnp.stack([totals_f[1], totals_f[3]])), Z_SWAPS[1])
-        both = jnp.concatenate([jnp.stack([sums2, sums1, sums0]), head[None]])
-        (mine, odd_f, even_f, dq, dk, dv, both) = together(mine, odd_f, [totals_f[0], totals_f[2]], dq, dk, dv, both)
+        mine = grads("query_grad_b", where, [tokens], [0, 0, 0], rights, other)
+        (mine, odd_f, even_f, dq, dk, dv, sums, heads) = together(
+            mine, odd_f, [totals_f[0], totals_f[2]], dq, dk, dv, sums, heads
+        )
         go_f = swap(low(wide(even_f[1], odd_f[1])), Z_SWAPS[2])
-        both = doubled(both, Z_SWAPS[1])
+        sums = sums + swap(sums, Z_SWAPS[1])
         tokens_grad = tokens_back(residual_grad, dq, dk, dv, wq, wk, wv)
-        (parts_i, mine, go_f, stay_f, tokens_grad, both) = together(
-            parts_i, mine, go_f, wide(even_f[0], odd_f[0]), tokens_grad, both
+        (parts_i, mine, go_f, stay_f, tokens_grad, heads, sums) = together(
+            parts_i, mine, go_f, wide(even_f[0], odd_f[0]), tokens_grad, heads, sums
         )
         parts_q = plane(mine)
-        own_f = low(wide(stay_f, go_f))
         totals_i = sums_by_z(parts_i)
         odd_i = swap(low(jnp.stack([totals_i[1], totals_i[3]])), Z_SWAPS[1])
-        both = doubled(both, Z_SWAPS[2])
-        (odd_i, own_f, even_i, both) = together(odd_i, own_f, [totals_i[0], totals_i[2]], both)
+        own_f = low(wide(stay_f, go_f))
+        sums = sums + swap(sums, Z_SWAPS[2])
+        (odd_i, even_i, own_f, sums, heads) = together(odd_i, [totals_i[0], totals_i[2]], own_f, sums, heads)
         go_i = swap(low(wide(even_i[1], odd_i[1])), Z_SWAPS[2])
-        stay_i = wide(even_i[0], odd_i[0])
-        (parts_q, go_i, stay_i, own_f, both) = together(parts_q, go_i, stay_i, own_f, both)
+        sums = sums + swap(sums, X_SWAP)
+        (parts_q, go_i, stay_i, own_f, sums, heads) = together(
+            parts_q, go_i, wide(even_i[0], odd_i[0]), own_f, sums, heads
+        )
         totals_q = sums_by_z(parts_q)
         z_q = [swap(low(totals_q[d]), Z_SWAPS[d]) for d in (1, 2, 3)]
-        own_i = low(wide(stay_i, go_i))
-        both = doubled(both, X_SWAP)
-        (z_q, own_q, own_i, both, own_f) = together(z_q, totals_q[0], own_i, both, own_f)
-        def shared(own):
-            return [own, swap(own, CORE_SWAP), swap(own, X_SWAP), swap(own, X_CORE_SWAP)]
-
-        all_f = shared(own_f)
+        own = jnp.concatenate([own_f, low(wide(stay_i, go_i))])
+        across = swap(own, X_SWAP)
+        sums = sums + swap(sums, Y_SWAP)
+        (z_q, own_q, own, across, sums, heads) = together(z_q, totals_q[0], own, across, sums, heads)
+        sums = sums + swap(sums, CORE_SWAP)
+        core = swap(jnp.stack([own, across]), CORE_SWAP)
         own_q = low(wide(own_q, *z_q))
-        both = doubled(both, Y_SWAP)
-        (all_f, own_q, both, own_i) = together(all_f, own_q, both, own_i)
-        all_q, all_i = shared(own_q), shared(own_i)
-        both = doubled(both, CORE_SWAP)
-        (outer_grad,) = place_shards(where, all_f, [width])
-        inner_weight_grad, output_grad = place_shards(where, all_i, [ff, width])
-        query_grad, key_grad, value_grad = place_shards(where, all_q, [width] * 3)
-        sums, heads = both[:3], both[3:]
+        all_q = [own_q, swap(own_q, CORE_SWAP), swap(own_q, X_SWAP), swap(own_q, X_CORE_SWAP)]
+        outer_grad, output_grad, inner_weight_grad = place_shards(
+            where,
+            [own, core[0], across, core[1]],
+            [(0, deep, 1), (deep, parts, 1), (deep + parts, parts, ff // width)],
+        )
+        query_grad, key_grad, value_grad = place_shards(where, all_q, [(at * parts, parts, 1) for at in range(3)])
     else:
 
         def reduced(left, right):

time: 289 us -> 273 us (0.945)
  waiting for transfers between devices: 120 us -> 100 us
  starting transfers between devices: 59.2 us -> 64.4 us
    ppermute x63 -> x64, waiting for transfers between devices: 120 us -> 100 us  [swap(): return lax.ppermute(a, MESH_AXES, pairs)]
    ppermute x63 -> x64, starting transfers between devices: 59.2 us -> 64.4 us  [swap(): return lax.ppermute(a, MESH_AXES, pairs)]
    pallas_call x22 -> x21, Pallas kernels: 89.5 us -> 88.6 us  [call(): pl.pallas_call(kernel, name=name, out_shape=outs, grid_spec=pltpu.Prefetc...]
  transfers between devices with their start and end apart: 63 -> 64, of which waited for: 31 -> 27; matrix products, arithmetic and copies ran while one was open for 1% -> 3% of each run, Pallas kernels for 25% -> 25%
where the time goes in v3:
time: 273 us; the launch traced here: 270 us
  waiting for transfers between devices  100 us (37%)
  Pallas kernels  88.6 us (32%)
  starting transfers between devices  64.4 us (24%)
  local copies, waits for them, and re-layouts  7.71 us (3%)
  other arithmetic  5.56 us (2%)
    ppermute x64, waiting for transfers between devices, swap(): return lax.ppermute(a, MESH_AXES, pairs)  100 us
    pallas_call x21, Pallas kernels, call(): pl.pallas_call(kernel, name=name, out_shape=outs, grid_spec=pltpu.Prefetc...  88.6 us
    ppermute x64, starting transfers between devices, swap(): return lax.ppermute(a, MESH_AXES, pairs)  64.4 us
  transfers between devices with their start and end apart: 64, of which 27 were waited for; matrix products, arithmetic and copies ran while one was open for 3% of the time, Pallas kernels for 25%

profile of v3, /device:TPU:0, one launch (start us, length us, event | category | flops | bytes accessed | tf_op | source)
XLA Modules:
  0.0 270.4 jit_solution(3821977355767661502)
XLA Ops:
  4.7 5.1 %collective-permute-start.2 = (bf16[56,1152]{1,0:T(8,128)(2,1)S(1)}, bf16[56,1152]{1,0:T(8,128)(2,1)S(1)}, u32[]{:S(2)}, u32[]{:S(2)}) collective-permute-start(bf16[56,1152]{1,0:T(8,128)(2,1)S(1)} %get-tuple-element.231), channel_id=1, source_target_pairs={{0,6},{1,7},{2,4},{3,5},{4,2},{5,3},{6,0},{7,1},{8,14},{9,15},{10,... | collective-permute-start | bytes 387080 | tf_op jit(solution)/shard_map/ppermute | solution.py:683
  10.5 3.7 %collective-permute-done.2 = bf16[56,1152]{1,0:T(8,128)(2,1)S(1)} collective-permute-done((bf16[56,1152]{1,0:T(8,128)(2,1)S(1)}, bf16[56,1152]{1,0:T(8,128)(2,1)S(1)}, u32[]{:S(2)}, u32[]{:S(2)}) %collective-permute-start.2) | collective-permute-done | bytes 129056 | tf_op jit(solution)/shard_map/ppermute | solution.py:683
  14.2 6.5 %collective-permute-done.1 = bf16[56,1152]{1,0:T(8,128)(2,1)S(1)} collective-permute-done((bf16[56,1152]{1,0:T(8,128)(2,1)S(1)}, bf16[56,1152]{1,0:T(8,128)(2,1)S(1)}, u32[]{:S(2)}, u32[]{:S(2)}) %collective-permute-start.1) | collective-permute-done | bytes 129056 | tf_op jit(solution)/shard_map/ppermute | solution.py:683
  23.9 2.5 collective-permute-start.7
  28.3 5.0 %collective-permute-done.7 = bf16[48,1920]{1,0:T(8,128)(2,1)S(1)} collective-permute-done((bf16[48,1920]{1,0:T(8,128)(2,1)S(1)}, bf16[48,1920]{1,0:T(8,128)(2,1)S(1)}, u32[]{:S(2)}, u32[]{:S(2)}) %collective-permute-start.7) | collective-permute-done | bytes 184352 | tf_op jit(solution)/shard_map/ppermute | solution.py:683
  33.3 7.3 %collective-permute-done.6 = bf16[48,1920]{1,0:T(8,128)(2,1)S(1)} collective-permute-done((bf16[48,1920]{1,0:T(8,128)(2,1)S(1)}, bf16[48,1920]{1,0:T(8,128)(2,1)S(1)}, u32[]{:S(2)}, u32[]{:S(2)}) %collective-permute-start.6) | collective-permute-done | bytes 184352 | tf_op jit(solution)/shard_map/ppermute | solution.py:683
  44.9 7.8 %collective-permute-done.12 = bf16[240,384]{1,0:T(8,128)(2,1)S(1)} collective-permute-done((bf16[240,384]{1,0:T(8,128)(2,1)S(1)}, bf16[240,384]{1,0:T(8,128)(2,1)S(1)}, u32[]{:S(2)}, u32[]{:S(2)}) %collective-permute-start.12) | collective-permute-done | bytes 184352 | tf_op jit(solution)/shard_map/ppermute | solution.py:683
  52.7 3.5 %collective-permute-start.10 = (bf16[240,384]{1,0:T(8,128)(2,1)S(1)}, bf16[240,384]{1,0:T(8,128)(2,1)}, u32[]{:S(2)}, u32[]{:S(2)}) collective-permute-start(bf16[240,384]{1,0:T(8,128)(2,1)S(1)} %get-tuple-element.261), channel_id=1, source_target_pairs={{0,2},{1,3},{2,0},{3,1},{4,6},{5,7},{6,4},{7,5},{8,10},{9,11},{10,... | collective-permute-start | bytes 552968 | tf_op jit(solution)/shard_map/ppermute | solution.py:683
  56.6 3.5 %collective-permute-done.11 = bf16[240,384]{1,0:T(8,128)(2,1)} collective-permute-done((bf16[240,384]{1,0:T(8,128)(2,1)S(1)}, bf16[240,384]{1,0:T(8,128)(2,1)}, u32[]{:S(2)}, u32[]{:S(2)}) %collective-permute-start.11) | collective-permute-done | bytes 184352 | tf_op jit(solution)/shard_map/ppermute | solution.py:683
  69.3 3.1 %place_weights.3 = (bf16[4,2,2,48,768]{4,3,2,1,0:T(8,128)(2,1)S(1)}, bf16[4,2,2,48,768]{4,3,2,1,0:T(8,128)(2,1)S(1)}, bf16[4,2,2,48,768]{4,3,2,1,0:T(8,128)(2,1)S(1)}) custom-call(s32[4]{0:T(128)S(1)} %pad_add_fusion.where, bf16[4,56,1152]{2,1,0:T(8,128)(2,1)S(1)} %pad_maximum_fusion.4.refs_0_, bf16[4,56,1152]{2,1,0:T(8,128)(2,1)S(1)} %get-tuple-element.448.refs_1_, ...), custom_call_target="tpu_custom_call" | custom-call | bytes 516096 | tf_op jit(solution)/shard_map/place_weights/pallas_call | solution.py:46
  72.5 8.9 %attention.1 = (bf16[512,768]{1,0:T(8,128)(2,1)S(1)}, bf16[512,768]{1,0:T(8,128)(2,1)S(1)}, bf16[512,768]{1,0:T(8,128)(2,1)S(1)}, bf16[512,768]{1,0:T(8,128)(2,1)S(1)}, f32[3,8,512]{2,1,0:T(8,128)S(1)}) custom-call(bf16[512,768]{1,0:T(8,128)(2,1)S(1)} %bitcast.130, bf16[768,768]{1,0:T(8,128)(2,1)S(1)} %bitcast.137, bf16[768,768]{1,0:T(8,128)(2,1)S(1)} %bitcast.139, ...), custom_call_target="tpu_custom_call" | custom-call | flops 163577856 | bytes 417792 | tf_op jit(solution)/shard_map/attention/pallas_call | solution.py:46
  85.0 15.6 %collective-permute-done.21.refs_2_ = bf16[4,240,384]{2,1,0:T(8,128)(2,1)S(1)} collective-permute-done((bf16[4,240,384]{2,1,0:T(8,128)(2,1)S(1)}, bf16[4,240,384]{2,1,0:T(8,128)(2,1)S(1)}, u32[]{:S(2)}, u32[]{:S(2)}) %collective-permute-start.21) | collective-permute-done | bytes 737312 | tf_op jit(solution)/shard_map/ppermute | solution.py:683
  105.1 2.7 %place_weights.4 = (bf16[4,2,2,48,768]{4,3,2,1,0:T(8,128)(2,1)S(1)}, bf16[4,2,2,48,3072]{4,3,2,1,0:T(8,128)(2,1)S(1)}) custom-call(s32[4]{0:T(128)S(1)} %pad_add_fusion.where, bf16[4,48,1920]{2,1,0:T(8,128)(2,1)S(1)} %pad_maximum_fusion.1.refs_0_, bf16[4,48,1920]{2,1,0:T(8,128)(2,1)S(1)} %collective-permute-done.18.refs_1_, ...), custom_call_target="tpu_custom_call" | custom-call | bytes 737280 | tf_op jit(solution)/shard_map/place_weights/pallas_call | solution.py:46
  110.1 11.4 %inner.1 = (bf16[512,3072]{1,0:T(8,128)(2,1)S(1)}, bf16[512,3072]{1,0:T(8,128)(2,1)S(1)}) custom-call(bf16[512,768]{1,0:T(8,128)(2,1)S(1)} %get-tuple-element.282.low.refs_1_, bf16[768,3072]{1,0:T(8,128)(2,1)S(1)} %bitcast.126, f32[1,3072]{1,0:T(1,128)S(1)} %reshape.178.bi), custom_call_target="tpu_custom_call" | custom-call | flops 150994944 | bytes 688128 | tf_op jit(solution)/shard_map/inner/pallas_call | solution.py:46
  124.7 2.8 %place_weights.5 = (bf16[4,2,2,192,768]{4,3,2,1,0:T(8,128)(2,1)S(1)}, bf16[4,2,2,48,768]{4,3,2,1,0:T(8,128)(2,1)S(1)}) custom-call(s32[4]{0:T(128)S(1)} %pad_add_fusion.where, bf16[4,240,384]{2,1,0:T(8,128)(2,1)S(1)} %pad_maximum_fusion.2.refs_0_, bf16[4,240,384]{2,1,0:T(8,128)(2,1)S(1)} %collective-permute-done.23.refs_1_, ...), custom_call_target="tpu_custom_call" | custom-call | bytes 737280 | tf_op jit(solution)/shard_map/place_weights/pallas_call | solution.py:46
  127.6 7.8 %outer.1 = (bf16[512,768]{1,0:T(8,128)(2,1)}, f32[512,768]{1,0:T(8,128)S(1)}, bf16[512,768]{1,0:T(8,128)(2,1)S(1)}, f32[8,768]{1,0:T(8,128)S(1)}, f32[8,768]{1,0:T(8,128)S(1)}, /*index=5*/f32[8,128]{1,0:T(8,128)S(1)}) custom-call(s32[1]{0:T(128)S(6)} %copy.74.labels, f32[3]{0:T(128)S(1)} %convert_element_type.265.bias3, ...), custom_call_target="tpu_custom_call" | custom-call | flops 150994944 | bytes 835584 | tf_op jit(solution)/shard_map/outer/pallas_call | solution.py:46
  135.4 3.2 %outer_grad_a.1 = bf16[4,4,192,384]{3,2,1,0:T(8,128)(2,1)S(1)} custom-call(s32[4]{0:T(128)S(1)} %pad_add_fusion.where, bf16[512,3072]{1,0:T(8,128)(2,1)S(1)} %get-tuple-element.287.act.refs_0_, bf16[512,768]{1,0:T(8,128)(2,1)S(1)} %get-tuple-element.300.refs_1_.bg), custom_call_target="tpu_custom_call" | custom-call | flops 75497472 | bytes 344064 | tf_op jit(solution)/shard_map/outer_grad_a/pallas_call | solution.py:46
  138.8 4.1 %inner_grads.1.ig.refs_3_ = bf16[512,3072]{1,0:T(8,128)(2,1)S(1)} custom-call(bf16[512,768]{1,0:T(8,128)(2,1)S(1)} %get-tuple-element.300.refs_1_.bg, bf16[3072,768]{1,0:T(8,128)(2,1)S(1)} %bitcast.129, bf16[512,3072]{1,0:T(8,128)(2,1)S(1)} %get-tuple-element.302.slope), custom_call_target="tpu_custom_call" | custom-call | flops 150994944 | bytes 688128 | tf_op jit(solution)/shard_map/inner_grads/pallas_call | solution.py:46
  143.2 3.2 %outer_grad_b.1 = (bf16[4,192,384]{2,1,0:T(8,128)(2,1)S(1)}, bf16[4,192,384]{2,1,0:T(8,128)(2,1)S(1)}, bf16[4,192,384]{2,1,0:T(8,128)(2,1)S(1)}, bf16[4,192,384]{2,1,0:T(8,128)(2,1)S(1)}) custom-call(s32[4]{0:T(128)S(1)} %pad_add_fusion.where, bf16[512,3072]{1,0:T(8,128)(2,1)S(1)} %get-tuple-element.287.act.refs_0_, ...), custom_call_target="tpu_custom_call" | custom-call | flops 75497472 | bytes 344064 | tf_op jit(solution)/shard_map/outer_grad_b/pallas_call | solution.py:46
  151.8 6.0 %inner_back.1 = (f32[512,768]{1,0:T(8,128)S(1)}, bf16[512,768]{1,0:T(8,128)(2,1)S(1)}, f32[8,768]{1,0:T(8,128)S(1)}) custom-call(bf16[512,3072]{1,0:T(8,128)(2,1)S(1)} %inner_grads.1.ig.refs_3_, bf16[768,3072]{1,0:T(8,128)(2,1)S(1)} %bitcast.127, f32[512,768]{1,0:T(8,128)S(1)} %get-tuple-element.312.sg, f32[512,768]{1,0:T(8,128)S(1)} %get-tuple-element.296.n1, ...), custom_call_target="tpu_custom_call" | custom-call | flops 150994944 | bytes 884736 | tf_op jit(solution)/shard_map/inner_back/pallas_call | solution.py:46
  157.9 2.7 %inner_grad_a.1 = bf16[4,4,240,384]{3,2,1,0:T(8,128)(2,1)S(1)} custom-call(s32[4]{0:T(128)S(1)} %pad_add_fusion.where, bf16[512,768]{1,0:T(8,128)(2,1)S(1)} %get-tuple-element.273.ctx.refs_0_, bf16[512,768]{1,0:T(8,128)(2,1)S(1)} %get-tuple-element.282.low.refs_1_, bf16[512,768]{1,0:T(8,128)(2,1)S(1)} %get-tuple-element.340.refs_2_.ag, ...), custom_call_target="tpu_custom_call" | custom-call | flops 94371840 | bytes 233472 | tf_op jit(solution)/shard_map/inner_grad_a/pallas_call | solution.py:46
  165.7 7.9 %attention_back.2 = (bf16[512,512]{1,0:T(8,128)(2,1)S(1)}, bf16[512,512]{1,0:T(8,128)(2,1)S(1)}, bf16[512,512]{1,0:T(8,128)(2,1)S(1)}, f32[8,512]{1,0:T(8,128)S(1)}) custom-call(bf16[512,768]{1,0:T(8,128)(2,1)S(1)} %get-tuple-element.322.q, bf16[512,768]{1,0:T(8,128)(2,1)S(1)} %get-tuple-element.323.k, bf16[512,768]{1,0:T(8,128)(2,1)S(1)} %get-tuple-element.324.v, ...), custom_call_target="tpu_custom_call" | custom-call | flops 109051904 | bytes 311296 | tf_op jit(solution)/shard_map/attention_back/pallas_call | solution.py:46
  173.7 2.8 %inner_grad_b.1 = (bf16[4,240,384]{2,1,0:T(8,128)(2,1)S(1)}, bf16[4,240,384]{2,1,0:T(8,128)(2,1)S(1)}, bf16[4,240,384]{2,1,0:T(8,128)(2,1)S(1)}, bf16[4,240,384]{2,1,0:T(8,128)(2,1)S(1)}) custom-call(s32[4]{0:T(128)S(1)} %pad_add_fusion.where, bf16[512,768]{1,0:T(8,128)(2,1)S(1)} %get-tuple-element.273.ctx.refs_0_, ...), custom_call_target="tpu_custom_call" | custom-call | flops 94371840 | bytes 233472 | tf_op jit(solution)/shard_map/inner_grad_b/pallas_call | solution.py:46
  176.5 3.6 %attention_back.3 = (bf16[512,256]{1,0:T(8,128)(2,1)S(1)}, bf16[512,256]{1,0:T(8,128)(2,1)S(1)}, bf16[512,256]{1,0:T(8,128)(2,1)S(1)}, f32[8,256]{1,0:T(8,128)S(1)}) custom-call(bf16[512,768]{1,0:T(8,128)(2,1)S(1)} %get-tuple-element.322.q, bf16[512,768]{1,0:T(8,128)(2,1)S(1)} %get-tuple-element.323.k, bf16[512,768]{1,0:T(8,128)(2,1)S(1)} %get-tuple-element.324.v, ...), custom_call_target="tpu_custom_call" | custom-call | flops 54525952 | bytes 155648 | tf_op jit(solution)/shard_map/attention_back/pallas_call | solution.py:46
  182.7 3.2 %collective-permute-done.38 = bf16[4,192,384]{2,1,0:T(8,128)(2,1)S(1)} collective-permute-done((bf16[4,192,384]{2,1,0:T(8,128)(2,1)S(1)}, bf16[4,192,384]{2,1,0:T(8,128)(2,1)S(1)}, u32[]{:S(2)}, u32[]{:S(2)}) %collective-permute-start.38) | collective-permute-done | bytes 589856 | tf_op jit(solution)/shard_map/ppermute | solution.py:683
  193.8 4.6 %collective-permute-done.44 = bf16[2,192,384]{2,1,0:T(8,128)(2,1)S(1)} collective-permute-done((bf16[2,192,384]{2,1,0:T(8,128)(2,1)S(1)}, bf16[2,192,384]{2,1,0:T(8,128)(2,1)S(1)}, u32[]{:S(2)}, u32[]{:S(2)}) %collective-permute-start.44) | collective-permute-done | bytes 294944 | tf_op jit(solution)/shard_map/ppermute | solution.py:683
  201.1 6.1 %tokens_back.1 = f32[512,768]{1,0:T(8,128)} custom-call(f32[512,768]{1,0:T(8,128)S(1)} %get-tuple-element.385.res, bf16[512,768]{1,0:T(8,128)(2,1)S(1)} %constant_dynamic-update-slice_fusion.refs_1_.dq, bf16[512,768]{1,0:T(8,128)(2,1)S(1)} %constant_dynamic-update-slice_fusion.2.refs_2_.dk, ...), custom_call_target="tpu_custom_call" | custom-call | flops 113246208 | bytes 565248 | tf_op jit(solution)/shard_map/tokens_back/pallas_call | solution.py:46
  207.2 13.6 %collective-permute-done.41 = bf16[4,240,384]{2,1,0:T(8,128)(2,1)S(1)} collective-permute-done((bf16[4,240,384]{2,1,0:T(8,128)(2,1)S(1)}, bf16[4,240,384]{2,1,0:T(8,128)(2,1)S(1)}, u32[]{:S(2)}, u32[]{:S(2)}) %collective-permute-start.41) | collective-permute-done | bytes 737312 | tf_op jit(solution)/shard_map/ppermute | solution.py:683
  227.9 4.2 %collective-permute-done.51 = f32[3,8,768]{2,1,0:T(8,128)S(1)} collective-permute-done((f32[3,8,768]{2,1,0:T(8,128)S(1)}, f32[3,8,768]{2,1,0:T(8,128)S(1)}, u32[]{:S(2)}, u32[]{:S(2)}) %collective-permute-start.51) | collective-permute-done | bytes 73760 | tf_op jit(solution)/shard_map/ppermute | solution.py:683
  233.0 2.7 %collective-permute-start.52 = (bf16[240,384]{1,0:T(8,128)(2,1)S(1)}, bf16[240,384]{1,0:T(8,128)(2,1)S(1)}, u32[]{:S(2)}, u32[]{:S(2)}) collective-permute-start(bf16[240,384]{1,0:T(8,128)(2,1)S(1)} %get-tuple-element.461), channel_id=1, source_target_pairs={{0,4},{1,5},{2,6},{3,7},{4,0},{5,1},{6,2},{7,3},{8,12},{9,13},{10,... | collective-permute-start | bytes 552968 | tf_op jit(solution)/shard_map/ppermute | solution.py:683
  237.2 9.6 %collective-permute-done.53 = f32[3,8,768]{2,1,0:T(8,128)S(1)} collective-permute-done((f32[3,8,768]{2,1,0:T(8,128)S(1)}, f32[3,8,768]{2,1,0:T(8,128)S(1)}, u32[]{:S(2)}, u32[]{:S(2)}) %collective-permute-start.53) | collective-permute-done | bytes 73760 | tf_op jit(solution)/shard_map/ppermute | solution.py:683
  254.2 2.6 collective-permute-done.58
  (196 shorter events, 90.5 us)
Async XLA Ops:
  20.8 19.8 %collective-permute-start.4 = (bf16[4,56,1152]{2,1,0:T(8,128)(2,1)S(1)}, bf16[4,56,1152]{2,1,0:T(8,128)(2,1)S(1)}, u32[]{:S(2)}, u32[]{:S(2)}) collective-permute-start(bf16[4,56,1152]{2,1,0:T(8,128)(2,1)S(1)} %pad_maximum_fusion.4.refs_0_), channel_id=1, source_target_pairs={{0,1},{1,0},{2,3},{3,2},{4,5},{5,4},{6,7},{7,6},{8,9},{9,8},{10,11... | collective-permute-start | bytes 1548296 | tf_op jit(solution)/shard_map/ppermute | solution.py:683
  22.4 18.2 %collective-permute-start.3 = (bf16[4,56,1152]{2,1,0:T(8,128)(2,1)S(1)}, bf16[4,56,1152]{2,1,0:T(8,128)(2,1)S(1)}, u32[]{:S(2)}, u32[]{:S(2)}) collective-permute-start(bf16[4,56,1152]{2,1,0:T(8,128)(2,1)S(1)} %pad_maximum_fusion.4.refs_0_), channel_id=1, source_target_pairs={{0,16},{1,17},{2,18},{3,19},{4,20},{5,21},{6,22},{7,23},{8,24},{9,... | collective-permute-start | bytes 1548296 | tf_op jit(solution)/shard_map/ppermute | solution.py:683
  26.4 14.2 %collective-permute-start.6 = (bf16[48,1920]{1,0:T(8,128)(2,1)S(1)}, bf16[48,1920]{1,0:T(8,128)(2,1)S(1)}, u32[]{:S(2)}, u32[]{:S(2)}) collective-permute-start(bf16[48,1920]{1,0:T(8,128)(2,1)S(1)} %get-tuple-element.240), channel_id=1, source_target_pairs={{0,4},{1,5},{2,6},{3,7},{4,0},{5,1},{6,2},{7,3},{8,12},{9,13},{10,... | collective-permute-start | bytes 552968 | tf_op jit(solution)/shard_map/ppermute | solution.py:683
  26.4 14.2 %collective-permute-start.5 = (bf16[48,1920]{1,0:T(8,128)(2,1)S(1)}, bf16[48,1920]{1,0:T(8,128)(2,1)S(1)}, u32[]{:S(2)}, u32[]{:S(2)}) collective-permute-start(bf16[48,1920]{1,0:T(8,128)(2,1)S(1)} %get-tuple-element.240), channel_id=1, source_target_pairs={{0,2},{1,3},{2,0},{3,1},{4,6},{5,7},{6,4},{7,5},{8,10},{9,11},{10,... | collective-permute-start | bytes 552968 | tf_op jit(solution)/shard_map/ppermute | solution.py:683
  42.0 20.0 %collective-permute-start.13 = (bf16[12,56,1152]{2,1,0:T(8,128)(2,1)}, bf16[12,56,1152]{2,1,0:T(8,128)(2,1)}, u32[]{:S(2)}, u32[]{:S(2)}) collective-permute-start(bf16[12,56,1152]{2,1,0:T(8,128)(2,1)} %pad_maximum_fusion), channel_id=1, source_target_pairs={{0,8},{1,9},{2,10},{3,11},{4,12},{5,13},{6,14},{7,15},{8,0},{9,1},... | collective-permute-start | bytes 4644872 | tf_op jit(solution)/shard_map/ppermute | solution.py:683
  42.1 19.8 %collective-permute-start.9 = (bf16[4,48,1920]{2,1,0:T(8,128)(2,1)S(1)}, bf16[4,48,1920]{2,1,0:T(8,128)(2,1)S(1)}, u32[]{:S(2)}, u32[]{:S(2)}) collective-permute-start(bf16[4,48,1920]{2,1,0:T(8,128)(2,1)S(1)} %pad_maximum_fusion.1.refs_0_), channel_id=1, source_target_pairs={{0,16},{1,17},{2,18},{3,19},{4,20},{5,21},{6,22},{7,23},{8,24},{9,... | collective-permute-start | bytes 2211848 | tf_op jit(solution)/shard_map/ppermute | solution.py:683
  42.7 19.2 %collective-permute-start.8 = (bf16[4,56,1152]{2,1,0:T(8,128)(2,1)S(1)}, bf16[4,56,1152]{2,1,0:T(8,128)(2,1)}, u32[]{:S(2)}, u32[]{:S(2)}) collective-permute-start(bf16[4,56,1152]{2,1,0:T(8,128)(2,1)S(1)} %collective-permute-done.3.refs_4_), channel_id=1, source_target_pairs={{0,1},{1,0},{2,3},{3,2},{4,5},{5,4},{6,7},{7,6},{8,9},{9,8},{10,11... | collective-permute-start | bytes 1548296 | tf_op jit(solution)/shard_map/ppermute | solution.py:683
  44.9 15.2 %collective-permute-start.11 = (bf16[240,384]{1,0:T(8,128)(2,1)S(1)}, bf16[240,384]{1,0:T(8,128)(2,1)}, u32[]{:S(2)}, u32[]{:S(2)}) collective-permute-start(bf16[240,384]{1,0:T(8,128)(2,1)S(1)} %get-tuple-element.261), channel_id=1, source_target_pairs={{0,4},{1,5},{2,6},{3,7},{4,0},{5,1},{6,2},{7,3},{8,12},{9,13},{10,... | collective-permute-start | bytes 552968 | tf_op jit(solution)/shard_map/ppermute | solution.py:683
  63.9 17.5 %collective-permute-start.16 = (bf16[4,240,384]{2,1,0:T(8,128)(2,1)S(1)}, bf16[4,240,384]{2,1,0:T(8,128)(2,1)}, u32[]{:S(2)}, u32[]{:S(2)}) collective-permute-start(bf16[4,240,384]{2,1,0:T(8,128)(2,1)S(1)} %pad_maximum_fusion.2.refs_0_), channel_id=1, source_target_pairs={{0,16},{1,17},{2,18},{3,19},{4,20},{5,21},{6,22},{7,23},{8,24},{9,... | collective-permute-start | bytes 2211848 | tf_op jit(solution)/shard_map/ppermute | solution.py:683
  65.5 16.3 %collective-permute-start.15 = (bf16[4,48,1920]{2,1,0:T(8,128)(2,1)S(1)}, bf16[4,48,1920]{2,1,0:T(8,128)(2,1)}, u32[]{:S(2)}, u32[]{:S(2)}) collective-permute-start(bf16[4,48,1920]{2,1,0:T(8,128)(2,1)S(1)} %pad_maximum_fusion.1.refs_0_), channel_id=1, source_target_pairs={{0,1},{1,0},{2,3},{3,2},{4,5},{5,4},{6,7},{7,6},{8,9},{9,8},{10,11... | collective-permute-start | bytes 2211848 | tf_op jit(solution)/shard_map/ppermute | solution.py:683
  82.3 18.4 %collective-permute-start.21 = (bf16[4,240,384]{2,1,0:T(8,128)(2,1)S(1)}, bf16[4,240,384]{2,1,0:T(8,128)(2,1)S(1)}, u32[]{:S(2)}, u32[]{:S(2)}) collective-permute-start(bf16[4,240,384]{2,1,0:T(8,128)(2,1)S(1)} %pad_maximum_fusion.2.refs_0_), channel_id=1, source_target_pairs={{0,1},{1,0},{2,3},{3,2},{4,5},{5,4},{6,7},{7,6},{8,9},{9,8},{10,11... | collective-permute-start | bytes 2211848 | tf_op jit(solution)/shard_map/ppermute | solution.py:683
  83.8 16.9 %collective-permute-start.19 = (bf16[4,48,1920]{2,1,0:T(8,128)(2,1)}, bf16[4,48,1920]{2,1,0:T(8,128)(2,1)S(1)}, u32[]{:S(2)}, u32[]{:S(2)}) collective-permute-start(bf16[4,48,1920]{2,1,0:T(8,128)(2,1)} %collective-permute-done.15.refs_2_), channel_id=1, source_target_pairs={{0,8},{1,9},{2,10},{3,11},{4,12},{5,13},{6,14},{7,15},{8,0},{9,1},... | collective-permute-start | bytes 2211848 | tf_op jit(solution)/shard_map/ppermute | solution.py:683
  83.8 19.1 %collective-permute-start.17 = (bf16[4,48,1920]{2,1,0:T(8,128)(2,1)}, bf16[4,48,1920]{2,1,0:T(8,128)(2,1)S(1)}, u32[]{:S(2)}, u32[]{:S(2)}) collective-permute-start(bf16[4,48,1920]{2,1,0:T(8,128)(2,1)} %collective-permute-done.15.refs_2_), channel_id=1, source_target_pairs={{0,16},{1,17},{2,18},{3,19},{4,20},{5,21},{6,22},{7,23},{8,24},{9,... | collective-permute-start | bytes 2211848 | tf_op jit(solution)/shard_map/ppermute | solution.py:683
  102.9 18.6 %collective-permute-start.23 = (bf16[4,240,384]{2,1,0:T(8,128)(2,1)S(1)}, bf16[4,240,384]{2,1,0:T(8,128)(2,1)S(1)}, u32[]{:S(2)}, u32[]{:S(2)}) collective-permute-start(bf16[4,240,384]{2,1,0:T(8,128)(2,1)S(1)} %pad_maximum_fusion.2.refs_0_), channel_id=1, source_target_pairs={{0,8},{1,9},{2,10},{3,11},{4,12},{5,13},{6,14},{7,15},{8,0},{9,1},... | collective-permute-start | bytes 2211848 | tf_op jit(solution)/shard_map/ppermute | solution.py:683
  103.4 18.1 %collective-permute-start.24 = (bf16[4,240,384]{2,1,0:T(8,128)(2,1)S(1)}, bf16[4,240,384]{2,1,0:T(8,128)(2,1)S(1)}, u32[]{:S(2)}, u32[]{:S(2)}) collective-permute-start(bf16[4,240,384]{2,1,0:T(8,128)(2,1)S(1)} %collective-permute-done.21.refs_2_), channel_id=1, source_target_pairs={{0,8},{1,9},{2,10},{3,11},{4,12},{5,13},{6,14},{7,15},{8,0},{9,1},... | collective-permute-start | bytes 2211848 | tf_op jit(solution)/shard_map/ppermute | solution.py:683
  103.4 18.1 %collective-permute-start.25 = (bf16[4,240,384]{2,1,0:T(8,128)(2,1)}, bf16[4,240,384]{2,1,0:T(8,128)(2,1)S(1)}, u32[]{:S(2)}, u32[]{:S(2)}) collective-permute-start(bf16[4,240,384]{2,1,0:T(8,128)(2,1)} %collective-permute-done.16.refs_4_), channel_id=1, source_target_pairs={{0,8},{1,9},{2,10},{3,11},{4,12},{5,13},{6,14},{7,15},{8,0},{9,1},... | collective-permute-start | bytes 2211848 | tf_op jit(solution)/shard_map/ppermute | solution.py:683
  103.9 18.6 %collective-permute-start.22 = (bf16[4,240,384]{2,1,0:T(8,128)(2,1)}, bf16[4,240,384]{2,1,0:T(8,128)(2,1)S(1)}, u32[]{:S(2)}, u32[]{:S(2)}) collective-permute-start(bf16[4,240,384]{2,1,0:T(8,128)(2,1)} %collective-permute-done.16.refs_4_), channel_id=1, source_target_pairs={{0,1},{1,0},{2,3},{3,2},{4,5},{5,4},{6,7},{7,6},{8,9},{9,8},{10,11... | collective-permute-start | bytes 2211848 | tf_op jit(solution)/shard_map/ppermute | solution.py:683
  148.4 12.3 %collective-permute-start.30 = (bf16[2,192,384]{2,1,0:T(8,128)(2,1)S(1)}, bf16[2,192,384]{2,1,0:T(8,128)(2,1)S(1)}, u32[]{:S(2)}, u32[]{:S(2)}) collective-permute-start(bf16[2,192,384]{2,1,0:T(8,128)(2,1)S(1)} %get-tuple-element.456), channel_id=1, source_target_pairs={{0,16},{1,17},{2,18},{3,19},{4,20},{5,21},{6,22},{7,23},{8,24},{9,... | collective-permute-start | bytes 884744 | tf_op jit(solution)/shard_map/ppermute | solution.py:683
  149.0 11.7 %collective-permute-start.31 = (bf16[2,192,384]{2,1,0:T(8,128)(2,1)S(1)}, bf16[2,192,384]{2,1,0:T(8,128)(2,1)S(1)}, u32[]{:S(2)}, u32[]{:S(2)}) collective-permute-start(bf16[2,192,384]{2,1,0:T(8,128)(2,1)S(1)} %get-tuple-element.454), channel_id=1, source_target_pairs={{0,1},{1,0},{2,3},{3,2},{4,5},{5,4},{6,7},{7,6},{8,9},{9,8},{10,11... | collective-permute-start | bytes 884744 | tf_op jit(solution)/shard_map/ppermute | solution.py:683
  160.7 13.1 %collective-permute-start.34 = (bf16[4,4,240,384]{3,2,1,0:T(8,128)(2,1)S(1)}, bf16[4,4,240,384]{3,2,1,0:T(8,128)(2,1)S(1)}, u32[]{:S(2)}, u32[]{:S(2)}) collective-permute-start(bf16[4,4,240,384]{3,2,1,0:T(8,128)(2,1)S(1)} %inner_grad_a.1), channel_id=1, source_target_pairs={{0,8},{1,9},{2,10},{3,11},{4,12},{5,13},{6,14},{7,15},{8,0},{9,1},... | collective-permute-start | bytes 8847368 | tf_op jit(solution)/shard_map/ppermute | solution.py:683
  160.7 12.9 %collective-permute-start.35 = (bf16[8,8,768]{2,1,0:T(8,128)(2,1)S(1)}, bf16[8,8,768]{2,1,0:T(8,128)(2,1)S(1)}, u32[]{:S(2)}, u32[]{:S(2)}) collective-permute-start(bf16[8,8,768]{2,1,0:T(8,128)(2,1)S(1)} %pad_maximum_fusion.10), channel_id=1, source_target_pairs={{0,16},{1,17},{2,18},{3,19},{4,20},{5,21},{6,22},{7,23},{8,24},{9,... | collective-permute-start | bytes 294920 | tf_op jit(solution)/shard_map/ppermute | solution.py:683
  162.2 20.4 %collective-permute-start.36 = (bf16[2,192,384]{2,1,0:T(8,128)(2,1)S(1)}, bf16[2,192,384]{2,1,0:T(8,128)(2,1)S(1)}, u32[]{:S(2)}, u32[]{:S(2)}) collective-permute-start(bf16[2,192,384]{2,1,0:T(8,128)(2,1)S(1)} %get-tuple-element.350), channel_id=1, source_target_pairs={{0,16},{1,17},{2,18},{3,19},{4,20},{5,21},{6,22},{7,23},{8,24},{9,... | collective-permute-start | bytes 884744 | tf_op jit(solution)/shard_map/ppermute | solution.py:683
  162.8 19.9 %collective-permute-start.37 = (bf16[2,192,384]{2,1,0:T(8,128)(2,1)S(1)}, bf16[2,192,384]{2,1,0:T(8,128)(2,1)S(1)}, u32[]{:S(2)}, u32[]{:S(2)}) collective-permute-start(bf16[2,192,384]{2,1,0:T(8,128)(2,1)S(1)} %get-tuple-element.351), channel_id=1, source_target_pairs={{0,1},{1,0},{2,3},{3,2},{4,5},{5,4},{6,7},{7,6},{8,9},{9,8},{10,11... | collective-permute-start | bytes 884744 | tf_op jit(solution)/shard_map/ppermute | solution.py:683
  164.3 21.5 %collective-permute-start.38 = (bf16[4,192,384]{2,1,0:T(8,128)(2,1)S(1)}, bf16[4,192,384]{2,1,0:T(8,128)(2,1)S(1)}, u32[]{:S(2)}, u32[]{:S(2)}) collective-permute-start(bf16[4,192,384]{2,1,0:T(8,128)(2,1)S(1)} %get-tuple-element.352), channel_id=1, source_target_pairs={{0,17},{1,16},{2,19},{3,18},{4,21},{5,20},{6,23},{7,22},{8,25},{9,... | collective-permute-start | bytes 1769480 | tf_op jit(solution)/shard_map/ppermute | solution.py:683
  185.9 21.4 %collective-permute-start.40 = (bf16[4,240,384]{2,1,0:T(8,128)(2,1)S(1)}, bf16[4,240,384]{2,1,0:T(8,128)(2,1)S(1)}, u32[]{:S(2)}, u32[]{:S(2)}) collective-permute-start(bf16[4,240,384]{2,1,0:T(8,128)(2,1)S(1)} %get-tuple-element.359), channel_id=1, source_target_pairs={{0,16},{1,17},{2,18},{3,19},{4,20},{5,21},{6,22},{7,23},{8,24},{9,... | collective-permute-start | bytes 2211848 | tf_op jit(solution)/shard_map/ppermute | solution.py:683
  186.4 34.4 %collective-permute-start.41 = (bf16[4,240,384]{2,1,0:T(8,128)(2,1)S(1)}, bf16[4,240,384]{2,1,0:T(8,128)(2,1)S(1)}, u32[]{:S(2)}, u32[]{:S(2)}) collective-permute-start(bf16[4,240,384]{2,1,0:T(8,128)(2,1)S(1)} %get-tuple-element.360), channel_id=1, source_target_pairs={{0,1},{1,0},{2,3},{3,2},{4,5},{5,4},{6,7},{7,6},{8,9},{9,8},{10,11... | collective-permute-start | bytes 2211848 | tf_op jit(solution)/shard_map/ppermute | solution.py:683
  187.8 33.0 %collective-permute-start.42 = (bf16[4,240,384]{2,1,0:T(8,128)(2,1)S(1)}, bf16[4,240,384]{2,1,0:T(8,128)(2,1)S(1)}, u32[]{:S(2)}, u32[]{:S(2)}) collective-permute-start(bf16[4,240,384]{2,1,0:T(8,128)(2,1)S(1)} %get-tuple-element.361), channel_id=1, source_target_pairs={{0,17},{1,16},{2,19},{3,18},{4,21},{5,20},{6,23},{7,22},{8,25},{9,... | collective-permute-start | bytes 2211848 | tf_op jit(solution)/shard_map/ppermute | solution.py:683
  198.5 22.4 %collective-permute-start.45 = (bf16[192,384]{1,0:T(8,128)(2,1)S(1)}, bf16[192,384]{1,0:T(8,128)(2,1)S(1)}, u32[]{:S(2)}, u32[]{:S(2)}) collective-permute-start(bf16[192,384]{1,0:T(8,128)(2,1)S(1)} %get-tuple-element.463), channel_id=1, source_target_pairs={{0,4},{1,5},{2,6},{3,7},{4,0},{5,1},{6,2},{7,3},{8,12},{9,13},{10,... | collective-permute-start | bytes 442376 | tf_op jit(solution)/shard_map/ppermute | solution.py:683
  224.4 22.4 %collective-permute-start.47 = (bf16[4,144,384]{2,1,0:T(8,128)(2,1)S(1)}, bf16[4,144,384]{2,1,0:T(8,128)(2,1)S(1)}, u32[]{:S(2)}, u32[]{:S(2)}) collective-permute-start(bf16[4,144,384]{2,1,0:T(8,128)(2,1)S(1)} %get-tuple-element.394), channel_id=1, source_target_pairs={{0,16},{1,17},{2,18},{3,19},{4,20},{5,21},{6,22},{7,23},{8,24},{9,... | collective-permute-start | bytes 1327112 | tf_op jit(solution)/shard_map/ppermute | solution.py:683
  225.5 21.3 %collective-permute-start.48 = (bf16[4,144,384]{2,1,0:T(8,128)(2,1)S(1)}, bf16[4,144,384]{2,1,0:T(8,128)(2,1)S(1)}, u32[]{:S(2)}, u32[]{:S(2)}) collective-permute-start(bf16[4,144,384]{2,1,0:T(8,128)(2,1)S(1)} %get-tuple-element.395), channel_id=1, source_target_pairs={{0,1},{1,0},{2,3},{3,2},{4,5},{5,4},{6,7},{7,6},{8,9},{9,8},{10,11... | collective-permute-start | bytes 1327112 | tf_op jit(solution)/shard_map/ppermute | solution.py:683
  226.7 20.1 %collective-permute-start.49 = (bf16[4,144,384]{2,1,0:T(8,128)(2,1)S(1)}, bf16[4,144,384]{2,1,0:T(8,128)(2,1)S(1)}, u32[]{:S(2)}, u32[]{:S(2)}) collective-permute-start(bf16[4,144,384]{2,1,0:T(8,128)(2,1)S(1)} %get-tuple-element.396), channel_id=1, source_target_pairs={{0,17},{1,16},{2,19},{3,18},{4,21},{5,20},{6,23},{7,22},{8,25},{9,... | collective-permute-start | bytes 1327112 | tf_op jit(solution)/shard_map/ppermute | solution.py:683
  233.0 13.8 %collective-permute-start.52 = (bf16[240,384]{1,0:T(8,128)(2,1)S(1)}, bf16[240,384]{1,0:T(8,128)(2,1)S(1)}, u32[]{:S(2)}, u32[]{:S(2)}) collective-permute-start(bf16[240,384]{1,0:T(8,128)(2,1)S(1)} %get-tuple-element.461), channel_id=1, source_target_pairs={{0,4},{1,5},{2,6},{3,7},{4,0},{5,1},{6,2},{7,3},{8,12},{9,13},{10,... | collective-permute-start | bytes 552968 | tf_op jit(solution)/shard_map/ppermute | solution.py:683
  (38 other events, 276.6 us)

commit v4 on v3

--- a/solution.py
+++ b/solution.py
@@ -159,29 +159,28 @@
 
 
 ERFC_POLY = (
-    0.2820605933666229,
-    0.28293782472610474,
-    0.237934872508049,
-    0.22901807725429535,
-    -0.10879392176866531,
-    0.44148358702659607,
-    -0.6950507164001465,
-    0.44817423820495605,
-    -0.13161660730838776,
-    0.013852047733962536,
+    0.14103029668331146,
+    0.14146891236305237,
+    0.1189674362540245,
+    0.11450903862714767,
+    -0.05439696088433266,
+    0.22074179351329803,
+    -0.34752535820007324,
+    0.22408711910247803,
+    -0.06580830365419388,
+    0.006926023866981268,
 )
 
 
 def gelu_parts(v):
-    u = jnp.abs(v) * (0.5**0.5)
-    t = 1.0 / (1.0 + 0.5 * u)
-    poly = jnp.full_like(t, ERFC_POLY[-1])
-    for coefficient in ERFC_POLY[-2::-1]:
+    t = 1.0 / (1.0 + (0.5 * 0.5**0.5) * jnp.abs(v))
+    poly = ERFC_POLY[-1] * t + ERFC_POLY[-2]
+    for coefficient in ERFC_POLY[-3::-1]:
         poly = poly * t + coefficient
-    bell = jnp.exp(v * v * -0.5)
-    tail = (0.5 * t) * poly * bell
+    bell = jnp.exp2(v * v * (-0.5 * math.log2(math.e)))
+    tail = t * poly * bell
     below = jnp.where(v < 0, tail, 1.0 - tail)
-    return v * below, below + v * (bell * 0.3989422804014327)
+    return v * below, below + v * (bell * (2 * math.pi) ** -0.5)
 
 
 def inner_kernel(low, wi, bi, act_o, slope_o):
@@ -291,7 +290,7 @@
 def outer(act, w, n1, table, out_grad, wp, labels, bias3):
     seq, width = n1.shape
     ff = act.shape[1]
-    blk = 512
+    blk = 1536
     whole = full((seq, width))
     return call(
         outer_kernel,
@@ -329,7 +328,7 @@
 def inner_grads(bg, w_out, slope):
     seq, width = bg.shape
     ff = slope.shape[1]
-    blk = 512
+    blk = 1024
     cols = pl.BlockSpec((seq, blk), lambda i: (0, i))
     return call(
         inner_grad_kernel,
@@ -388,7 +387,7 @@
 def inner_back(ig, w_in, sg, n1, r1, table):
     seq, width = n1.shape
     ff = ig.shape[1]
-    blk = 512
+    blk = 1536
     whole = full((seq, width))
     return call(
         inner_back_kernel,
@@ -598,10 +597,10 @@
     )
 
 
-def weights_kernel(spans, where, *refs):
-    pieces, outs, sem = refs[:8], refs[8:-1], refs[-1]
+def weights_kernel(spans, places, where, *refs):
+    pieces, outs, sem = refs[: len(places)], refs[-1 - len(spans) : -1], refs[-1]
     copies = []
-    for place in range(8):
+    for place, piece in zip(places, pieces):
         hh = jnp.bitwise_xor(where[0], place // 4)
         yy = jnp.bitwise_xor(where[1], place // 2 % 2)
         cc = jnp.bitwise_xor(where[3], place % 2)
@@ -609,7 +608,7 @@
             zz = jnp.bitwise_xor(where[2], dz)
             for (top, rows, left, width), out in zip(spans, outs):
                 to = out.at[zz, yy, hh, :, pl.ds(pl.multiple_of(cc * width, 128), width)]
-                come = pieces[place].at[dz, top : top + rows, left : left + width]
+                come = piece.at[dz, top : top + rows, left : left + width]
                 copies.append(pltpu.make_async_copy(come, to, sem.at[len(copies)]))
     for one in copies:
         one.start()
@@ -617,20 +616,33 @@
         one.wait()
 
 
+def place_some(where, pieces, spans, places, begun=()):
+    anywhere = pl.BlockSpec(memory_space=pl.ANY)
+    count = 1 + len(pieces)
+    return pl.pallas_call(
+        functools.partial(weights_kernel, tuple(spans), tuple(places)),
+        name="place_weights",
+        out_shape=tuple(shape(4, 2, 2, rows, 2 * width) for _, rows, _, width in spans),
+        grid_spec=pltpu.PrefetchScalarGridSpec(
+            num_scalar_prefetch=1,
+            grid=(1,),
+            in_specs=[anywhere] * (len(pieces) + len(begun)),
+            out_specs=(anywhere,) * len(spans),
+            scratch_shapes=[pltpu.SemaphoreType.DMA((4 * len(places) * len(spans),))],
+        ),
+        input_output_aliases={count + at: at for at in range(len(begun))},
+        compiler_params=pltpu.CompilerParams(vmem_limit_bytes=4 * MIB),
+        cost_estimate=pl.CostEstimate(flops=0, bytes_accessed=pieces[0].size, transcendentals=0),
+    )(where, *pieces, *begun)
+
+
 def place_weights(where, pieces, spans):
-    anywhere = pl.BlockSpec(memory_space=pl.ANY)
-    outs = call(
-        functools.partial(weights_kernel, tuple(spans)),
-        tuple(shape(4, 2, 2, rows, 2 * width) for _, rows, _, width in spans),
-        [anywhere] * 8,
-        (anywhere,) * len(spans),
-        (where, *(pltpu.with_memory_space_constraint(p, pltpu.VMEM) for p in pieces)),
-        scratch=[pltpu.SemaphoreType.DMA((32 * len(spans),))],
-        prefetch=1,
-        moved=4 * 8 * pieces[0].size,
-        vmem=4,
-        name="place_weights",
-    )
+    begun = place_some(where, pieces[:6], spans, range(6))
+    return finish_weights(where, begun, pieces[6:], spans)
+
+
+def finish_weights(where, begun, pieces, spans):
+    outs = place_some(where, pieces, spans, (6, 7), begun)
     return [o.reshape(16 * rows, 2 * width) for o, (_, rows, _, width) in zip(outs, spans)]
 
 
@@ -819,20 +831,17 @@
         xy_b = swap(y_b, X_SWAP)
         y_c = swap(far_c, Y_SWAP)
         core_b = to_core([far_b, y_b, x_b])
-        (far_b, y_b, x_b, xy_b, core_b, far_c, x_c, y_c) = together(
-            far_b, y_b, x_b, xy_b, core_b, far_c, x_c, y_c
-        )
+        begun_b = place_some(where, mixed((far_b, y_b, x_b), core_b), spans_b, range(6))
+        (xy_b, begun_b, far_c, x_c, y_c) = together(xy_b, begun_b, far_c, x_c, y_c)
         xy_c = swap(x_c, Y_SWAP)
-        core_b += to_core([xy_b])
+        (core_xy_b,) = to_core([xy_b])
         core_c = to_core([far_c, y_c, x_c])
-        wo, wi = place_weights(where, mixed((far_b, y_b, x_b, xy_b), core_b), spans_b)
+        wo, wi = finish_weights(where, begun_b, [xy_b, core_xy_b], spans_b)
         n1, r1, first_low = attended(context, wo, tokens, table)
         activated, slope = inner(first_low, wi, inner_row)
-        (far_c, y_c, x_c, xy_c, core_c, activated, slope) = together(
-            far_c, y_c, x_c, xy_c, core_c, activated, slope
-        )
-        core_c += to_core([xy_c])
-        wf, wp = place_weights(where, mixed((far_c, y_c, x_c, xy_c), core_c), spans_c)
+        begun_c = place_some(where, mixed((far_c, y_c, x_c), core_c), spans_c, range(6))
+        (xy_c, begun_c, activated, slope) = together(xy_c, begun_c, activated, slope)
+        wf, wp = finish_weights(where, begun_c, [xy_c, *to_core([xy_c])], spans_c)
     else:
         wq, wk, wv, wo, wp, wi, wf = (
             lax.all_gather(w, "fsdp", axis=0, tiled=True)
@@ -877,14 +886,14 @@
         mine = grads("outer_grad_b", where, [activated], [0], [branch_grad], other)
         (mine, inner_grad, heads) = together(mine, inner_grad, heads)
         same_f, y_f, x_f, xy_f = mine
-        from_x, from_y = swap(x_f[:2], X_SWAP), swap(y_f[:2], Y_SWAP)
+        from_x, from_y = swap(x_f[:3], X_SWAP), swap(y_f[:3], Y_SWAP)
         heads = gathered(gathered(heads, Z_SWAPS[2]), Y_SWAP)
         residual_grad, attended_grad, sums1 = inner_back(inner_grad, wi, second_grad, n1, r1, table)
         (attended_grad, inner_grad) = together(attended_grad, inner_grad)
         lefts, rights = [context, first_low], [attended_grad, inner_grad]
         other = grads("inner_grad_a", where, lefts, [0, 1], rights)
         (other, attended_grad, from_x, from_y, x_f, y_f, xy_f, heads) = together(
-            other, attended_grad, from_x, from_y, x_f[2:], y_f[2:], xy_f, heads
+            other, attended_grad, from_x, from_y, x_f[3], y_f[3], xy_f, heads
         )
         other = swap(other, CORE_SWAP)
         x_f, y_f, xy_f = swap(x_f, X_SWAP), swap(y_f, Y_SWAP), swap(xy_f, XY_SWAP)
@@ -905,8 +914,8 @@
         rights = [dq, dk, dv]
         parts_i = plane(mine)
         other = swap(other, CORE_SWAP)
-        totals_f = [wide(same_f[d], xy_f[d], from_x[d], from_y[d]) for d in range(2)]
-        totals_f += [wide(same_f[2 + d], xy_f[2 + d], x_f[d], y_f[d]) for d in range(2)]
+        totals_f = [wide(same_f[d], xy_f[d], from_x[d], from_y[d]) for d in range(3)]
+        totals_f.append(wide(same_f[3], xy_f[3], x_f, y_f))
         odd_f = swap(low(jnp.stack([totals_f[1], totals_f[3]])), Z_SWAPS[1])
         mine = grads("query_grad_b", where, [tokens], [0, 0, 0], rights, other)
         (mine, odd_f, even_f, dq, dk, dv, sums, heads) = together(

time: 273 us -> 268 us (0.982)
  starting transfers between devices: 64.4 us -> 61.3 us
    pallas_call x21 -> x18, Pallas kernels: 88.6 us -> 77.1 us  [call(): pl.pallas_call(kernel, name=name, out_shape=outs, grid_spec=pltpu.Prefetc...]
    pallas_call x0 -> x6, Pallas kernels: none -> 11 us  [place_some(): pl.pallas_call(functools.partial(weights_kernel, tuple(spans), tuple(plac...]
    ppermute x64, starting transfers between devices: 64.4 us -> 61.3 us  [swap(): return lax.ppermute(a, MESH_AXES, pairs)]
  transfers between devices with their start and end apart: 64 -> 64, of which waited for: 27 -> 29; matrix products, arithmetic and copies ran while one was open for 3% -> 3% of each run, Pallas kernels for 25% -> 26%
where the time goes in v4:
time: 268 us; the launch traced here: 265 us
  waiting for transfers between devices  98 us (37%)
  Pallas kernels  88.1 us (33%)
  starting transfers between devices  61.3 us (23%)
  local copies, waits for them, and re-layouts  7.71 us (3%)
  other arithmetic  5.57 us (2%)
    ppermute x64, waiting for transfers between devices, swap(): return lax.ppermute(a, MESH_AXES, pairs)  98 us
    pallas_call x18, Pallas kernels, call(): pl.pallas_call(kernel, name=name, out_shape=outs, grid_spec=pltpu.Prefetc...  77.1 us
    ppermute x64, starting transfers between devices, swap(): return lax.ppermute(a, MESH_AXES, pairs)  61.3 us
    pallas_call x6, Pallas kernels, place_some(): pl.pallas_call(functools.partial(weights_kernel, tuple(spans), tuple(plac...  11 us
  transfers between devices with their start and end apart: 64, of which 29 were waited for; matrix products, arithmetic and copies ran while one was open for 3% of the time, Pallas kernels for 26%

profile of v4, /device:TPU:0, one launch (start us, length us, event | category | flops | bytes accessed | tf_op | source)
XLA Modules:
  0.0 264.6 jit_solution(264596328072045249)
XLA Ops:
  4.7 5.1 %collective-permute-start.2 = (bf16[56,1152]{1,0:T(8,128)(2,1)S(1)}, bf16[56,1152]{1,0:T(8,128)(2,1)S(1)}, u32[]{:S(2)}, u32[]{:S(2)}) collective-permute-start(bf16[56,1152]{1,0:T(8,128)(2,1)S(1)} %get-tuple-element.230), channel_id=1, source_target_pairs={{0,6},{1,7},{2,4},{3,5},{4,2},{5,3},{6,0},{7,1},{8,14},{9,15},{10,... | collective-permute-start | bytes 387080 | tf_op jit(solution)/shard_map/ppermute | solution.py:695
  10.5 3.7 %collective-permute-done.2 = bf16[56,1152]{1,0:T(8,128)(2,1)S(1)} collective-permute-done((bf16[56,1152]{1,0:T(8,128)(2,1)S(1)}, bf16[56,1152]{1,0:T(8,128)(2,1)S(1)}, u32[]{:S(2)}, u32[]{:S(2)}) %collective-permute-start.2) | collective-permute-done | bytes 129056 | tf_op jit(solution)/shard_map/ppermute | solution.py:695
  14.2 6.5 %collective-permute-done.1 = bf16[56,1152]{1,0:T(8,128)(2,1)S(1)} collective-permute-done((bf16[56,1152]{1,0:T(8,128)(2,1)S(1)}, bf16[56,1152]{1,0:T(8,128)(2,1)S(1)}, u32[]{:S(2)}, u32[]{:S(2)}) %collective-permute-start.1) | collective-permute-done | bytes 129056 | tf_op jit(solution)/shard_map/ppermute | solution.py:695
  23.9 2.5 collective-permute-start.7
  28.3 5.0 %collective-permute-done.7 = bf16[48,1920]{1,0:T(8,128)(2,1)S(1)} collective-permute-done((bf16[48,1920]{1,0:T(8,128)(2,1)S(1)}, bf16[48,1920]{1,0:T(8,128)(2,1)S(1)}, u32[]{:S(2)}, u32[]{:S(2)}) %collective-permute-start.7) | collective-permute-done | bytes 184352 | tf_op jit(solution)/shard_map/ppermute | solution.py:695
  33.3 7.3 %collective-permute-done.6 = bf16[48,1920]{1,0:T(8,128)(2,1)S(1)} collective-permute-done((bf16[48,1920]{1,0:T(8,128)(2,1)S(1)}, bf16[48,1920]{1,0:T(8,128)(2,1)S(1)}, u32[]{:S(2)}, u32[]{:S(2)}) %collective-permute-start.6) | collective-permute-done | bytes 184352 | tf_op jit(solution)/shard_map/ppermute | solution.py:695
  44.9 7.8 %collective-permute-done.12 = bf16[240,384]{1,0:T(8,128)(2,1)S(1)} collective-permute-done((bf16[240,384]{1,0:T(8,128)(2,1)S(1)}, bf16[240,384]{1,0:T(8,128)(2,1)S(1)}, u32[]{:S(2)}, u32[]{:S(2)}) %collective-permute-start.12) | collective-permute-done | bytes 184352 | tf_op jit(solution)/shard_map/ppermute | solution.py:695
  52.7 3.5 %collective-permute-start.10 = (bf16[240,384]{1,0:T(8,128)(2,1)S(1)}, bf16[240,384]{1,0:T(8,128)(2,1)}, u32[]{:S(2)}, u32[]{:S(2)}) collective-permute-start(bf16[240,384]{1,0:T(8,128)(2,1)S(1)} %get-tuple-element.263), channel_id=1, source_target_pairs={{0,2},{1,3},{2,0},{3,1},{4,6},{5,7},{6,4},{7,5},{8,10},{9,11},{10,... | collective-permute-start | bytes 552968 | tf_op jit(solution)/shard_map/ppermute | solution.py:695
  56.6 3.5 %collective-permute-done.11 = bf16[240,384]{1,0:T(8,128)(2,1)} collective-permute-done((bf16[240,384]{1,0:T(8,128)(2,1)S(1)}, bf16[240,384]{1,0:T(8,128)(2,1)}, u32[]{:S(2)}, u32[]{:S(2)}) %collective-permute-start.11) | collective-permute-done | bytes 184352 | tf_op jit(solution)/shard_map/ppermute | solution.py:695
  72.6 8.8 %attention.1 = (bf16[512,768]{1,0:T(8,128)(2,1)S(1)}, bf16[512,768]{1,0:T(8,128)(2,1)S(1)}, bf16[512,768]{1,0:T(8,128)(2,1)S(1)}, bf16[512,768]{1,0:T(8,128)(2,1)S(1)}, f32[3,8,512]{2,1,0:T(8,128)S(1)}) custom-call(bf16[512,768]{1,0:T(8,128)(2,1)S(1)} %bitcast.147, bf16[768,768]{1,0:T(8,128)(2,1)S(1)} %bitcast.151, bf16[768,768]{1,0:T(8,128)(2,1)S(1)} %bitcast.153, ...), custom_call_target="tpu_custom_call" | custom-call | flops 163577856 | bytes 417792 | tf_op jit(solution)/shard_map/attention/pallas_call | solution.py:46
  86.3 2.6 place_weights.8
  88.9 12.3 %collective-permute-done.21.refs_2_ = bf16[4,240,384]{2,1,0:T(8,128)(2,1)S(1)} collective-permute-done((bf16[4,240,384]{2,1,0:T(8,128)(2,1)S(1)}, bf16[4,240,384]{2,1,0:T(8,128)(2,1)S(1)}, u32[]{:S(2)}, u32[]{:S(2)}) %collective-permute-start.21) | collective-permute-done | bytes 737312 | tf_op jit(solution)/shard_map/ppermute | solution.py:695
  108.0 2.6 place_weights.9
  110.6 2.2 attended.1
  112.9 10.8 %inner.1 = (bf16[512,3072]{1,0:T(8,128)(2,1)S(1)}, bf16[512,3072]{1,0:T(8,128)(2,1)S(1)}) custom-call(bf16[512,768]{1,0:T(8,128)(2,1)S(1)} %get-tuple-element.284.low.refs_1_, bf16[768,3072]{1,0:T(8,128)(2,1)S(1)} %bitcast.140, f32[1,3072]{1,0:T(1,128)S(1)} %reshape.181.bi), custom_call_target="tpu_custom_call" | custom-call | flops 150994944 | bytes 688128 | tf_op jit(solution)/shard_map/inner/pallas_call | solution.py:46
  126.9 7.1 %outer.1 = (bf16[512,768]{1,0:T(8,128)(2,1)}, f32[512,768]{1,0:T(8,128)S(1)}, bf16[512,768]{1,0:T(8,128)(2,1)S(1)}, f32[8,768]{1,0:T(8,128)S(1)}, f32[8,768]{1,0:T(8,128)S(1)}, /*index=5*/f32[8,128]{1,0:T(8,128)S(1)}) custom-call(s32[1]{0:T(128)S(6)} %copy.88.labels, f32[3]{0:T(128)S(1)} %convert_element_type.263.bias3, ...), custom_call_target="tpu_custom_call" | custom-call | flops 150994944 | bytes 835584 | tf_op jit(solution)/shard_map/outer/pallas_call | solution.py:46
  134.0 3.2 %outer_grad_a.1 = bf16[4,4,192,384]{3,2,1,0:T(8,128)(2,1)S(1)} custom-call(s32[4]{0:T(128)S(1)} %pad_add_fusion.where, bf16[512,3072]{1,0:T(8,128)(2,1)S(1)} %get-tuple-element.289.act.refs_0_, bf16[512,768]{1,0:T(8,128)(2,1)S(1)} %get-tuple-element.298.refs_1_.bg), custom_call_target="tpu_custom_call" | custom-call | flops 75497472 | bytes 344064 | tf_op jit(solution)/shard_map/outer_grad_a/pallas_call | solution.py:46
  137.4 3.5 %inner_grads.1.ig.refs_3_ = bf16[512,3072]{1,0:T(8,128)(2,1)S(1)} custom-call(bf16[512,768]{1,0:T(8,128)(2,1)S(1)} %get-tuple-element.298.refs_1_.bg, bf16[3072,768]{1,0:T(8,128)(2,1)S(1)} %bitcast.143, bf16[512,3072]{1,0:T(8,128)(2,1)S(1)} %get-tuple-element.300.slope), custom_call_target="tpu_custom_call" | custom-call | flops 150994944 | bytes 688128 | tf_op jit(solution)/shard_map/inner_grads/pallas_call | solution.py:46
  141.8 3.2 %outer_grad_b.1 = (bf16[4,192,384]{2,1,0:T(8,128)(2,1)S(1)}, bf16[4,192,384]{2,1,0:T(8,128)(2,1)S(1)}, bf16[4,192,384]{2,1,0:T(8,128)(2,1)S(1)}, bf16[4,192,384]{2,1,0:T(8,128)(2,1)S(1)}) custom-call(s32[4]{0:T(128)S(1)} %pad_add_fusion.where, bf16[512,3072]{1,0:T(8,128)(2,1)S(1)} %get-tuple-element.289.act.refs_0_, ...), custom_call_target="tpu_custom_call" | custom-call | flops 75497472 | bytes 344064 | tf_op jit(solution)/shard_map/outer_grad_b/pallas_call | solution.py:46
  150.4 5.3 %inner_back.1 = (f32[512,768]{1,0:T(8,128)S(1)}, bf16[512,768]{1,0:T(8,128)(2,1)S(1)}, f32[8,768]{1,0:T(8,128)S(1)}) custom-call(bf16[512,3072]{1,0:T(8,128)(2,1)S(1)} %inner_grads.1.ig.refs_3_, bf16[768,3072]{1,0:T(8,128)(2,1)S(1)} %bitcast.141, f32[512,768]{1,0:T(8,128)S(1)} %get-tuple-element.310.sg, f32[512,768]{1,0:T(8,128)S(1)} %get-tuple-element.294.n1, ...), custom_call_target="tpu_custom_call" | custom-call | flops 150994944 | bytes 884736 | tf_op jit(solution)/shard_map/inner_back/pallas_call | solution.py:46
  155.6 2.8 %inner_grad_a.1 = bf16[4,4,240,384]{3,2,1,0:T(8,128)(2,1)S(1)} custom-call(s32[4]{0:T(128)S(1)} %pad_add_fusion.where, bf16[512,768]{1,0:T(8,128)(2,1)S(1)} %get-tuple-element.279.ctx.refs_0_, bf16[512,768]{1,0:T(8,128)(2,1)S(1)} %get-tuple-element.284.low.refs_1_, bf16[512,768]{1,0:T(8,128)(2,1)S(1)} %get-tuple-element.338.refs_2_.ag, ...), custom_call_target="tpu_custom_call" | custom-call | flops 94371840 | bytes 233472 | tf_op jit(solution)/shard_map/inner_grad_a/pallas_call | solution.py:46
  163.6 7.9 %attention_back.2 = (bf16[512,512]{1,0:T(8,128)(2,1)S(1)}, bf16[512,512]{1,0:T(8,128)(2,1)S(1)}, bf16[512,512]{1,0:T(8,128)(2,1)S(1)}, f32[8,512]{1,0:T(8,128)S(1)}) custom-call(bf16[512,768]{1,0:T(8,128)(2,1)S(1)} %get-tuple-element.320.q, bf16[512,768]{1,0:T(8,128)(2,1)S(1)} %get-tuple-element.321.k, bf16[512,768]{1,0:T(8,128)(2,1)S(1)} %get-tuple-element.322.v, ...), custom_call_target="tpu_custom_call" | custom-call | flops 109051904 | bytes 311296 | tf_op jit(solution)/shard_map/attention_back/pallas_call | solution.py:46
  171.5 2.8 %inner_grad_b.1 = (bf16[4,240,384]{2,1,0:T(8,128)(2,1)S(1)}, bf16[4,240,384]{2,1,0:T(8,128)(2,1)S(1)}, bf16[4,240,384]{2,1,0:T(8,128)(2,1)S(1)}, bf16[4,240,384]{2,1,0:T(8,128)(2,1)S(1)}) custom-call(s32[4]{0:T(128)S(1)} %pad_add_fusion.where, bf16[512,768]{1,0:T(8,128)(2,1)S(1)} %get-tuple-element.279.ctx.refs_0_, ...), custom_call_target="tpu_custom_call" | custom-call | flops 94371840 | bytes 233472 | tf_op jit(solution)/shard_map/inner_grad_b/pallas_call | solution.py:46
  174.3 3.6 %attention_back.3 = (bf16[512,256]{1,0:T(8,128)(2,1)S(1)}, bf16[512,256]{1,0:T(8,128)(2,1)S(1)}, bf16[512,256]{1,0:T(8,128)(2,1)S(1)}, f32[8,256]{1,0:T(8,128)S(1)}) custom-call(bf16[512,768]{1,0:T(8,128)(2,1)S(1)} %get-tuple-element.320.q, bf16[512,768]{1,0:T(8,128)(2,1)S(1)} %get-tuple-element.321.k, bf16[512,768]{1,0:T(8,128)(2,1)S(1)} %get-tuple-element.322.v, ...), custom_call_target="tpu_custom_call" | custom-call | flops 54525952 | bytes 155648 | tf_op jit(solution)/shard_map/attention_back/pallas_call | solution.py:46
  186.1 2.2 query_grad_b.1
  188.3 5.3 %collective-permute-done.44 = bf16[2,192,384]{2,1,0:T(8,128)(2,1)S(1)} collective-permute-done((bf16[2,192,384]{2,1,0:T(8,128)(2,1)S(1)}, bf16[2,192,384]{2,1,0:T(8,128)(2,1)S(1)}, u32[]{:S(2)}, u32[]{:S(2)}) %collective-permute-start.44) | collective-permute-done | bytes 294944 | tf_op jit(solution)/shard_map/ppermute | solution.py:695
  196.2 6.1 %tokens_back.1 = f32[512,768]{1,0:T(8,128)} custom-call(f32[512,768]{1,0:T(8,128)S(1)} %get-tuple-element.383.res, bf16[512,768]{1,0:T(8,128)(2,1)S(1)} %constant_dynamic-update-slice_fusion.refs_1_.dq, bf16[512,768]{1,0:T(8,128)(2,1)S(1)} %constant_dynamic-update-slice_fusion.2.refs_2_.dk, ...), custom_call_target="tpu_custom_call" | custom-call | flops 113246208 | bytes 565248 | tf_op jit(solution)/shard_map/tokens_back/pallas_call | solution.py:46
  202.3 14.2 %collective-permute-done.41 = bf16[4,240,384]{2,1,0:T(8,128)(2,1)S(1)} collective-permute-done((bf16[4,240,384]{2,1,0:T(8,128)(2,1)S(1)}, bf16[4,240,384]{2,1,0:T(8,128)(2,1)S(1)}, u32[]{:S(2)}, u32[]{:S(2)}) %collective-permute-start.41) | collective-permute-done | bytes 737312 | tf_op jit(solution)/shard_map/ppermute | solution.py:695
  223.5 3.0 %collective-permute-done.51 = f32[3,8,768]{2,1,0:T(8,128)S(1)} collective-permute-done((f32[3,8,768]{2,1,0:T(8,128)S(1)}, f32[3,8,768]{2,1,0:T(8,128)S(1)}, u32[]{:S(2)}, u32[]{:S(2)}) %collective-permute-start.51) | collective-permute-done | bytes 73760 | tf_op jit(solution)/shard_map/ppermute | solution.py:695
  231.5 10.1 %collective-permute-done.53 = f32[3,8,768]{2,1,0:T(8,128)S(1)} collective-permute-done((f32[3,8,768]{2,1,0:T(8,128)S(1)}, f32[3,8,768]{2,1,0:T(8,128)S(1)}, u32[]{:S(2)}, u32[]{:S(2)}) %collective-permute-start.53) | collective-permute-done | bytes 73760 | tf_op jit(solution)/shard_map/ppermute | solution.py:695
  249.0 2.4 collective-permute-done.58
  262.2 2.3 place_shards.3
  (202 shorter events, 93.2 us)
Async XLA Ops:
  9.8 10.9 %collective-permute-start.1 = (bf16[56,1152]{1,0:T(8,128)(2,1)S(1)}, bf16[56,1152]{1,0:T(8,128)(2,1)S(1)}, u32[]{:S(2)}, u32[]{:S(2)}) collective-permute-start(bf16[56,1152]{1,0:T(8,128)(2,1)S(1)} %get-tuple-element.230), channel_id=1, source_target_pairs={{0,4},{1,5},{2,6},{3,7},{4,0},{5,1},{6,2},{7,3},{8,12},{9,13},{10,... | collective-permute-start | bytes 387080 | tf_op jit(solution)/shard_map/ppermute | solution.py:695
  9.8 10.9 %collective-permute-start = (bf16[56,1152]{1,0:T(8,128)(2,1)S(1)}, bf16[56,1152]{1,0:T(8,128)(2,1)S(1)}, u32[]{:S(2)}, u32[]{:S(2)}) collective-permute-start(bf16[56,1152]{1,0:T(8,128)(2,1)S(1)} %get-tuple-element.230), channel_id=1, source_target_pairs={{0,2},{1,3},{2,0},{3,1},{4,6},{5,7},{6,4},{7,5},{8,10},{9,11},{10,... | collective-permute-start | bytes 387080 | tf_op jit(solution)/shard_map/ppermute | solution.py:695
  20.8 19.8 %collective-permute-start.4 = (bf16[4,56,1152]{2,1,0:T(8,128)(2,1)S(1)}, bf16[4,56,1152]{2,1,0:T(8,128)(2,1)S(1)}, u32[]{:S(2)}, u32[]{:S(2)}) collective-permute-start(bf16[4,56,1152]{2,1,0:T(8,128)(2,1)S(1)} %pad_maximum_fusion.4.refs_0_), channel_id=1, source_target_pairs={{0,1},{1,0},{2,3},{3,2},{4,5},{5,4},{6,7},{7,6},{8,9},{9,8},{10,11... | collective-permute-start | bytes 1548296 | tf_op jit(solution)/shard_map/ppermute | solution.py:695
  22.4 18.2 %collective-permute-start.3 = (bf16[4,56,1152]{2,1,0:T(8,128)(2,1)S(1)}, bf16[4,56,1152]{2,1,0:T(8,128)(2,1)S(1)}, u32[]{:S(2)}, u32[]{:S(2)}) collective-permute-start(bf16[4,56,1152]{2,1,0:T(8,128)(2,1)S(1)} %pad_maximum_fusion.4.refs_0_), channel_id=1, source_target_pairs={{0,16},{1,17},{2,18},{3,19},{4,20},{5,21},{6,22},{7,23},{8,24},{9,... | collective-permute-start | bytes 1548296 | tf_op jit(solution)/shard_map/ppermute | solution.py:695
  26.4 14.2 %collective-permute-start.6 = (bf16[48,1920]{1,0:T(8,128)(2,1)S(1)}, bf16[48,1920]{1,0:T(8,128)(2,1)S(1)}, u32[]{:S(2)}, u32[]{:S(2)}) collective-permute-start(bf16[48,1920]{1,0:T(8,128)(2,1)S(1)} %get-tuple-element.239), channel_id=1, source_target_pairs={{0,4},{1,5},{2,6},{3,7},{4,0},{5,1},{6,2},{7,3},{8,12},{9,13},{10,... | collective-permute-start | bytes 552968 | tf_op jit(solution)/shard_map/ppermute | solution.py:695
  26.4 14.2 %collective-permute-start.5 = (bf16[48,1920]{1,0:T(8,128)(2,1)S(1)}, bf16[48,1920]{1,0:T(8,128)(2,1)S(1)}, u32[]{:S(2)}, u32[]{:S(2)}) collective-permute-start(bf16[48,1920]{1,0:T(8,128)(2,1)S(1)} %get-tuple-element.239), channel_id=1, source_target_pairs={{0,2},{1,3},{2,0},{3,1},{4,6},{5,7},{6,4},{7,5},{8,10},{9,11},{10,... | collective-permute-start | bytes 552968 | tf_op jit(solution)/shard_map/ppermute | solution.py:695
  42.0 20.0 %collective-permute-start.13 = (bf16[12,56,1152]{2,1,0:T(8,128)(2,1)}, bf16[12,56,1152]{2,1,0:T(8,128)(2,1)}, u32[]{:S(2)}, u32[]{:S(2)}) collective-permute-start(bf16[12,56,1152]{2,1,0:T(8,128)(2,1)} %pad_maximum_fusion), channel_id=1, source_target_pairs={{0,8},{1,9},{2,10},{3,11},{4,12},{5,13},{6,14},{7,15},{8,0},{9,1},... | collective-permute-start | bytes 4644872 | tf_op jit(solution)/shard_map/ppermute | solution.py:695
  42.1 19.8 %collective-permute-start.9 = (bf16[4,48,1920]{2,1,0:T(8,128)(2,1)S(1)}, bf16[4,48,1920]{2,1,0:T(8,128)(2,1)S(1)}, u32[]{:S(2)}, u32[]{:S(2)}) collective-permute-start(bf16[4,48,1920]{2,1,0:T(8,128)(2,1)S(1)} %pad_maximum_fusion.1.refs_0_), channel_id=1, source_target_pairs={{0,16},{1,17},{2,18},{3,19},{4,20},{5,21},{6,22},{7,23},{8,24},{9,... | collective-permute-start | bytes 2211848 | tf_op jit(solution)/shard_map/ppermute | solution.py:695
  42.7 19.2 %collective-permute-start.8 = (bf16[4,56,1152]{2,1,0:T(8,128)(2,1)S(1)}, bf16[4,56,1152]{2,1,0:T(8,128)(2,1)}, u32[]{:S(2)}, u32[]{:S(2)}) collective-permute-start(bf16[4,56,1152]{2,1,0:T(8,128)(2,1)S(1)} %collective-permute-done.3.refs_4_), channel_id=1, source_target_pairs={{0,1},{1,0},{2,3},{3,2},{4,5},{5,4},{6,7},{7,6},{8,9},{9,8},{10,11... | collective-permute-start | bytes 1548296 | tf_op jit(solution)/shard_map/ppermute | solution.py:695
  44.9 15.2 %collective-permute-start.11 = (bf16[240,384]{1,0:T(8,128)(2,1)S(1)}, bf16[240,384]{1,0:T(8,128)(2,1)}, u32[]{:S(2)}, u32[]{:S(2)}) collective-permute-start(bf16[240,384]{1,0:T(8,128)(2,1)S(1)} %get-tuple-element.263), channel_id=1, source_target_pairs={{0,4},{1,5},{2,6},{3,7},{4,0},{5,1},{6,2},{7,3},{8,12},{9,13},{10,... | collective-permute-start | bytes 552968 | tf_op jit(solution)/shard_map/ppermute | solution.py:695
  63.9 17.5 %collective-permute-start.16 = (bf16[4,240,384]{2,1,0:T(8,128)(2,1)S(1)}, bf16[4,240,384]{2,1,0:T(8,128)(2,1)}, u32[]{:S(2)}, u32[]{:S(2)}) collective-permute-start(bf16[4,240,384]{2,1,0:T(8,128)(2,1)S(1)} %pad_maximum_fusion.2.refs_0_), channel_id=1, source_target_pairs={{0,16},{1,17},{2,18},{3,19},{4,20},{5,21},{6,22},{7,23},{8,24},{9,... | collective-permute-start | bytes 2211848 | tf_op jit(solution)/shard_map/ppermute | solution.py:695
  65.5 16.3 %collective-permute-start.15 = (bf16[4,48,1920]{2,1,0:T(8,128)(2,1)S(1)}, bf16[4,48,1920]{2,1,0:T(8,128)(2,1)}, u32[]{:S(2)}, u32[]{:S(2)}) collective-permute-start(bf16[4,48,1920]{2,1,0:T(8,128)(2,1)S(1)} %pad_maximum_fusion.1.refs_0_), channel_id=1, source_target_pairs={{0,1},{1,0},{2,3},{3,2},{4,5},{5,4},{6,7},{7,6},{8,9},{9,8},{10,11... | collective-permute-start | bytes 2211848 | tf_op jit(solution)/shard_map/ppermute | solution.py:695
  82.5 18.6 %collective-permute-start.21 = (bf16[4,240,384]{2,1,0:T(8,128)(2,1)S(1)}, bf16[4,240,384]{2,1,0:T(8,128)(2,1)S(1)}, u32[]{:S(2)}, u32[]{:S(2)}) collective-permute-start(bf16[4,240,384]{2,1,0:T(8,128)(2,1)S(1)} %pad_maximum_fusion.2.refs_0_), channel_id=1, source_target_pairs={{0,1},{1,0},{2,3},{3,2},{4,5},{5,4},{6,7},{7,6},{8,9},{9,8},{10,11... | collective-permute-start | bytes 2211848 | tf_op jit(solution)/shard_map/ppermute | solution.py:695
  83.8 18.8 %collective-permute-start.17 = (bf16[4,48,1920]{2,1,0:T(8,128)(2,1)}, bf16[4,48,1920]{2,1,0:T(8,128)(2,1)S(1)}, u32[]{:S(2)}, u32[]{:S(2)}) collective-permute-start(bf16[4,48,1920]{2,1,0:T(8,128)(2,1)} %collective-permute-done.15.refs_2_), channel_id=1, source_target_pairs={{0,16},{1,17},{2,18},{3,19},{4,20},{5,21},{6,22},{7,23},{8,24},{9,... | collective-permute-start | bytes 2211848 | tf_op jit(solution)/shard_map/ppermute | solution.py:695
  103.6 20.1 %collective-permute-start.22 = (bf16[4,240,384]{2,1,0:T(8,128)(2,1)}, bf16[4,240,384]{2,1,0:T(8,128)(2,1)S(1)}, u32[]{:S(2)}, u32[]{:S(2)}) collective-permute-start(bf16[4,240,384]{2,1,0:T(8,128)(2,1)} %collective-permute-done.16.refs_4_), channel_id=1, source_target_pairs={{0,1},{1,0},{2,3},{3,2},{4,5},{5,4},{6,7},{7,6},{8,9},{9,8},{10,11... | collective-permute-start | bytes 2211848 | tf_op jit(solution)/shard_map/ppermute | solution.py:695
  146.4 13.0 %collective-permute-start.31 = (bf16[3,192,384]{2,1,0:T(8,128)(2,1)S(1)}, bf16[3,192,384]{2,1,0:T(8,128)(2,1)S(1)}, u32[]{:S(2)}, u32[]{:S(2)}) collective-permute-start(bf16[3,192,384]{2,1,0:T(8,128)(2,1)S(1)} %slice.243), channel_id=1, source_target_pairs={{0,1},{1,0},{2,3},{3,2},{4,5},{5,4},{6,7},{7,6},{8,9},{9,8},{10,11... | collective-permute-start | bytes 1327112 | tf_op jit(solution)/shard_map/ppermute | solution.py:695
  147.6 11.8 %collective-permute-start.30 = (bf16[3,192,384]{2,1,0:T(8,128)(2,1)S(1)}, bf16[3,192,384]{2,1,0:T(8,128)(2,1)S(1)}, u32[]{:S(2)}, u32[]{:S(2)}) collective-permute-start(bf16[3,192,384]{2,1,0:T(8,128)(2,1)S(1)} %slice.242), channel_id=1, source_target_pairs={{0,16},{1,17},{2,18},{3,19},{4,20},{5,21},{6,22},{7,23},{8,24},{9,... | collective-permute-start | bytes 1327112 | tf_op jit(solution)/shard_map/ppermute | solution.py:695
  159.4 12.1 %collective-permute-start.34 = (bf16[4,4,240,384]{3,2,1,0:T(8,128)(2,1)S(1)}, bf16[4,4,240,384]{3,2,1,0:T(8,128)(2,1)S(1)}, u32[]{:S(2)}, u32[]{:S(2)}) collective-permute-start(bf16[4,4,240,384]{3,2,1,0:T(8,128)(2,1)S(1)} %inner_grad_a.1), channel_id=1, source_target_pairs={{0,8},{1,9},{2,10},{3,11},{4,12},{5,13},{6,14},{7,15},{8,0},{9,1},... | collective-permute-start | bytes 8847368 | tf_op jit(solution)/shard_map/ppermute | solution.py:695
  159.5 12.0 %collective-permute-start.35 = (bf16[8,8,768]{2,1,0:T(8,128)(2,1)S(1)}, bf16[8,8,768]{2,1,0:T(8,128)(2,1)S(1)}, u32[]{:S(2)}, u32[]{:S(2)}) collective-permute-start(bf16[8,8,768]{2,1,0:T(8,128)(2,1)S(1)} %pad_maximum_fusion.10), channel_id=1, source_target_pairs={{0,16},{1,17},{2,18},{3,19},{4,20},{5,21},{6,22},{7,23},{8,24},{9,... | collective-permute-start | bytes 294920 | tf_op jit(solution)/shard_map/ppermute | solution.py:695
  160.1 20.4 %collective-permute-start.36 = (bf16[192,384]{1,0:T(8,128)(2,1)S(1)}, bf16[192,384]{1,0:T(8,128)(2,1)S(1)}, u32[]{:S(2)}, u32[]{:S(2)}) collective-permute-start(bf16[192,384]{1,0:T(8,128)(2,1)S(1)} %get-tuple-element.348), channel_id=1, source_target_pairs={{0,16},{1,17},{2,18},{3,19},{4,20},{5,21},{6,22},{7,23},{8,24},{9,... | collective-permute-start | bytes 442376 | tf_op jit(solution)/shard_map/ppermute | solution.py:695
  161.6 18.9 %collective-permute-start.37 = (bf16[192,384]{1,0:T(8,128)(2,1)S(1)}, bf16[192,384]{1,0:T(8,128)(2,1)S(1)}, u32[]{:S(2)}, u32[]{:S(2)}) collective-permute-start(bf16[192,384]{1,0:T(8,128)(2,1)S(1)} %get-tuple-element.349), channel_id=1, source_target_pairs={{0,1},{1,0},{2,3},{3,2},{4,5},{5,4},{6,7},{7,6},{8,9},{9,8},{10,11... | collective-permute-start | bytes 442376 | tf_op jit(solution)/shard_map/ppermute | solution.py:695
  162.8 18.4 %collective-permute-start.38 = (bf16[4,192,384]{2,1,0:T(8,128)(2,1)S(1)}, bf16[4,192,384]{2,1,0:T(8,128)(2,1)S(1)}, u32[]{:S(2)}, u32[]{:S(2)}) collective-permute-start(bf16[4,192,384]{2,1,0:T(8,128)(2,1)S(1)} %get-tuple-element.350), channel_id=1, source_target_pairs={{0,17},{1,16},{2,19},{3,18},{4,21},{5,20},{6,23},{7,22},{8,25},{9,... | collective-permute-start | bytes 1769480 | tf_op jit(solution)/shard_map/ppermute | solution.py:695
  181.1 21.2 %collective-permute-start.40 = (bf16[4,240,384]{2,1,0:T(8,128)(2,1)S(1)}, bf16[4,240,384]{2,1,0:T(8,128)(2,1)S(1)}, u32[]{:S(2)}, u32[]{:S(2)}) collective-permute-start(bf16[4,240,384]{2,1,0:T(8,128)(2,1)S(1)} %get-tuple-element.357), channel_id=1, source_target_pairs={{0,16},{1,17},{2,18},{3,19},{4,20},{5,21},{6,22},{7,23},{8,24},{9,... | collective-permute-start | bytes 2211848 | tf_op jit(solution)/shard_map/ppermute | solution.py:695
  182.6 34.0 %collective-permute-start.41 = (bf16[4,240,384]{2,1,0:T(8,128)(2,1)S(1)}, bf16[4,240,384]{2,1,0:T(8,128)(2,1)S(1)}, u32[]{:S(2)}, u32[]{:S(2)}) collective-permute-start(bf16[4,240,384]{2,1,0:T(8,128)(2,1)S(1)} %get-tuple-element.358), channel_id=1, source_target_pairs={{0,1},{1,0},{2,3},{3,2},{4,5},{5,4},{6,7},{7,6},{8,9},{9,8},{10,11... | collective-permute-start | bytes 2211848 | tf_op jit(solution)/shard_map/ppermute | solution.py:695
  183.7 32.8 %collective-permute-start.42 = (bf16[4,240,384]{2,1,0:T(8,128)(2,1)S(1)}, bf16[4,240,384]{2,1,0:T(8,128)(2,1)S(1)}, u32[]{:S(2)}, u32[]{:S(2)}) collective-permute-start(bf16[4,240,384]{2,1,0:T(8,128)(2,1)S(1)} %get-tuple-element.359), channel_id=1, source_target_pairs={{0,17},{1,16},{2,19},{3,18},{4,21},{5,20},{6,23},{7,22},{8,25},{9,... | collective-permute-start | bytes 2211848 | tf_op jit(solution)/shard_map/ppermute | solution.py:695
  193.7 22.9 %collective-permute-start.45 = (bf16[192,384]{1,0:T(8,128)(2,1)S(1)}, bf16[192,384]{1,0:T(8,128)(2,1)S(1)}, u32[]{:S(2)}, u32[]{:S(2)}) collective-permute-start(bf16[192,384]{1,0:T(8,128)(2,1)S(1)} %get-tuple-element.454), channel_id=1, source_target_pairs={{0,4},{1,5},{2,6},{3,7},{4,0},{5,1},{6,2},{7,3},{8,12},{9,13},{10,... | collective-permute-start | bytes 442376 | tf_op jit(solution)/shard_map/ppermute | solution.py:695
  217.0 11.1 %collective-permute-start.50 = (bf16[2,240,384]{2,1,0:T(8,128)(2,1)S(1)}, bf16[2,240,384]{2,1,0:T(8,128)(2,1)S(1)}, u32[]{:S(2)}, u32[]{:S(2)}) collective-permute-start(bf16[2,240,384]{2,1,0:T(8,128)(2,1)S(1)} %pad_maximum_fusion.6), channel_id=1, source_target_pairs={{0,2},{1,3},{2,0},{3,1},{4,6},{5,7},{6,4},{7,5},{8,10},{9,11},{10,... | collective-permute-start | bytes 1105928 | tf_op jit(solution)/shard_map/ppermute | solution.py:695
  220.0 21.5 %collective-permute-start.47 = (bf16[4,144,384]{2,1,0:T(8,128)(2,1)S(1)}, bf16[4,144,384]{2,1,0:T(8,128)(2,1)S(1)}, u32[]{:S(2)}, u32[]{:S(2)}) collective-permute-start(bf16[4,144,384]{2,1,0:T(8,128)(2,1)S(1)} %get-tuple-element.392), channel_id=1, source_target_pairs={{0,16},{1,17},{2,18},{3,19},{4,20},{5,21},{6,22},{7,23},{8,24},{9,... | collective-permute-start | bytes 1327112 | tf_op jit(solution)/shard_map/ppermute | solution.py:695
  220.5 21.0 %collective-permute-start.48 = (bf16[4,144,384]{2,1,0:T(8,128)(2,1)S(1)}, bf16[4,144,384]{2,1,0:T(8,128)(2,1)S(1)}, u32[]{:S(2)}, u32[]{:S(2)}) collective-permute-start(bf16[4,144,384]{2,1,0:T(8,128)(2,1)S(1)} %get-tuple-element.393), channel_id=1, source_target_pairs={{0,1},{1,0},{2,3},{3,2},{4,5},{5,4},{6,7},{7,6},{8,9},{9,8},{10,11... | collective-permute-start | bytes 1327112 | tf_op jit(solution)/shard_map/ppermute | solution.py:695
  221.9 19.6 %collective-permute-start.49 = (bf16[4,144,384]{2,1,0:T(8,128)(2,1)S(1)}, bf16[4,144,384]{2,1,0:T(8,128)(2,1)S(1)}, u32[]{:S(2)}, u32[]{:S(2)}) collective-permute-start(bf16[4,144,384]{2,1,0:T(8,128)(2,1)S(1)} %get-tuple-element.394), channel_id=1, source_target_pairs={{0,17},{1,16},{2,19},{3,18},{4,21},{5,20},{6,23},{7,22},{8,25},{9,... | collective-permute-start | bytes 1327112 | tf_op jit(solution)/shard_map/ppermute | solution.py:695
  228.2 13.4 %collective-permute-start.52 = (bf16[240,384]{1,0:T(8,128)(2,1)S(1)}, bf16[240,384]{1,0:T(8,128)(2,1)S(1)}, u32[]{:S(2)}, u32[]{:S(2)}) collective-permute-start(bf16[240,384]{1,0:T(8,128)(2,1)S(1)} %get-tuple-element.452), channel_id=1, source_target_pairs={{0,4},{1,5},{2,6},{3,7},{4,0},{5,1},{6,2},{7,3},{8,12},{9,13},{10,... | collective-permute-start | bytes 552968 | tf_op jit(solution)/shard_map/ppermute | solution.py:695
  230.1 11.4 %collective-permute-start.53 = (f32[3,8,768]{2,1,0:T(8,128)S(1)}, f32[3,8,768]{2,1,0:T(8,128)S(1)}, u32[]{:S(2)}, u32[]{:S(2)}) collective-permute-start(f32[3,8,768]{2,1,0:T(8,128)S(1)} %add.287), channel_id=1, source_target_pairs={{0,16},{1,17},{2,18},{3,19},{4,20},{5,21},{6,22},{7,23},{8,24},{9,... | collective-permute-start | bytes 221192 | tf_op jit(solution)/shard_map/ppermute | solution.py:695
  (38 other events, 245.3 us)

commit v5 on v4

--- a/solution.py
+++ b/solution.py
@@ -184,10 +184,12 @@
 
 
 def inner_kernel(low, wi, bi, act_o, slope_o):
-    v = dot(low[...], wi[...]) + bi[...]
-    act, slope = gelu_parts(v)
-    act_o[...] = act.astype(LOW)
-    slope_o[...] = slope.astype(LOW)
+    blk = 128
+    for at in range(0, low.shape[0], blk):
+        rows = slice(at, at + blk)
+        act, slope = gelu_parts(dot(low[rows, :], wi[...]) + bi[...])
+        act_o[rows, :] = act.astype(LOW)
+        slope_o[rows, :] = slope.astype(LOW)
 
 
 def inner(low, wi, bi):
@@ -503,8 +505,8 @@
 
 
 def grads(name, where, lefts, which, rights, add=None):
-    seq = lefts[0].shape[0]
-    parts = lefts[0].shape[1] // 16
+    features, seq = lefts[0].shape if add is not None else lefts[0].shape[::-1]
+    parts = features // 16
     widths = tuple((w, r.shape[1] // 2) for w, r in zip(which, rights))
     total = sum(w for _, w in widths)
     half = (lambda i, where: (0, 1 - where[3])) if add is None else (lambda i, where: (0, where[3]))
@@ -512,7 +514,7 @@
     specs += [pl.BlockSpec((seq, w), half, pipeline_mode=pl.Buffered(1)) for _, w in widths]
     args = [where, *lefts, *rights]
     piece = (4, parts * total // COLUMNS, COLUMNS)
-    outs = ((4, *piece),) if add is None else (piece,) * 4
+    outs = ((4, *piece),) + ((features, seq),) * len(lefts) if add is None else (piece,) * 4
     if add is not None:
         specs.append(full(add.shape))
         args.append(add)
@@ -520,12 +522,14 @@
     def kernel(where, *refs):
         left_refs, refs = refs[: len(lefts)], refs[len(lefts) :]
         right_refs, refs = refs[: len(rights)], refs[len(rights) :]
-        add_ref = None if add is None else refs[0]
-        out_refs, turned = refs[: len(outs)] if add is None else refs[1 : 1 + len(outs)], refs[-len(lefts) :]
         x, y, z0 = where[0], where[1], where[2]
-        for left, store in zip(left_refs, turned):
-            for start in range(0, left.shape[1], 256):
-                store[start : start + 256, :] = left[:, start : start + 256].T
+        if add is None:
+            out_refs, turned = refs[:1], refs[1:]
+            for left, store in zip(left_refs, turned):
+                for start in range(0, features, 256):
+                    store[start : start + 256, :] = left[:, start : start + 256].T
+        else:
+            add_ref, out_refs, turned = refs[0], refs[1:], left_refs
         for place in range(4):
             hh = jnp.bitwise_xor(x, place // 2)
             yy = jnp.bitwise_xor(y, place % 2)
@@ -551,13 +555,12 @@
         specs,
         tuple(full(o) for o in outs),
         args,
-        scratch=[pltpu.VMEM((a.shape[1], seq), LOW) for a in lefts],
         prefetch=1,
         flops=2 * seq * 16 * parts * total,
         moved=2 * 16 * parts * total + 2 * seq * 16 * parts,
         name=name,
     )
-    return got[0] if add is None else got
+    return (got[0], list(got[1:])) if add is None else got
 
 
 def pack_kernel(where, wq, wk, wv, wo, wi, wf, wp, small, own_a, own_b, own_c):
@@ -839,6 +842,7 @@
         wo, wi = finish_weights(where, begun_b, [xy_b, core_xy_b], spans_b)
         n1, r1, first_low = attended(context, wo, tokens, table)
         activated, slope = inner(first_low, wi, inner_row)
+        (core_c, activated, slope) = together(core_c, activated, slope)
         begun_c = place_some(where, mixed((far_c, y_c, x_c), core_c), spans_c, range(6))
         (xy_c, begun_c, activated, slope) = together(xy_c, begun_c, activated, slope)
         wf, wp = finish_weights(where, begun_c, [xy_c, *to_core([xy_c])], spans_c)
@@ -878,12 +882,12 @@
             same, y, x, xy = parts
             return [same, swap(x, X_SWAP), swap(y, Y_SWAP), swap(xy, XY_SWAP)]
 
-        other = grads("outer_grad_a", where, [activated], [0], [branch_grad])
+        other, lefts = grads("outer_grad_a", where, [activated], [0], [branch_grad])
         (other, branch_grad) = together(other, branch_grad)
         other, heads = swap(other, CORE_SWAP), gathered(heads, Z_SWAPS[1])
         inner_grad = inner_grads(branch_grad, wf, slope)
         (other, inner_grad, heads) = together(other, inner_grad, heads)
-        mine = grads("outer_grad_b", where, [activated], [0], [branch_grad], other)
+        mine = grads("outer_grad_b", where, lefts, [0], [branch_grad], other)
         (mine, inner_grad, heads) = together(mine, inner_grad, heads)
         same_f, y_f, x_f, xy_f = mine
         from_x, from_y = swap(x_f[:3], X_SWAP), swap(y_f[:3], Y_SWAP)
@@ -891,7 +895,7 @@
         residual_grad, attended_grad, sums1 = inner_back(inner_grad, wi, second_grad, n1, r1, table)
         (attended_grad, inner_grad) = together(attended_grad, inner_grad)
         lefts, rights = [context, first_low], [attended_grad, inner_grad]
-        other = grads("inner_grad_a", where, lefts, [0, 1], rights)
+        other, lefts = grads("inner_grad_a", where, lefts, [0, 1], rights)
         (other, attended_grad, from_x, from_y, x_f, y_f, xy_f, heads) = together(
             other, attended_grad, from_x, from_y, x_f[3], y_f[3], xy_f, heads
         )
@@ -906,7 +910,7 @@
         back_b = attention_step(attended_grad, cut, width - cut)
         dq, dk, dv, sums0 = (jnp.concatenate([a, b], axis=1) for a, b in zip(back_a, back_b))
         rights = [dq, dk, dv]
-        other = grads("query_grad_a", where, [tokens], [0, 0, 0], rights)
+        other, lefts = grads("query_grad_a", where, [tokens], [0, 0, 0], rights)
         sums = jnp.stack([sums2, sums1, sums0])
         (other, dq, dk, dv, sums, x_f, y_f, xy_f, mine, heads) = together(
             other, dq, dk, dv, sums, x_f, y_f, xy_f, mine, heads
@@ -917,7 +921,7 @@
         totals_f = [wide(same_f[d], xy_f[d], from_x[d], from_y[d]) for d in range(3)]
         totals_f.append(wide(same_f[3], xy_f[3], x_f, y_f))
         odd_f = swap(low(jnp.stack([totals_f[1], totals_f[3]])), Z_SWAPS[1])
-        mine = grads("query_grad_b", where, [tokens], [0, 0, 0], rights, other)
+        mine = grads("query_grad_b", where, lefts, [0, 0, 0], rights, other)
         (mine, odd_f, even_f, dq, dk, dv, sums, heads) = together(
             mine, odd_f, [totals_f[0], totals_f[2]], dq, dk, dv, sums, heads
         )

time: 268 us -> 266 us (level)
  transfers between devices with their start and end apart: 64 -> 64, of which waited for: 29 -> 28; matrix products, arithmetic and copies ran while one was open for 3% -> 3% of each run, Pallas kernels for 26% -> 26%
where the time goes in v5:
time: 266 us; the launch traced here: 263 us
  waiting for transfers between devices  96.6 us (36%)
  Pallas kernels  86.2 us (32%)
  starting transfers between devices  62 us (23%)
  local copies, waits for them, and re-layouts  7.72 us (3%)
  other arithmetic  6.35 us (2%)
    ppermute x64, waiting for transfers between devices, swap(): return lax.ppermute(a, MESH_AXES, pairs)  96.6 us
    pallas_call x18, Pallas kernels, call(): pl.pallas_call(kernel, name=name, out_shape=outs, grid_spec=pltpu.Prefetc...  75.2 us
    ppermute x64, starting transfers between devices, swap(): return lax.ppermute(a, MESH_AXES, pairs)  62 us
    pallas_call x6, Pallas kernels, place_some(): pl.pallas_call(functools.partial(weights_kernel, tuple(spans), tuple(plac...  11 us
  transfers between devices with their start and end apart: 64, of which 28 were waited for; matrix products, arithmetic and copies ran while one was open for 3% of the time, Pallas kernels for 26%

profile of v5, /device:TPU:0, one launch (start us, length us, event | category | flops | bytes accessed | tf_op | source)
XLA Modules:
  0.0 262.8 jit_solution(4483055754784176628)
XLA Ops:
  4.7 5.1 %collective-permute-start.2 = (bf16[56,1152]{1,0:T(8,128)(2,1)S(1)}, bf16[56,1152]{1,0:T(8,128)(2,1)S(1)}, u32[]{:S(2)}, u32[]{:S(2)}) collective-permute-start(bf16[56,1152]{1,0:T(8,128)(2,1)S(1)} %get-tuple-element.242), channel_id=1, source_target_pairs={{0,6},{1,7},{2,4},{3,5},{4,2},{5,3},{6,0},{7,1},{8,14},{9,15},{10,... | collective-permute-start | bytes 387080 | tf_op jit(solution)/shard_map/ppermute | solution.py:698
  10.5 3.7 %collective-permute-done.2 = bf16[56,1152]{1,0:T(8,128)(2,1)S(1)} collective-permute-done((bf16[56,1152]{1,0:T(8,128)(2,1)S(1)}, bf16[56,1152]{1,0:T(8,128)(2,1)S(1)}, u32[]{:S(2)}, u32[]{:S(2)}) %collective-permute-start.2) | collective-permute-done | bytes 129056 | tf_op jit(solution)/shard_map/ppermute | solution.py:698
  14.2 6.5 %collective-permute-done.1 = bf16[56,1152]{1,0:T(8,128)(2,1)S(1)} collective-permute-done((bf16[56,1152]{1,0:T(8,128)(2,1)S(1)}, bf16[56,1152]{1,0:T(8,128)(2,1)S(1)}, u32[]{:S(2)}, u32[]{:S(2)}) %collective-permute-start.1) | collective-permute-done | bytes 129056 | tf_op jit(solution)/shard_map/ppermute | solution.py:698
  23.9 2.5 collective-permute-start.7
  28.3 5.0 %collective-permute-done.7 = bf16[48,1920]{1,0:T(8,128)(2,1)S(1)} collective-permute-done((bf16[48,1920]{1,0:T(8,128)(2,1)S(1)}, bf16[48,1920]{1,0:T(8,128)(2,1)S(1)}, u32[]{:S(2)}, u32[]{:S(2)}) %collective-permute-start.7) | collective-permute-done | bytes 184352 | tf_op jit(solution)/shard_map/ppermute | solution.py:698
  33.3 7.3 %collective-permute-done.6 = bf16[48,1920]{1,0:T(8,128)(2,1)S(1)} collective-permute-done((bf16[48,1920]{1,0:T(8,128)(2,1)S(1)}, bf16[48,1920]{1,0:T(8,128)(2,1)S(1)}, u32[]{:S(2)}, u32[]{:S(2)}) %collective-permute-start.6) | collective-permute-done | bytes 184352 | tf_op jit(solution)/shard_map/ppermute | solution.py:698
  44.9 7.8 %collective-permute-done.12 = bf16[240,384]{1,0:T(8,128)(2,1)S(1)} collective-permute-done((bf16[240,384]{1,0:T(8,128)(2,1)S(1)}, bf16[240,384]{1,0:T(8,128)(2,1)S(1)}, u32[]{:S(2)}, u32[]{:S(2)}) %collective-permute-start.12) | collective-permute-done | bytes 184352 | tf_op jit(solution)/shard_map/ppermute | solution.py:698
  52.7 3.5 %collective-permute-start.10 = (bf16[240,384]{1,0:T(8,128)(2,1)S(1)}, bf16[240,384]{1,0:T(8,128)(2,1)}, u32[]{:S(2)}, u32[]{:S(2)}) collective-permute-start(bf16[240,384]{1,0:T(8,128)(2,1)S(1)} %get-tuple-element.275), channel_id=1, source_target_pairs={{0,2},{1,3},{2,0},{3,1},{4,6},{5,7},{6,4},{7,5},{8,10},{9,11},{10,... | collective-permute-start | bytes 552968 | tf_op jit(solution)/shard_map/ppermute | solution.py:698
  56.6 3.5 %collective-permute-done.11 = bf16[240,384]{1,0:T(8,128)(2,1)} collective-permute-done((bf16[240,384]{1,0:T(8,128)(2,1)S(1)}, bf16[240,384]{1,0:T(8,128)(2,1)}, u32[]{:S(2)}, u32[]{:S(2)}) %collective-permute-start.11) | collective-permute-done | bytes 184352 | tf_op jit(solution)/shard_map/ppermute | solution.py:698
  72.6 8.8 %attention.1 = (bf16[512,768]{1,0:T(8,128)(2,1)S(1)}, bf16[512,768]{1,0:T(8,128)(2,1)S(1)}, bf16[512,768]{1,0:T(8,128)(2,1)S(1)}, bf16[512,768]{1,0:T(8,128)(2,1)S(1)}, f32[3,8,512]{2,1,0:T(8,128)S(1)}) custom-call(bf16[512,768]{1,0:T(8,128)(2,1)S(1)} %bitcast.153, bf16[768,768]{1,0:T(8,128)(2,1)S(1)} %bitcast.147, bf16[768,768]{1,0:T(8,128)(2,1)S(1)} %bitcast.149, ...), custom_call_target="tpu_custom_call" | custom-call | flops 163577856 | bytes 417792 | tf_op jit(solution)/shard_map/attention/pallas_call | solution.py:46
  86.3 2.6 place_weights.8
  88.9 12.3 %collective-permute-done.21.refs_2_ = bf16[4,240,384]{2,1,0:T(8,128)(2,1)S(1)} collective-permute-done((bf16[4,240,384]{2,1,0:T(8,128)(2,1)S(1)}, bf16[4,240,384]{2,1,0:T(8,128)(2,1)S(1)}, u32[]{:S(2)}, u32[]{:S(2)}) %collective-permute-start.21) | collective-permute-done | bytes 737312 | tf_op jit(solution)/shard_map/ppermute | solution.py:698
  105.9 2.2 attended.1
  108.1 9.9 %inner.1 = (bf16[512,3072]{1,0:T(8,128)(2,1)S(1)}, bf16[512,3072]{1,0:T(8,128)(2,1)S(1)}) custom-call(bf16[512,768]{1,0:T(8,128)(2,1)S(1)} %get-tuple-element.294.low.refs_1_, bf16[768,3072]{1,0:T(8,128)(2,1)S(1)} %bitcast.140, f32[1,3072]{1,0:T(1,128)S(1)} %reshape.181.bi), custom_call_target="tpu_custom_call" | custom-call | flops 150994944 | bytes 688128 | tf_op jit(solution)/shard_map/inner/pallas_call | solution.py:46
  118.1 2.6 %place_weights.10 = (bf16[4,2,2,192,768]{4,3,2,1,0:T(8,128)(2,1)S(1)}, bf16[4,2,2,48,768]{4,3,2,1,0:T(8,128)(2,1)S(1)}) custom-call(s32[4]{0:T(128)S(1)} %pad_add_fusion.where, bf16[4,240,384]{2,1,0:T(8,128)(2,1)S(1)} %pad_maximum_fusion.2.refs_0_, bf16[4,240,384]{2,1,0:T(8,128)(2,1)S(1)} %collective-permute-done.23.refs_1_, ...), custom_call_target="tpu_custom_call" | custom-call | bytes 368640 | tf_op jit(solution)/shard_map/place_weights/pallas_call | solution.py:625
  125.4 7.1 %outer.1 = (bf16[512,768]{1,0:T(8,128)(2,1)}, f32[512,768]{1,0:T(8,128)S(1)}, bf16[512,768]{1,0:T(8,128)(2,1)S(1)}, f32[8,768]{1,0:T(8,128)S(1)}, f32[8,768]{1,0:T(8,128)S(1)}, /*index=5*/f32[8,128]{1,0:T(8,128)S(1)}) custom-call(s32[1]{0:T(128)S(6)} %copy.88.labels, f32[3]{0:T(128)S(1)} %convert_element_type.263.bias3, ...), custom_call_target="tpu_custom_call" | custom-call | flops 150994944 | bytes 835584 | tf_op jit(solution)/shard_map/outer/pallas_call | solution.py:46
  132.5 3.2 %outer_grad_a.1 = (bf16[4,4,192,384]{3,2,1,0:T(8,128)(2,1)S(1)}, bf16[3072,512]{1,0:T(8,128)(2,1)S(1)}) custom-call(s32[4]{0:T(128)S(1)} %pad_add_fusion.where, bf16[512,3072]{1,0:T(8,128)(2,1)S(1)} %get-tuple-element.306.act.refs_0_, bf16[512,768]{1,0:T(8,128)(2,1)S(1)} %get-tuple-element.317.refs_1_.bg), custom_call_target="tpu_custom_call" | custom-call | flops 75497472 | bytes 344064 | tf_op jit(solution)/shard_map/outer_grad_a/pallas_call | solution.py:46
  135.9 3.5 %inner_grads.1.ig.refs_3_ = bf16[512,3072]{1,0:T(8,128)(2,1)S(1)} custom-call(bf16[512,768]{1,0:T(8,128)(2,1)S(1)} %get-tuple-element.317.refs_1_.bg, bf16[3072,768]{1,0:T(8,128)(2,1)S(1)} %bitcast.143, bf16[512,3072]{1,0:T(8,128)(2,1)S(1)} %get-tuple-element.319.slope), custom_call_target="tpu_custom_call" | custom-call | flops 150994944 | bytes 688128 | tf_op jit(solution)/shard_map/inner_grads/pallas_call | solution.py:46
  140.3 2.4 outer_grad_b.1
  148.1 5.3 %inner_back.1 = (f32[512,768]{1,0:T(8,128)S(1)}, bf16[512,768]{1,0:T(8,128)(2,1)S(1)}, f32[8,768]{1,0:T(8,128)S(1)}) custom-call(bf16[512,3072]{1,0:T(8,128)(2,1)S(1)} %inner_grads.1.ig.refs_3_, bf16[768,3072]{1,0:T(8,128)(2,1)S(1)} %bitcast.141, f32[512,768]{1,0:T(8,128)S(1)} %get-tuple-element.329.sg, f32[512,768]{1,0:T(8,128)S(1)} %get-tuple-element.311.n1, ...), custom_call_target="tpu_custom_call" | custom-call | flops 150994944 | bytes 884736 | tf_op jit(solution)/shard_map/inner_back/pallas_call | solution.py:46
  153.4 2.8 %inner_grad_a.1 = (bf16[4,4,240,384]{3,2,1,0:T(8,128)(2,1)S(1)}, bf16[768,512]{1,0:T(8,128)(2,1)S(1)}, bf16[768,512]{1,0:T(8,128)(2,1)S(1)}) custom-call(s32[4]{0:T(128)S(1)} %pad_add_fusion.where, bf16[512,768]{1,0:T(8,128)(2,1)S(1)} %get-tuple-element.289.ctx.refs_0_, bf16[512,768]{1,0:T(8,128)(2,1)S(1)} %get-tuple-element.294.low.refs_1_, ...), custom_call_target="tpu_custom_call" | custom-call | flops 94371840 | bytes 233472 | tf_op jit(solution)/shard_map/inner_grad_a/pallas_call | solution.py:46
  161.3 7.9 %attention_back.2 = (bf16[512,512]{1,0:T(8,128)(2,1)S(1)}, bf16[512,512]{1,0:T(8,128)(2,1)S(1)}, bf16[512,512]{1,0:T(8,128)(2,1)S(1)}, f32[8,512]{1,0:T(8,128)S(1)}) custom-call(bf16[512,768]{1,0:T(8,128)(2,1)S(1)} %get-tuple-element.340.q, bf16[512,768]{1,0:T(8,128)(2,1)S(1)} %get-tuple-element.341.k, bf16[512,768]{1,0:T(8,128)(2,1)S(1)} %get-tuple-element.342.v, ...), custom_call_target="tpu_custom_call" | custom-call | flops 109051904 | bytes 311296 | tf_op jit(solution)/shard_map/attention_back/pallas_call | solution.py:46
  169.3 2.5 inner_grad_b.1
  171.8 3.6 %attention_back.3 = (bf16[512,256]{1,0:T(8,128)(2,1)S(1)}, bf16[512,256]{1,0:T(8,128)(2,1)S(1)}, bf16[512,256]{1,0:T(8,128)(2,1)S(1)}, f32[8,256]{1,0:T(8,128)S(1)}) custom-call(bf16[512,768]{1,0:T(8,128)(2,1)S(1)} %get-tuple-element.340.q, bf16[512,768]{1,0:T(8,128)(2,1)S(1)} %get-tuple-element.341.k, bf16[512,768]{1,0:T(8,128)(2,1)S(1)} %get-tuple-element.342.v, ...), custom_call_target="tpu_custom_call" | custom-call | flops 54525952 | bytes 155648 | tf_op jit(solution)/shard_map/attention_back/pallas_call | solution.py:46
  175.7 2.2 query_grad_a.1
  186.5 4.9 %collective-permute-done.44 = bf16[2,192,384]{2,1,0:T(8,128)(2,1)S(1)} collective-permute-done((bf16[2,192,384]{2,1,0:T(8,128)(2,1)S(1)}, bf16[2,192,384]{2,1,0:T(8,128)(2,1)S(1)}, u32[]{:S(2)}, u32[]{:S(2)}) %collective-permute-start.44) | collective-permute-done | bytes 294944 | tf_op jit(solution)/shard_map/ppermute | solution.py:698
  194.4 6.1 %tokens_back.1 = f32[512,768]{1,0:T(8,128)} custom-call(f32[512,768]{1,0:T(8,128)S(1)} %get-tuple-element.407.res, bf16[512,768]{1,0:T(8,128)(2,1)S(1)} %constant_dynamic-update-slice_fusion.refs_1_.dq, bf16[512,768]{1,0:T(8,128)(2,1)S(1)} %constant_dynamic-update-slice_fusion.2.refs_2_.dk, ...), custom_call_target="tpu_custom_call" | custom-call | flops 113246208 | bytes 565248 | tf_op jit(solution)/shard_map/tokens_back/pallas_call | solution.py:46
  200.5 14.3 %collective-permute-done.41 = bf16[4,240,384]{2,1,0:T(8,128)(2,1)S(1)} collective-permute-done((bf16[4,240,384]{2,1,0:T(8,128)(2,1)S(1)}, bf16[4,240,384]{2,1,0:T(8,128)(2,1)S(1)}, u32[]{:S(2)}, u32[]{:S(2)}) %collective-permute-start.41) | collective-permute-done | bytes 737312 | tf_op jit(solution)/shard_map/ppermute | solution.py:698
  221.8 3.0 %collective-permute-done.51 = f32[3,8,768]{2,1,0:T(8,128)S(1)} collective-permute-done((f32[3,8,768]{2,1,0:T(8,128)S(1)}, f32[3,8,768]{2,1,0:T(8,128)S(1)}, u32[]{:S(2)}, u32[]{:S(2)}) %collective-permute-start.51) | collective-permute-done | bytes 73760 | tf_op jit(solution)/shard_map/ppermute | solution.py:698
  229.6 10.1 %collective-permute-done.53 = f32[3,8,768]{2,1,0:T(8,128)S(1)} collective-permute-done((f32[3,8,768]{2,1,0:T(8,128)S(1)}, f32[3,8,768]{2,1,0:T(8,128)S(1)}, u32[]{:S(2)}, u32[]{:S(2)}) %collective-permute-start.53) | collective-permute-done | bytes 73760 | tf_op jit(solution)/shard_map/ppermute | solution.py:698
  247.3 2.4 collective-permute-done.58
  260.4 2.3 place_shards.3
  (204 shorter events, 93.4 us)
Async XLA Ops:
  20.8 19.8 %collective-permute-start.4 = (bf16[4,56,1152]{2,1,0:T(8,128)(2,1)S(1)}, bf16[4,56,1152]{2,1,0:T(8,128)(2,1)S(1)}, u32[]{:S(2)}, u32[]{:S(2)}) collective-permute-start(bf16[4,56,1152]{2,1,0:T(8,128)(2,1)S(1)} %pad_maximum_fusion.4.refs_0_), channel_id=1, source_target_pairs={{0,1},{1,0},{2,3},{3,2},{4,5},{5,4},{6,7},{7,6},{8,9},{9,8},{10,11... | collective-permute-start | bytes 1548296 | tf_op jit(solution)/shard_map/ppermute | solution.py:698
  22.4 18.2 %collective-permute-start.3 = (bf16[4,56,1152]{2,1,0:T(8,128)(2,1)S(1)}, bf16[4,56,1152]{2,1,0:T(8,128)(2,1)S(1)}, u32[]{:S(2)}, u32[]{:S(2)}) collective-permute-start(bf16[4,56,1152]{2,1,0:T(8,128)(2,1)S(1)} %pad_maximum_fusion.4.refs_0_), channel_id=1, source_target_pairs={{0,16},{1,17},{2,18},{3,19},{4,20},{5,21},{6,22},{7,23},{8,24},{9,... | collective-permute-start | bytes 1548296 | tf_op jit(solution)/shard_map/ppermute | solution.py:698
  26.4 14.2 %collective-permute-start.6 = (bf16[48,1920]{1,0:T(8,128)(2,1)S(1)}, bf16[48,1920]{1,0:T(8,128)(2,1)S(1)}, u32[]{:S(2)}, u32[]{:S(2)}) collective-permute-start(bf16[48,1920]{1,0:T(8,128)(2,1)S(1)} %get-tuple-element.251), channel_id=1, source_target_pairs={{0,4},{1,5},{2,6},{3,7},{4,0},{5,1},{6,2},{7,3},{8,12},{9,13},{10,... | collective-permute-start | bytes 552968 | tf_op jit(solution)/shard_map/ppermute | solution.py:698
  26.4 14.2 %collective-permute-start.5 = (bf16[48,1920]{1,0:T(8,128)(2,1)S(1)}, bf16[48,1920]{1,0:T(8,128)(2,1)S(1)}, u32[]{:S(2)}, u32[]{:S(2)}) collective-permute-start(bf16[48,1920]{1,0:T(8,128)(2,1)S(1)} %get-tuple-element.251), channel_id=1, source_target_pairs={{0,2},{1,3},{2,0},{3,1},{4,6},{5,7},{6,4},{7,5},{8,10},{9,11},{10,... | collective-permute-start | bytes 552968 | tf_op jit(solution)/shard_map/ppermute | solution.py:698
  42.0 20.0 %collective-permute-start.13 = (bf16[12,56,1152]{2,1,0:T(8,128)(2,1)}, bf16[12,56,1152]{2,1,0:T(8,128)(2,1)}, u32[]{:S(2)}, u32[]{:S(2)}) collective-permute-start(bf16[12,56,1152]{2,1,0:T(8,128)(2,1)} %pad_maximum_fusion), channel_id=1, source_target_pairs={{0,8},{1,9},{2,10},{3,11},{4,12},{5,13},{6,14},{7,15},{8,0},{9,1},... | collective-permute-start | bytes 4644872 | tf_op jit(solution)/shard_map/ppermute | solution.py:698
  42.1 19.8 %collective-permute-start.9 = (bf16[4,48,1920]{2,1,0:T(8,128)(2,1)S(1)}, bf16[4,48,1920]{2,1,0:T(8,128)(2,1)S(1)}, u32[]{:S(2)}, u32[]{:S(2)}) collective-permute-start(bf16[4,48,1920]{2,1,0:T(8,128)(2,1)S(1)} %pad_maximum_fusion.1.refs_0_), channel_id=1, source_target_pairs={{0,16},{1,17},{2,18},{3,19},{4,20},{5,21},{6,22},{7,23},{8,24},{9,... | collective-permute-start | bytes 2211848 | tf_op jit(solution)/shard_map/ppermute | solution.py:698
  42.7 19.2 %collective-permute-start.8 = (bf16[4,56,1152]{2,1,0:T(8,128)(2,1)S(1)}, bf16[4,56,1152]{2,1,0:T(8,128)(2,1)}, u32[]{:S(2)}, u32[]{:S(2)}) collective-permute-start(bf16[4,56,1152]{2,1,0:T(8,128)(2,1)S(1)} %collective-permute-done.3.refs_4_), channel_id=1, source_target_pairs={{0,1},{1,0},{2,3},{3,2},{4,5},{5,4},{6,7},{7,6},{8,9},{9,8},{10,11... | collective-permute-start | bytes 1548296 | tf_op jit(solution)/shard_map/ppermute | solution.py:698
  44.9 15.2 %collective-permute-start.11 = (bf16[240,384]{1,0:T(8,128)(2,1)S(1)}, bf16[240,384]{1,0:T(8,128)(2,1)}, u32[]{:S(2)}, u32[]{:S(2)}) collective-permute-start(bf16[240,384]{1,0:T(8,128)(2,1)S(1)} %get-tuple-element.275), channel_id=1, source_target_pairs={{0,4},{1,5},{2,6},{3,7},{4,0},{5,1},{6,2},{7,3},{8,12},{9,13},{10,... | collective-permute-start | bytes 552968 | tf_op jit(solution)/shard_map/ppermute | solution.py:698
  63.9 17.5 %collective-permute-start.16 = (bf16[4,240,384]{2,1,0:T(8,128)(2,1)S(1)}, bf16[4,240,384]{2,1,0:T(8,128)(2,1)}, u32[]{:S(2)}, u32[]{:S(2)}) collective-permute-start(bf16[4,240,384]{2,1,0:T(8,128)(2,1)S(1)} %pad_maximum_fusion.2.refs_0_), channel_id=1, source_target_pairs={{0,16},{1,17},{2,18},{3,19},{4,20},{5,21},{6,22},{7,23},{8,24},{9,... | collective-permute-start | bytes 2211848 | tf_op jit(solution)/shard_map/ppermute | solution.py:698
  65.5 16.3 %collective-permute-start.15 = (bf16[4,48,1920]{2,1,0:T(8,128)(2,1)S(1)}, bf16[4,48,1920]{2,1,0:T(8,128)(2,1)}, u32[]{:S(2)}, u32[]{:S(2)}) collective-permute-start(bf16[4,48,1920]{2,1,0:T(8,128)(2,1)S(1)} %pad_maximum_fusion.1.refs_0_), channel_id=1, source_target_pairs={{0,1},{1,0},{2,3},{3,2},{4,5},{5,4},{6,7},{7,6},{8,9},{9,8},{10,11... | collective-permute-start | bytes 2211848 | tf_op jit(solution)/shard_map/ppermute | solution.py:698
  82.5 18.6 %collective-permute-start.21 = (bf16[4,240,384]{2,1,0:T(8,128)(2,1)S(1)}, bf16[4,240,384]{2,1,0:T(8,128)(2,1)S(1)}, u32[]{:S(2)}, u32[]{:S(2)}) collective-permute-start(bf16[4,240,384]{2,1,0:T(8,128)(2,1)S(1)} %pad_maximum_fusion.2.refs_0_), channel_id=1, source_target_pairs={{0,1},{1,0},{2,3},{3,2},{4,5},{5,4},{6,7},{7,6},{8,9},{9,8},{10,11... | collective-permute-start | bytes 2211848 | tf_op jit(solution)/shard_map/ppermute | solution.py:698
  83.8 18.8 %collective-permute-start.17 = (bf16[4,48,1920]{2,1,0:T(8,128)(2,1)}, bf16[4,48,1920]{2,1,0:T(8,128)(2,1)S(1)}, u32[]{:S(2)}, u32[]{:S(2)}) collective-permute-start(bf16[4,48,1920]{2,1,0:T(8,128)(2,1)} %collective-permute-done.15.refs_2_), channel_id=1, source_target_pairs={{0,16},{1,17},{2,18},{3,19},{4,20},{5,21},{6,22},{7,23},{8,24},{9,... | collective-permute-start | bytes 2211848 | tf_op jit(solution)/shard_map/ppermute | solution.py:698
  102.6 15.5 %collective-permute-start.23 = (bf16[4,240,384]{2,1,0:T(8,128)(2,1)S(1)}, bf16[4,240,384]{2,1,0:T(8,128)(2,1)S(1)}, u32[]{:S(2)}, u32[]{:S(2)}) collective-permute-start(bf16[4,240,384]{2,1,0:T(8,128)(2,1)S(1)} %pad_maximum_fusion.2.refs_0_), channel_id=1, source_target_pairs={{0,8},{1,9},{2,10},{3,11},{4,12},{5,13},{6,14},{7,15},{8,0},{9,1},... | collective-permute-start | bytes 2211848 | tf_op jit(solution)/shard_map/ppermute | solution.py:698
  103.1 15.0 %collective-permute-start.24 = (bf16[4,240,384]{2,1,0:T(8,128)(2,1)S(1)}, bf16[4,240,384]{2,1,0:T(8,128)(2,1)S(1)}, u32[]{:S(2)}, u32[]{:S(2)}) collective-permute-start(bf16[4,240,384]{2,1,0:T(8,128)(2,1)S(1)} %collective-permute-done.21.refs_2_), channel_id=1, source_target_pairs={{0,8},{1,9},{2,10},{3,11},{4,12},{5,13},{6,14},{7,15},{8,0},{9,1},... | collective-permute-start | bytes 2211848 | tf_op jit(solution)/shard_map/ppermute | solution.py:698
  103.1 15.0 %collective-permute-start.25 = (bf16[4,240,384]{2,1,0:T(8,128)(2,1)}, bf16[4,240,384]{2,1,0:T(8,128)(2,1)S(1)}, u32[]{:S(2)}, u32[]{:S(2)}) collective-permute-start(bf16[4,240,384]{2,1,0:T(8,128)(2,1)} %collective-permute-done.16.refs_4_), channel_id=1, source_target_pairs={{0,8},{1,9},{2,10},{3,11},{4,12},{5,13},{6,14},{7,15},{8,0},{9,1},... | collective-permute-start | bytes 2211848 | tf_op jit(solution)/shard_map/ppermute | solution.py:698
  103.6 18.6 %collective-permute-start.22 = (bf16[4,240,384]{2,1,0:T(8,128)(2,1)}, bf16[4,240,384]{2,1,0:T(8,128)(2,1)S(1)}, u32[]{:S(2)}, u32[]{:S(2)}) collective-permute-start(bf16[4,240,384]{2,1,0:T(8,128)(2,1)} %collective-permute-done.16.refs_4_), channel_id=1, source_target_pairs={{0,1},{1,0},{2,3},{3,2},{4,5},{5,4},{6,7},{7,6},{8,9},{9,8},{10,11... | collective-permute-start | bytes 2211848 | tf_op jit(solution)/shard_map/ppermute | solution.py:698
  144.1 13.0 %collective-permute-start.31 = (bf16[3,192,384]{2,1,0:T(8,128)(2,1)S(1)}, bf16[3,192,384]{2,1,0:T(8,128)(2,1)S(1)}, u32[]{:S(2)}, u32[]{:S(2)}) collective-permute-start(bf16[3,192,384]{2,1,0:T(8,128)(2,1)S(1)} %slice.243), channel_id=1, source_target_pairs={{0,1},{1,0},{2,3},{3,2},{4,5},{5,4},{6,7},{7,6},{8,9},{9,8},{10,11... | collective-permute-start | bytes 1327112 | tf_op jit(solution)/shard_map/ppermute | solution.py:698
  145.3 11.8 %collective-permute-start.30 = (bf16[3,192,384]{2,1,0:T(8,128)(2,1)S(1)}, bf16[3,192,384]{2,1,0:T(8,128)(2,1)S(1)}, u32[]{:S(2)}, u32[]{:S(2)}) collective-permute-start(bf16[3,192,384]{2,1,0:T(8,128)(2,1)S(1)} %slice.242), channel_id=1, source_target_pairs={{0,16},{1,17},{2,18},{3,19},{4,20},{5,21},{6,22},{7,23},{8,24},{9,... | collective-permute-start | bytes 1327112 | tf_op jit(solution)/shard_map/ppermute | solution.py:698
  157.2 12.2 %collective-permute-start.34 = (bf16[4,4,240,384]{3,2,1,0:T(8,128)(2,1)S(1)}, bf16[4,4,240,384]{3,2,1,0:T(8,128)(2,1)S(1)}, u32[]{:S(2)}, u32[]{:S(2)}) collective-permute-start(bf16[4,4,240,384]{3,2,1,0:T(8,128)(2,1)S(1)} %get-tuple-element.339), channel_id=1, source_target_pairs={{0,8},{1,9},{2,10},{3,11},{4,12},{5,13},{6,14},{7,15},{8,0},{9,1},... | collective-permute-start | bytes 8847368 | tf_op jit(solution)/shard_map/ppermute | solution.py:698
  157.2 12.0 %collective-permute-start.35 = (bf16[8,8,768]{2,1,0:T(8,128)(2,1)S(1)}, bf16[8,8,768]{2,1,0:T(8,128)(2,1)S(1)}, u32[]{:S(2)}, u32[]{:S(2)}) collective-permute-start(bf16[8,8,768]{2,1,0:T(8,128)(2,1)S(1)} %pad_maximum_fusion.10), channel_id=1, source_target_pairs={{0,16},{1,17},{2,18},{3,19},{4,20},{5,21},{6,22},{7,23},{8,24},{9,... | collective-permute-start | bytes 294920 | tf_op jit(solution)/shard_map/ppermute | solution.py:698
  157.8 20.9 %collective-permute-start.36 = (bf16[192,384]{1,0:T(8,128)(2,1)S(1)}, bf16[192,384]{1,0:T(8,128)(2,1)S(1)}, u32[]{:S(2)}, u32[]{:S(2)}) collective-permute-start(bf16[192,384]{1,0:T(8,128)(2,1)S(1)} %get-tuple-element.371), channel_id=1, source_target_pairs={{0,16},{1,17},{2,18},{3,19},{4,20},{5,21},{6,22},{7,23},{8,24},{9,... | collective-permute-start | bytes 442376 | tf_op jit(solution)/shard_map/ppermute | solution.py:698
  159.3 19.4 %collective-permute-start.37 = (bf16[192,384]{1,0:T(8,128)(2,1)S(1)}, bf16[192,384]{1,0:T(8,128)(2,1)S(1)}, u32[]{:S(2)}, u32[]{:S(2)}) collective-permute-start(bf16[192,384]{1,0:T(8,128)(2,1)S(1)} %get-tuple-element.372), channel_id=1, source_target_pairs={{0,1},{1,0},{2,3},{3,2},{4,5},{5,4},{6,7},{7,6},{8,9},{9,8},{10,11... | collective-permute-start | bytes 442376 | tf_op jit(solution)/shard_map/ppermute | solution.py:698
  160.5 18.4 %collective-permute-start.38 = (bf16[4,192,384]{2,1,0:T(8,128)(2,1)S(1)}, bf16[4,192,384]{2,1,0:T(8,128)(2,1)S(1)}, u32[]{:S(2)}, u32[]{:S(2)}) collective-permute-start(bf16[4,192,384]{2,1,0:T(8,128)(2,1)S(1)} %get-tuple-element.373), channel_id=1, source_target_pairs={{0,17},{1,16},{2,19},{3,18},{4,21},{5,20},{6,23},{7,22},{8,25},{9,... | collective-permute-start | bytes 1769480 | tf_op jit(solution)/shard_map/ppermute | solution.py:698
  179.3 21.2 %collective-permute-start.40 = (bf16[4,240,384]{2,1,0:T(8,128)(2,1)S(1)}, bf16[4,240,384]{2,1,0:T(8,128)(2,1)S(1)}, u32[]{:S(2)}, u32[]{:S(2)}) collective-permute-start(bf16[4,240,384]{2,1,0:T(8,128)(2,1)S(1)} %get-tuple-element.380), channel_id=1, source_target_pairs={{0,16},{1,17},{2,18},{3,19},{4,20},{5,21},{6,22},{7,23},{8,24},{9,... | collective-permute-start | bytes 2211848 | tf_op jit(solution)/shard_map/ppermute | solution.py:698
  180.8 34.0 %collective-permute-start.41 = (bf16[4,240,384]{2,1,0:T(8,128)(2,1)S(1)}, bf16[4,240,384]{2,1,0:T(8,128)(2,1)S(1)}, u32[]{:S(2)}, u32[]{:S(2)}) collective-permute-start(bf16[4,240,384]{2,1,0:T(8,128)(2,1)S(1)} %get-tuple-element.381), channel_id=1, source_target_pairs={{0,1},{1,0},{2,3},{3,2},{4,5},{5,4},{6,7},{7,6},{8,9},{9,8},{10,11... | collective-permute-start | bytes 2211848 | tf_op jit(solution)/shard_map/ppermute | solution.py:698
  182.0 32.9 %collective-permute-start.42 = (bf16[4,240,384]{2,1,0:T(8,128)(2,1)S(1)}, bf16[4,240,384]{2,1,0:T(8,128)(2,1)S(1)}, u32[]{:S(2)}, u32[]{:S(2)}) collective-permute-start(bf16[4,240,384]{2,1,0:T(8,128)(2,1)S(1)} %get-tuple-element.382), channel_id=1, source_target_pairs={{0,17},{1,16},{2,19},{3,18},{4,21},{5,20},{6,23},{7,22},{8,25},{9,... | collective-permute-start | bytes 2211848 | tf_op jit(solution)/shard_map/ppermute | solution.py:698
  191.5 23.4 %collective-permute-start.45 = (bf16[192,384]{1,0:T(8,128)(2,1)S(1)}, bf16[192,384]{1,0:T(8,128)(2,1)S(1)}, u32[]{:S(2)}, u32[]{:S(2)}) collective-permute-start(bf16[192,384]{1,0:T(8,128)(2,1)S(1)} %get-tuple-element.478), channel_id=1, source_target_pairs={{0,4},{1,5},{2,6},{3,7},{4,0},{5,1},{6,2},{7,3},{8,12},{9,13},{10,... | collective-permute-start | bytes 442376 | tf_op jit(solution)/shard_map/ppermute | solution.py:698
  218.2 21.5 %collective-permute-start.47 = (bf16[4,144,384]{2,1,0:T(8,128)(2,1)S(1)}, bf16[4,144,384]{2,1,0:T(8,128)(2,1)S(1)}, u32[]{:S(2)}, u32[]{:S(2)}) collective-permute-start(bf16[4,144,384]{2,1,0:T(8,128)(2,1)S(1)} %get-tuple-element.416), channel_id=1, source_target_pairs={{0,16},{1,17},{2,18},{3,19},{4,20},{5,21},{6,22},{7,23},{8,24},{9,... | collective-permute-start | bytes 1327112 | tf_op jit(solution)/shard_map/ppermute | solution.py:698
  218.8 21.0 %collective-permute-start.48 = (bf16[4,144,384]{2,1,0:T(8,128)(2,1)S(1)}, bf16[4,144,384]{2,1,0:T(8,128)(2,1)S(1)}, u32[]{:S(2)}, u32[]{:S(2)}) collective-permute-start(bf16[4,144,384]{2,1,0:T(8,128)(2,1)S(1)} %get-tuple-element.417), channel_id=1, source_target_pairs={{0,1},{1,0},{2,3},{3,2},{4,5},{5,4},{6,7},{7,6},{8,9},{9,8},{10,11... | collective-permute-start | bytes 1327112 | tf_op jit(solution)/shard_map/ppermute | solution.py:698
  220.2 19.6 %collective-permute-start.49 = (bf16[4,144,384]{2,1,0:T(8,128)(2,1)S(1)}, bf16[4,144,384]{2,1,0:T(8,128)(2,1)S(1)}, u32[]{:S(2)}, u32[]{:S(2)}) collective-permute-start(bf16[4,144,384]{2,1,0:T(8,128)(2,1)S(1)} %get-tuple-element.418), channel_id=1, source_target_pairs={{0,17},{1,16},{2,19},{3,18},{4,21},{5,20},{6,23},{7,22},{8,25},{9,... | collective-permute-start | bytes 1327112 | tf_op jit(solution)/shard_map/ppermute | solution.py:698
  226.4 13.4 %collective-permute-start.52 = (bf16[240,384]{1,0:T(8,128)(2,1)S(1)}, bf16[240,384]{1,0:T(8,128)(2,1)S(1)}, u32[]{:S(2)}, u32[]{:S(2)}) collective-permute-start(bf16[240,384]{1,0:T(8,128)(2,1)S(1)} %get-tuple-element.476), channel_id=1, source_target_pairs={{0,4},{1,5},{2,6},{3,7},{4,0},{5,1},{6,2},{7,3},{8,12},{9,13},{10,... | collective-permute-start | bytes 552968 | tf_op jit(solution)/shard_map/ppermute | solution.py:698
  228.3 11.4 %collective-permute-start.53 = (f32[3,8,768]{2,1,0:T(8,128)S(1)}, f32[3,8,768]{2,1,0:T(8,128)S(1)}, u32[]{:S(2)}, u32[]{:S(2)}) collective-permute-start(f32[3,8,768]{2,1,0:T(8,128)S(1)} %add.287), channel_id=1, source_target_pairs={{0,16},{1,17},{2,18},{3,19},{4,20},{5,21},{6,22},{7,23},{8,24},{9,... | collective-permute-start | bytes 221192 | tf_op jit(solution)/shard_map/ppermute | solution.py:698
  (39 other events, 268.6 us)

commit v6 on v5

--- a/solution.py
+++ b/solution.py
@@ -143,7 +143,7 @@
 
 def attended(ctx, wo, tokens, table):
     seq, width = tokens.shape
-    blk = 128
+    blk = 256
     rows = pl.BlockSpec((blk, width), lambda i: (i, 0))
     return call(
         attended_kernel,
@@ -195,7 +195,7 @@
 def inner(low, wi, bi):
     seq, width = low.shape
     ff = wi.shape[1]
-    blk = 512
+    blk = 1024
     cols = pl.BlockSpec((seq, blk), lambda i: (0, i))
     return call(
         inner_kernel,

time: 266 us -> 265 us (level)
  no operation moved by 1% of the time
where the time goes in v6:
time: 265 us; the launch traced here: 263 us
  waiting for transfers between devices  97.1 us (37%)
  Pallas kernels  85.8 us (32%)
  starting transfers between devices  61.6 us (23%)
  local copies, waits for them, and re-layouts  7.72 us (3%)
  other arithmetic  6.35 us (2%)
    ppermute x64, waiting for transfers between devices, swap(): return lax.ppermute(a, MESH_AXES, pairs)  97.1 us
    pallas_call x18, Pallas kernels, call(): pl.pallas_call(kernel, name=name, out_shape=outs, grid_spec=pltpu.Prefetc...  74.8 us
    ppermute x64, starting transfers between devices, swap(): return lax.ppermute(a, MESH_AXES, pairs)  61.6 us
    pallas_call x6, Pallas kernels, place_some(): pl.pallas_call(functools.partial(weights_kernel, tuple(spans), tuple(plac...  11 us
  transfers between devices with their start and end apart: 64, of which 28 were waited for; matrix products, arithmetic and copies ran while one was open for 3% of the time, Pallas kernels for 26%

profile of v6, /device:TPU:0, one launch (start us, length us, event | category | flops | bytes accessed | tf_op | source)
XLA Modules:
  0.0 262.6 jit_solution(7302389532597880727)
XLA Ops:
  4.7 5.1 %collective-permute-start.2 = (bf16[56,1152]{1,0:T(8,128)(2,1)S(1)}, bf16[56,1152]{1,0:T(8,128)(2,1)S(1)}, u32[]{:S(2)}, u32[]{:S(2)}) collective-permute-start(bf16[56,1152]{1,0:T(8,128)(2,1)S(1)} %get-tuple-element.242), channel_id=1, source_target_pairs={{0,6},{1,7},{2,4},{3,5},{4,2},{5,3},{6,0},{7,1},{8,14},{9,15},{10,... | collective-permute-start | bytes 387080 | tf_op jit(solution)/shard_map/ppermute | solution.py:698
  10.5 3.7 %collective-permute-done.2 = bf16[56,1152]{1,0:T(8,128)(2,1)S(1)} collective-permute-done((bf16[56,1152]{1,0:T(8,128)(2,1)S(1)}, bf16[56,1152]{1,0:T(8,128)(2,1)S(1)}, u32[]{:S(2)}, u32[]{:S(2)}) %collective-permute-start.2) | collective-permute-done | bytes 129056 | tf_op jit(solution)/shard_map/ppermute | solution.py:698
  14.2 6.5 %collective-permute-done.1 = bf16[56,1152]{1,0:T(8,128)(2,1)S(1)} collective-permute-done((bf16[56,1152]{1,0:T(8,128)(2,1)S(1)}, bf16[56,1152]{1,0:T(8,128)(2,1)S(1)}, u32[]{:S(2)}, u32[]{:S(2)}) %collective-permute-start.1) | collective-permute-done | bytes 129056 | tf_op jit(solution)/shard_map/ppermute | solution.py:698
  23.9 2.5 collective-permute-start.7
  28.3 5.0 %collective-permute-done.7 = bf16[48,1920]{1,0:T(8,128)(2,1)S(1)} collective-permute-done((bf16[48,1920]{1,0:T(8,128)(2,1)S(1)}, bf16[48,1920]{1,0:T(8,128)(2,1)S(1)}, u32[]{:S(2)}, u32[]{:S(2)}) %collective-permute-start.7) | collective-permute-done | bytes 184352 | tf_op jit(solution)/shard_map/ppermute | solution.py:698
  33.3 7.3 %collective-permute-done.6 = bf16[48,1920]{1,0:T(8,128)(2,1)S(1)} collective-permute-done((bf16[48,1920]{1,0:T(8,128)(2,1)S(1)}, bf16[48,1920]{1,0:T(8,128)(2,1)S(1)}, u32[]{:S(2)}, u32[]{:S(2)}) %collective-permute-start.6) | collective-permute-done | bytes 184352 | tf_op jit(solution)/shard_map/ppermute | solution.py:698
  44.9 7.8 %collective-permute-done.12 = bf16[240,384]{1,0:T(8,128)(2,1)S(1)} collective-permute-done((bf16[240,384]{1,0:T(8,128)(2,1)S(1)}, bf16[240,384]{1,0:T(8,128)(2,1)S(1)}, u32[]{:S(2)}, u32[]{:S(2)}) %collective-permute-start.12) | collective-permute-done | bytes 184352 | tf_op jit(solution)/shard_map/ppermute | solution.py:698
  52.7 3.5 %collective-permute-start.10 = (bf16[240,384]{1,0:T(8,128)(2,1)S(1)}, bf16[240,384]{1,0:T(8,128)(2,1)}, u32[]{:S(2)}, u32[]{:S(2)}) collective-permute-start(bf16[240,384]{1,0:T(8,128)(2,1)S(1)} %get-tuple-element.275), channel_id=1, source_target_pairs={{0,2},{1,3},{2,0},{3,1},{4,6},{5,7},{6,4},{7,5},{8,10},{9,11},{10,... | collective-permute-start | bytes 552968 | tf_op jit(solution)/shard_map/ppermute | solution.py:698
  56.6 3.5 %collective-permute-done.11 = bf16[240,384]{1,0:T(8,128)(2,1)} collective-permute-done((bf16[240,384]{1,0:T(8,128)(2,1)S(1)}, bf16[240,384]{1,0:T(8,128)(2,1)}, u32[]{:S(2)}, u32[]{:S(2)}) %collective-permute-start.11) | collective-permute-done | bytes 184352 | tf_op jit(solution)/shard_map/ppermute | solution.py:698
  68.7 2.1 place_weights.6
  72.6 8.9 %attention.1 = (bf16[512,768]{1,0:T(8,128)(2,1)S(1)}, bf16[512,768]{1,0:T(8,128)(2,1)S(1)}, bf16[512,768]{1,0:T(8,128)(2,1)S(1)}, bf16[512,768]{1,0:T(8,128)(2,1)S(1)}, f32[3,8,512]{2,1,0:T(8,128)S(1)}) custom-call(bf16[512,768]{1,0:T(8,128)(2,1)S(1)} %bitcast.153, bf16[768,768]{1,0:T(8,128)(2,1)S(1)} %bitcast.147, bf16[768,768]{1,0:T(8,128)(2,1)S(1)} %bitcast.149, ...), custom_call_target="tpu_custom_call" | custom-call | flops 163577856 | bytes 417792 | tf_op jit(solution)/shard_map/attention/pallas_call | solution.py:46
  86.3 2.6 place_weights.8
  88.9 12.3 %collective-permute-done.21.refs_2_ = bf16[4,240,384]{2,1,0:T(8,128)(2,1)S(1)} collective-permute-done((bf16[4,240,384]{2,1,0:T(8,128)(2,1)S(1)}, bf16[4,240,384]{2,1,0:T(8,128)(2,1)S(1)}, u32[]{:S(2)}, u32[]{:S(2)}) %collective-permute-start.21) | collective-permute-done | bytes 737312 | tf_op jit(solution)/shard_map/ppermute | solution.py:698
  107.3 10.3 %inner.1 = (bf16[512,3072]{1,0:T(8,128)(2,1)S(1)}, bf16[512,3072]{1,0:T(8,128)(2,1)S(1)}) custom-call(bf16[512,768]{1,0:T(8,128)(2,1)S(1)} %get-tuple-element.294.low.refs_1_, bf16[768,3072]{1,0:T(8,128)(2,1)S(1)} %bitcast.140, f32[1,3072]{1,0:T(1,128)S(1)} %reshape.181.bi), custom_call_target="tpu_custom_call" | custom-call | flops 150994944 | bytes 688128 | tf_op jit(solution)/shard_map/inner/pallas_call | solution.py:46
  117.7 2.6 %place_weights.10 = (bf16[4,2,2,192,768]{4,3,2,1,0:T(8,128)(2,1)S(1)}, bf16[4,2,2,48,768]{4,3,2,1,0:T(8,128)(2,1)S(1)}) custom-call(s32[4]{0:T(128)S(1)} %pad_add_fusion.where, bf16[4,240,384]{2,1,0:T(8,128)(2,1)S(1)} %pad_maximum_fusion.2.refs_0_, bf16[4,240,384]{2,1,0:T(8,128)(2,1)S(1)} %collective-permute-done.23.refs_1_, ...), custom_call_target="tpu_custom_call" | custom-call | bytes 368640 | tf_op jit(solution)/shard_map/place_weights/pallas_call | solution.py:625
  125.4 7.3 %outer.1 = (bf16[512,768]{1,0:T(8,128)(2,1)}, f32[512,768]{1,0:T(8,128)S(1)}, bf16[512,768]{1,0:T(8,128)(2,1)S(1)}, f32[8,768]{1,0:T(8,128)S(1)}, f32[8,768]{1,0:T(8,128)S(1)}, /*index=5*/f32[8,128]{1,0:T(8,128)S(1)}) custom-call(s32[1]{0:T(128)S(6)} %copy.88.labels, f32[3]{0:T(128)S(1)} %convert_element_type.263.bias3, ...), custom_call_target="tpu_custom_call" | custom-call | flops 150994944 | bytes 835584 | tf_op jit(solution)/shard_map/outer/pallas_call | solution.py:46
  132.7 3.2 %outer_grad_a.1 = (bf16[4,4,192,384]{3,2,1,0:T(8,128)(2,1)S(1)}, bf16[3072,512]{1,0:T(8,128)(2,1)S(1)}) custom-call(s32[4]{0:T(128)S(1)} %pad_add_fusion.where, bf16[512,3072]{1,0:T(8,128)(2,1)S(1)} %get-tuple-element.306.act.refs_0_, bf16[512,768]{1,0:T(8,128)(2,1)S(1)} %get-tuple-element.317.refs_1_.bg), custom_call_target="tpu_custom_call" | custom-call | flops 75497472 | bytes 344064 | tf_op jit(solution)/shard_map/outer_grad_a/pallas_call | solution.py:46
  136.1 3.5 %inner_grads.1.ig.refs_3_ = bf16[512,3072]{1,0:T(8,128)(2,1)S(1)} custom-call(bf16[512,768]{1,0:T(8,128)(2,1)S(1)} %get-tuple-element.317.refs_1_.bg, bf16[3072,768]{1,0:T(8,128)(2,1)S(1)} %bitcast.143, bf16[512,3072]{1,0:T(8,128)(2,1)S(1)} %get-tuple-element.319.slope), custom_call_target="tpu_custom_call" | custom-call | flops 150994944 | bytes 688128 | tf_op jit(solution)/shard_map/inner_grads/pallas_call | solution.py:46
  140.5 2.4 outer_grad_b.1
  148.3 5.5 %inner_back.1 = (f32[512,768]{1,0:T(8,128)S(1)}, bf16[512,768]{1,0:T(8,128)(2,1)S(1)}, f32[8,768]{1,0:T(8,128)S(1)}) custom-call(bf16[512,3072]{1,0:T(8,128)(2,1)S(1)} %inner_grads.1.ig.refs_3_, bf16[768,3072]{1,0:T(8,128)(2,1)S(1)} %bitcast.141, f32[512,768]{1,0:T(8,128)S(1)} %get-tuple-element.329.sg, f32[512,768]{1,0:T(8,128)S(1)} %get-tuple-element.311.n1, ...), custom_call_target="tpu_custom_call" | custom-call | flops 150994944 | bytes 884736 | tf_op jit(solution)/shard_map/inner_back/pallas_call | solution.py:46
  153.8 2.8 %inner_grad_a.1 = (bf16[4,4,240,384]{3,2,1,0:T(8,128)(2,1)S(1)}, bf16[768,512]{1,0:T(8,128)(2,1)S(1)}, bf16[768,512]{1,0:T(8,128)(2,1)S(1)}) custom-call(s32[4]{0:T(128)S(1)} %pad_add_fusion.where, bf16[512,768]{1,0:T(8,128)(2,1)S(1)} %get-tuple-element.289.ctx.refs_0_, bf16[512,768]{1,0:T(8,128)(2,1)S(1)} %get-tuple-element.294.low.refs_1_, ...), custom_call_target="tpu_custom_call" | custom-call | flops 94371840 | bytes 233472 | tf_op jit(solution)/shard_map/inner_grad_a/pallas_call | solution.py:46
  161.7 7.5 %attention_back.2 = (bf16[512,512]{1,0:T(8,128)(2,1)S(1)}, bf16[512,512]{1,0:T(8,128)(2,1)S(1)}, bf16[512,512]{1,0:T(8,128)(2,1)S(1)}, f32[8,512]{1,0:T(8,128)S(1)}) custom-call(bf16[512,768]{1,0:T(8,128)(2,1)S(1)} %get-tuple-element.340.q, bf16[512,768]{1,0:T(8,128)(2,1)S(1)} %get-tuple-element.341.k, bf16[512,768]{1,0:T(8,128)(2,1)S(1)} %get-tuple-element.342.v, ...), custom_call_target="tpu_custom_call" | custom-call | flops 109051904 | bytes 311296 | tf_op jit(solution)/shard_map/attention_back/pallas_call | solution.py:46
  169.3 2.5 inner_grad_b.1
  171.8 3.6 %attention_back.3 = (bf16[512,256]{1,0:T(8,128)(2,1)S(1)}, bf16[512,256]{1,0:T(8,128)(2,1)S(1)}, bf16[512,256]{1,0:T(8,128)(2,1)S(1)}, f32[8,256]{1,0:T(8,128)S(1)}) custom-call(bf16[512,768]{1,0:T(8,128)(2,1)S(1)} %get-tuple-element.340.q, bf16[512,768]{1,0:T(8,128)(2,1)S(1)} %get-tuple-element.341.k, bf16[512,768]{1,0:T(8,128)(2,1)S(1)} %get-tuple-element.342.v, ...), custom_call_target="tpu_custom_call" | custom-call | flops 54525952 | bytes 155648 | tf_op jit(solution)/shard_map/attention_back/pallas_call | solution.py:46
  175.7 2.2 query_grad_a.1
  186.4 5.1 %collective-permute-done.44 = bf16[2,192,384]{2,1,0:T(8,128)(2,1)S(1)} collective-permute-done((bf16[2,192,384]{2,1,0:T(8,128)(2,1)S(1)}, bf16[2,192,384]{2,1,0:T(8,128)(2,1)S(1)}, u32[]{:S(2)}, u32[]{:S(2)}) %collective-permute-start.44) | collective-permute-done | bytes 294944 | tf_op jit(solution)/shard_map/ppermute | solution.py:698
  194.2 6.1 %tokens_back.1 = f32[512,768]{1,0:T(8,128)} custom-call(f32[512,768]{1,0:T(8,128)S(1)} %get-tuple-element.407.res, bf16[512,768]{1,0:T(8,128)(2,1)S(1)} %constant_dynamic-update-slice_fusion.refs_1_.dq, bf16[512,768]{1,0:T(8,128)(2,1)S(1)} %constant_dynamic-update-slice_fusion.2.refs_2_.dk, ...), custom_call_target="tpu_custom_call" | custom-call | flops 113246208 | bytes 565248 | tf_op jit(solution)/shard_map/tokens_back/pallas_call | solution.py:46
  200.4 14.2 %collective-permute-done.41 = bf16[4,240,384]{2,1,0:T(8,128)(2,1)S(1)} collective-permute-done((bf16[4,240,384]{2,1,0:T(8,128)(2,1)S(1)}, bf16[4,240,384]{2,1,0:T(8,128)(2,1)S(1)}, u32[]{:S(2)}, u32[]{:S(2)}) %collective-permute-start.41) | collective-permute-done | bytes 737312 | tf_op jit(solution)/shard_map/ppermute | solution.py:698
  221.6 3.0 %collective-permute-done.51 = f32[3,8,768]{2,1,0:T(8,128)S(1)} collective-permute-done((f32[3,8,768]{2,1,0:T(8,128)S(1)}, f32[3,8,768]{2,1,0:T(8,128)S(1)}, u32[]{:S(2)}, u32[]{:S(2)}) %collective-permute-start.51) | collective-permute-done | bytes 73760 | tf_op jit(solution)/shard_map/ppermute | solution.py:698
  229.5 10.1 %collective-permute-done.53 = f32[3,8,768]{2,1,0:T(8,128)S(1)} collective-permute-done((f32[3,8,768]{2,1,0:T(8,128)S(1)}, f32[3,8,768]{2,1,0:T(8,128)S(1)}, u32[]{:S(2)}, u32[]{:S(2)}) %collective-permute-start.53) | collective-permute-done | bytes 73760 | tf_op jit(solution)/shard_map/ppermute | solution.py:698
  247.1 2.4 collective-permute-done.58
  260.1 2.3 place_shards.3
  (204 shorter events, 92.8 us)
Async XLA Ops:
  20.8 19.8 %collective-permute-start.4 = (bf16[4,56,1152]{2,1,0:T(8,128)(2,1)S(1)}, bf16[4,56,1152]{2,1,0:T(8,128)(2,1)S(1)}, u32[]{:S(2)}, u32[]{:S(2)}) collective-permute-start(bf16[4,56,1152]{2,1,0:T(8,128)(2,1)S(1)} %pad_maximum_fusion.4.refs_0_), channel_id=1, source_target_pairs={{0,1},{1,0},{2,3},{3,2},{4,5},{5,4},{6,7},{7,6},{8,9},{9,8},{10,11... | collective-permute-start | bytes 1548296 | tf_op jit(solution)/shard_map/ppermute | solution.py:698
  22.4 18.2 %collective-permute-start.3 = (bf16[4,56,1152]{2,1,0:T(8,128)(2,1)S(1)}, bf16[4,56,1152]{2,1,0:T(8,128)(2,1)S(1)}, u32[]{:S(2)}, u32[]{:S(2)}) collective-permute-start(bf16[4,56,1152]{2,1,0:T(8,128)(2,1)S(1)} %pad_maximum_fusion.4.refs_0_), channel_id=1, source_target_pairs={{0,16},{1,17},{2,18},{3,19},{4,20},{5,21},{6,22},{7,23},{8,24},{9,... | collective-permute-start | bytes 1548296 | tf_op jit(solution)/shard_map/ppermute | solution.py:698
  26.4 14.2 %collective-permute-start.6 = (bf16[48,1920]{1,0:T(8,128)(2,1)S(1)}, bf16[48,1920]{1,0:T(8,128)(2,1)S(1)}, u32[]{:S(2)}, u32[]{:S(2)}) collective-permute-start(bf16[48,1920]{1,0:T(8,128)(2,1)S(1)} %get-tuple-element.251), channel_id=1, source_target_pairs={{0,4},{1,5},{2,6},{3,7},{4,0},{5,1},{6,2},{7,3},{8,12},{9,13},{10,... | collective-permute-start | bytes 552968 | tf_op jit(solution)/shard_map/ppermute | solution.py:698
  26.4 14.2 %collective-permute-start.5 = (bf16[48,1920]{1,0:T(8,128)(2,1)S(1)}, bf16[48,1920]{1,0:T(8,128)(2,1)S(1)}, u32[]{:S(2)}, u32[]{:S(2)}) collective-permute-start(bf16[48,1920]{1,0:T(8,128)(2,1)S(1)} %get-tuple-element.251), channel_id=1, source_target_pairs={{0,2},{1,3},{2,0},{3,1},{4,6},{5,7},{6,4},{7,5},{8,10},{9,11},{10,... | collective-permute-start | bytes 552968 | tf_op jit(solution)/shard_map/ppermute | solution.py:698
  42.0 20.0 %collective-permute-start.13 = (bf16[12,56,1152]{2,1,0:T(8,128)(2,1)}, bf16[12,56,1152]{2,1,0:T(8,128)(2,1)}, u32[]{:S(2)}, u32[]{:S(2)}) collective-permute-start(bf16[12,56,1152]{2,1,0:T(8,128)(2,1)} %pad_maximum_fusion), channel_id=1, source_target_pairs={{0,8},{1,9},{2,10},{3,11},{4,12},{5,13},{6,14},{7,15},{8,0},{9,1},... | collective-permute-start | bytes 4644872 | tf_op jit(solution)/shard_map/ppermute | solution.py:698
  42.1 19.8 %collective-permute-start.9 = (bf16[4,48,1920]{2,1,0:T(8,128)(2,1)S(1)}, bf16[4,48,1920]{2,1,0:T(8,128)(2,1)S(1)}, u32[]{:S(2)}, u32[]{:S(2)}) collective-permute-start(bf16[4,48,1920]{2,1,0:T(8,128)(2,1)S(1)} %pad_maximum_fusion.1.refs_0_), channel_id=1, source_target_pairs={{0,16},{1,17},{2,18},{3,19},{4,20},{5,21},{6,22},{7,23},{8,24},{9,... | collective-permute-start | bytes 2211848 | tf_op jit(solution)/shard_map/ppermute | solution.py:698
  42.7 19.2 %collective-permute-start.8 = (bf16[4,56,1152]{2,1,0:T(8,128)(2,1)S(1)}, bf16[4,56,1152]{2,1,0:T(8,128)(2,1)}, u32[]{:S(2)}, u32[]{:S(2)}) collective-permute-start(bf16[4,56,1152]{2,1,0:T(8,128)(2,1)S(1)} %collective-permute-done.3.refs_4_), channel_id=1, source_target_pairs={{0,1},{1,0},{2,3},{3,2},{4,5},{5,4},{6,7},{7,6},{8,9},{9,8},{10,11... | collective-permute-start | bytes 1548296 | tf_op jit(solution)/shard_map/ppermute | solution.py:698
  44.9 15.2 %collective-permute-start.11 = (bf16[240,384]{1,0:T(8,128)(2,1)S(1)}, bf16[240,384]{1,0:T(8,128)(2,1)}, u32[]{:S(2)}, u32[]{:S(2)}) collective-permute-start(bf16[240,384]{1,0:T(8,128)(2,1)S(1)} %get-tuple-element.275), channel_id=1, source_target_pairs={{0,4},{1,5},{2,6},{3,7},{4,0},{5,1},{6,2},{7,3},{8,12},{9,13},{10,... | collective-permute-start | bytes 552968 | tf_op jit(solution)/shard_map/ppermute | solution.py:698
  63.9 17.5 %collective-permute-start.16 = (bf16[4,240,384]{2,1,0:T(8,128)(2,1)S(1)}, bf16[4,240,384]{2,1,0:T(8,128)(2,1)}, u32[]{:S(2)}, u32[]{:S(2)}) collective-permute-start(bf16[4,240,384]{2,1,0:T(8,128)(2,1)S(1)} %pad_maximum_fusion.2.refs_0_), channel_id=1, source_target_pairs={{0,16},{1,17},{2,18},{3,19},{4,20},{5,21},{6,22},{7,23},{8,24},{9,... | collective-permute-start | bytes 2211848 | tf_op jit(solution)/shard_map/ppermute | solution.py:698
  65.5 16.3 %collective-permute-start.15 = (bf16[4,48,1920]{2,1,0:T(8,128)(2,1)S(1)}, bf16[4,48,1920]{2,1,0:T(8,128)(2,1)}, u32[]{:S(2)}, u32[]{:S(2)}) collective-permute-start(bf16[4,48,1920]{2,1,0:T(8,128)(2,1)S(1)} %pad_maximum_fusion.1.refs_0_), channel_id=1, source_target_pairs={{0,1},{1,0},{2,3},{3,2},{4,5},{5,4},{6,7},{7,6},{8,9},{9,8},{10,11... | collective-permute-start | bytes 2211848 | tf_op jit(solution)/shard_map/ppermute | solution.py:698
  82.5 18.6 %collective-permute-start.21 = (bf16[4,240,384]{2,1,0:T(8,128)(2,1)S(1)}, bf16[4,240,384]{2,1,0:T(8,128)(2,1)S(1)}, u32[]{:S(2)}, u32[]{:S(2)}) collective-permute-start(bf16[4,240,384]{2,1,0:T(8,128)(2,1)S(1)} %pad_maximum_fusion.2.refs_0_), channel_id=1, source_target_pairs={{0,1},{1,0},{2,3},{3,2},{4,5},{5,4},{6,7},{7,6},{8,9},{9,8},{10,11... | collective-permute-start | bytes 2211848 | tf_op jit(solution)/shard_map/ppermute | solution.py:698
  83.8 18.8 %collective-permute-start.17 = (bf16[4,48,1920]{2,1,0:T(8,128)(2,1)}, bf16[4,48,1920]{2,1,0:T(8,128)(2,1)S(1)}, u32[]{:S(2)}, u32[]{:S(2)}) collective-permute-start(bf16[4,48,1920]{2,1,0:T(8,128)(2,1)} %collective-permute-done.15.refs_2_), channel_id=1, source_target_pairs={{0,16},{1,17},{2,18},{3,19},{4,20},{5,21},{6,22},{7,23},{8,24},{9,... | collective-permute-start | bytes 2211848 | tf_op jit(solution)/shard_map/ppermute | solution.py:698
  102.6 15.1 %collective-permute-start.23 = (bf16[4,240,384]{2,1,0:T(8,128)(2,1)S(1)}, bf16[4,240,384]{2,1,0:T(8,128)(2,1)S(1)}, u32[]{:S(2)}, u32[]{:S(2)}) collective-permute-start(bf16[4,240,384]{2,1,0:T(8,128)(2,1)S(1)} %pad_maximum_fusion.2.refs_0_), channel_id=1, source_target_pairs={{0,8},{1,9},{2,10},{3,11},{4,12},{5,13},{6,14},{7,15},{8,0},{9,1},... | collective-permute-start | bytes 2211848 | tf_op jit(solution)/shard_map/ppermute | solution.py:698
  103.1 14.6 %collective-permute-start.24 = (bf16[4,240,384]{2,1,0:T(8,128)(2,1)S(1)}, bf16[4,240,384]{2,1,0:T(8,128)(2,1)S(1)}, u32[]{:S(2)}, u32[]{:S(2)}) collective-permute-start(bf16[4,240,384]{2,1,0:T(8,128)(2,1)S(1)} %collective-permute-done.21.refs_2_), channel_id=1, source_target_pairs={{0,8},{1,9},{2,10},{3,11},{4,12},{5,13},{6,14},{7,15},{8,0},{9,1},... | collective-permute-start | bytes 2211848 | tf_op jit(solution)/shard_map/ppermute | solution.py:698
  103.1 14.6 %collective-permute-start.25 = (bf16[4,240,384]{2,1,0:T(8,128)(2,1)}, bf16[4,240,384]{2,1,0:T(8,128)(2,1)S(1)}, u32[]{:S(2)}, u32[]{:S(2)}) collective-permute-start(bf16[4,240,384]{2,1,0:T(8,128)(2,1)} %collective-permute-done.16.refs_4_), channel_id=1, source_target_pairs={{0,8},{1,9},{2,10},{3,11},{4,12},{5,13},{6,14},{7,15},{8,0},{9,1},... | collective-permute-start | bytes 2211848 | tf_op jit(solution)/shard_map/ppermute | solution.py:698
  103.6 18.6 %collective-permute-start.22 = (bf16[4,240,384]{2,1,0:T(8,128)(2,1)}, bf16[4,240,384]{2,1,0:T(8,128)(2,1)S(1)}, u32[]{:S(2)}, u32[]{:S(2)}) collective-permute-start(bf16[4,240,384]{2,1,0:T(8,128)(2,1)} %collective-permute-done.16.refs_4_), channel_id=1, source_target_pairs={{0,1},{1,0},{2,3},{3,2},{4,5},{5,4},{6,7},{7,6},{8,9},{9,8},{10,11... | collective-permute-start | bytes 2211848 | tf_op jit(solution)/shard_map/ppermute | solution.py:698
  144.3 13.0 %collective-permute-start.31 = (bf16[3,192,384]{2,1,0:T(8,128)(2,1)S(1)}, bf16[3,192,384]{2,1,0:T(8,128)(2,1)S(1)}, u32[]{:S(2)}, u32[]{:S(2)}) collective-permute-start(bf16[3,192,384]{2,1,0:T(8,128)(2,1)S(1)} %slice.243), channel_id=1, source_target_pairs={{0,1},{1,0},{2,3},{3,2},{4,5},{5,4},{6,7},{7,6},{8,9},{9,8},{10,11... | collective-permute-start | bytes 1327112 | tf_op jit(solution)/shard_map/ppermute | solution.py:698
  145.6 11.8 %collective-permute-start.30 = (bf16[3,192,384]{2,1,0:T(8,128)(2,1)S(1)}, bf16[3,192,384]{2,1,0:T(8,128)(2,1)S(1)}, u32[]{:S(2)}, u32[]{:S(2)}) collective-permute-start(bf16[3,192,384]{2,1,0:T(8,128)(2,1)S(1)} %slice.242), channel_id=1, source_target_pairs={{0,16},{1,17},{2,18},{3,19},{4,20},{5,21},{6,22},{7,23},{8,24},{9,... | collective-permute-start | bytes 1327112 | tf_op jit(solution)/shard_map/ppermute | solution.py:698
  157.4 11.9 %collective-permute-start.34 = (bf16[4,4,240,384]{3,2,1,0:T(8,128)(2,1)S(1)}, bf16[4,4,240,384]{3,2,1,0:T(8,128)(2,1)S(1)}, u32[]{:S(2)}, u32[]{:S(2)}) collective-permute-start(bf16[4,4,240,384]{3,2,1,0:T(8,128)(2,1)S(1)} %get-tuple-element.339), channel_id=1, source_target_pairs={{0,8},{1,9},{2,10},{3,11},{4,12},{5,13},{6,14},{7,15},{8,0},{9,1},... | collective-permute-start | bytes 8847368 | tf_op jit(solution)/shard_map/ppermute | solution.py:698
  157.4 11.8 %collective-permute-start.35 = (bf16[8,8,768]{2,1,0:T(8,128)(2,1)S(1)}, bf16[8,8,768]{2,1,0:T(8,128)(2,1)S(1)}, u32[]{:S(2)}, u32[]{:S(2)}) collective-permute-start(bf16[8,8,768]{2,1,0:T(8,128)(2,1)S(1)} %pad_maximum_fusion.10), channel_id=1, source_target_pairs={{0,16},{1,17},{2,18},{3,19},{4,20},{5,21},{6,22},{7,23},{8,24},{9,... | collective-permute-start | bytes 294920 | tf_op jit(solution)/shard_map/ppermute | solution.py:698
  158.2 20.5 %collective-permute-start.36 = (bf16[192,384]{1,0:T(8,128)(2,1)S(1)}, bf16[192,384]{1,0:T(8,128)(2,1)S(1)}, u32[]{:S(2)}, u32[]{:S(2)}) collective-permute-start(bf16[192,384]{1,0:T(8,128)(2,1)S(1)} %get-tuple-element.371), channel_id=1, source_target_pairs={{0,16},{1,17},{2,18},{3,19},{4,20},{5,21},{6,22},{7,23},{8,24},{9,... | collective-permute-start | bytes 442376 | tf_op jit(solution)/shard_map/ppermute | solution.py:698
  159.5 19.2 %collective-permute-start.37 = (bf16[192,384]{1,0:T(8,128)(2,1)S(1)}, bf16[192,384]{1,0:T(8,128)(2,1)S(1)}, u32[]{:S(2)}, u32[]{:S(2)}) collective-permute-start(bf16[192,384]{1,0:T(8,128)(2,1)S(1)} %get-tuple-element.372), channel_id=1, source_target_pairs={{0,1},{1,0},{2,3},{3,2},{4,5},{5,4},{6,7},{7,6},{8,9},{9,8},{10,11... | collective-permute-start | bytes 442376 | tf_op jit(solution)/shard_map/ppermute | solution.py:698
  160.7 18.4 %collective-permute-start.38 = (bf16[4,192,384]{2,1,0:T(8,128)(2,1)S(1)}, bf16[4,192,384]{2,1,0:T(8,128)(2,1)S(1)}, u32[]{:S(2)}, u32[]{:S(2)}) collective-permute-start(bf16[4,192,384]{2,1,0:T(8,128)(2,1)S(1)} %get-tuple-element.373), channel_id=1, source_target_pairs={{0,17},{1,16},{2,19},{3,18},{4,21},{5,20},{6,23},{7,22},{8,25},{9,... | collective-permute-start | bytes 1769480 | tf_op jit(solution)/shard_map/ppermute | solution.py:698
  179.3 21.1 %collective-permute-start.40 = (bf16[4,240,384]{2,1,0:T(8,128)(2,1)S(1)}, bf16[4,240,384]{2,1,0:T(8,128)(2,1)S(1)}, u32[]{:S(2)}, u32[]{:S(2)}) collective-permute-start(bf16[4,240,384]{2,1,0:T(8,128)(2,1)S(1)} %get-tuple-element.380), channel_id=1, source_target_pairs={{0,16},{1,17},{2,18},{3,19},{4,20},{5,21},{6,22},{7,23},{8,24},{9,... | collective-permute-start | bytes 2211848 | tf_op jit(solution)/shard_map/ppermute | solution.py:698
  180.6 34.0 %collective-permute-start.41 = (bf16[4,240,384]{2,1,0:T(8,128)(2,1)S(1)}, bf16[4,240,384]{2,1,0:T(8,128)(2,1)S(1)}, u32[]{:S(2)}, u32[]{:S(2)}) collective-permute-start(bf16[4,240,384]{2,1,0:T(8,128)(2,1)S(1)} %get-tuple-element.381), channel_id=1, source_target_pairs={{0,1},{1,0},{2,3},{3,2},{4,5},{5,4},{6,7},{7,6},{8,9},{9,8},{10,11... | collective-permute-start | bytes 2211848 | tf_op jit(solution)/shard_map/ppermute | solution.py:698
  181.8 32.8 %collective-permute-start.42 = (bf16[4,240,384]{2,1,0:T(8,128)(2,1)S(1)}, bf16[4,240,384]{2,1,0:T(8,128)(2,1)S(1)}, u32[]{:S(2)}, u32[]{:S(2)}) collective-permute-start(bf16[4,240,384]{2,1,0:T(8,128)(2,1)S(1)} %get-tuple-element.382), channel_id=1, source_target_pairs={{0,17},{1,16},{2,19},{3,18},{4,21},{5,20},{6,23},{7,22},{8,25},{9,... | collective-permute-start | bytes 2211848 | tf_op jit(solution)/shard_map/ppermute | solution.py:698
  191.6 23.0 %collective-permute-start.45 = (bf16[192,384]{1,0:T(8,128)(2,1)S(1)}, bf16[192,384]{1,0:T(8,128)(2,1)S(1)}, u32[]{:S(2)}, u32[]{:S(2)}) collective-permute-start(bf16[192,384]{1,0:T(8,128)(2,1)S(1)} %get-tuple-element.478), channel_id=1, source_target_pairs={{0,4},{1,5},{2,6},{3,7},{4,0},{5,1},{6,2},{7,3},{8,12},{9,13},{10,... | collective-permute-start | bytes 442376 | tf_op jit(solution)/shard_map/ppermute | solution.py:698
  218.0 21.5 %collective-permute-start.47 = (bf16[4,144,384]{2,1,0:T(8,128)(2,1)S(1)}, bf16[4,144,384]{2,1,0:T(8,128)(2,1)S(1)}, u32[]{:S(2)}, u32[]{:S(2)}) collective-permute-start(bf16[4,144,384]{2,1,0:T(8,128)(2,1)S(1)} %get-tuple-element.416), channel_id=1, source_target_pairs={{0,16},{1,17},{2,18},{3,19},{4,20},{5,21},{6,22},{7,23},{8,24},{9,... | collective-permute-start | bytes 1327112 | tf_op jit(solution)/shard_map/ppermute | solution.py:698
  218.6 21.0 %collective-permute-start.48 = (bf16[4,144,384]{2,1,0:T(8,128)(2,1)S(1)}, bf16[4,144,384]{2,1,0:T(8,128)(2,1)S(1)}, u32[]{:S(2)}, u32[]{:S(2)}) collective-permute-start(bf16[4,144,384]{2,1,0:T(8,128)(2,1)S(1)} %get-tuple-element.417), channel_id=1, source_target_pairs={{0,1},{1,0},{2,3},{3,2},{4,5},{5,4},{6,7},{7,6},{8,9},{9,8},{10,11... | collective-permute-start | bytes 1327112 | tf_op jit(solution)/shard_map/ppermute | solution.py:698
  220.0 19.6 %collective-permute-start.49 = (bf16[4,144,384]{2,1,0:T(8,128)(2,1)S(1)}, bf16[4,144,384]{2,1,0:T(8,128)(2,1)S(1)}, u32[]{:S(2)}, u32[]{:S(2)}) collective-permute-start(bf16[4,144,384]{2,1,0:T(8,128)(2,1)S(1)} %get-tuple-element.418), channel_id=1, source_target_pairs={{0,17},{1,16},{2,19},{3,18},{4,21},{5,20},{6,23},{7,22},{8,25},{9,... | collective-permute-start | bytes 1327112 | tf_op jit(solution)/shard_map/ppermute | solution.py:698
  226.2 13.3 %collective-permute-start.52 = (bf16[240,384]{1,0:T(8,128)(2,1)S(1)}, bf16[240,384]{1,0:T(8,128)(2,1)S(1)}, u32[]{:S(2)}, u32[]{:S(2)}) collective-permute-start(bf16[240,384]{1,0:T(8,128)(2,1)S(1)} %get-tuple-element.476), channel_id=1, source_target_pairs={{0,4},{1,5},{2,6},{3,7},{4,0},{5,1},{6,2},{7,3},{8,12},{9,13},{10,... | collective-permute-start | bytes 552968 | tf_op jit(solution)/shard_map/ppermute | solution.py:698
  228.1 11.4 %collective-permute-start.53 = (f32[3,8,768]{2,1,0:T(8,128)S(1)}, f32[3,8,768]{2,1,0:T(8,128)S(1)}, u32[]{:S(2)}, u32[]{:S(2)}) collective-permute-start(f32[3,8,768]{2,1,0:T(8,128)S(1)} %add.287), channel_id=1, source_target_pairs={{0,16},{1,17},{2,18},{3,19},{4,20},{5,21},{6,22},{7,23},{8,24},{9,... | collective-permute-start | bytes 221192 | tf_op jit(solution)/shard_map/ppermute | solution.py:698
  (39 other events, 268.9 us)
